TPU v7x, 32 devices: a whole 2x2x4 slice. The times are simulated.
32 devices in a mesh: dp: 4 (over z), row: 4 (over x, core), col: 2 (over y).
Axes of the slice: x: 2, y: 2, z: 4, core: 2. Of those that a mesh axis runs over, the one named last changes fastest.
Arguments:
- inputs: bfloat16 [2, 8192, 2048], P(None, ('dp', 'col'), 'row'), may hold values from -6 to 6
- lengths: int32 [2, 8], P(None, 'dp'), may hold values from 256 to 1024, as said below
- norm_gain: float32 [2048], P('row'), may hold values from 0.5 to 1.5
- norm_bias: float32 [2048], P('row'), may hold values from -1.75 to 1.75
- qkv_weight: bfloat16 [2048, 32, 3, 64], P('row', 'col'), may hold values from -0.125 to 0.125
- qkv_bias: float32 [32, 3, 64], P('col'), may hold values from -3 to 3
- out_weight: bfloat16 [2048, 2048], P('col', 'row'), may hold values from -1 to 1
- out_bias: float32 [2048], P('row'), may hold values from -3 to 3
- up_weight: bfloat16 [2048, 8192], P('row', 'col'), may hold values from -0.125 to 0.125
- up_bias: float32 [8192], P('col'), may hold values from -3 to 3
- down_weight: bfloat16 [8192, 2048], P('col', 'row'), may hold values from -0.0625 to 0.0625
- cotangent: bfloat16 [2, 8192, 2048], P(None, ('dp', 'col'), 'row'), may hold values from -6 to 6
Outputs:
- block_out: bfloat16 [2, 8192, 2048], P(None, ('dp', 'col'), 'row')
- input_grad: bfloat16 [2, 8192, 2048], P(None, ('dp', 'col'), 'row')
- norm_gain_grad: float32 [2048], P('row')
- norm_bias_grad: float32 [2048], P('row')
- qkv_weight_grad: float32 [2048, 32, 3, 64], P('row', 'col')
- qkv_bias_grad: float32 [32, 3, 64], P('col')
- out_weight_grad: float32 [2048, 2048], P('col', 'row')
- out_bias_grad: float32 [2048], P('row')
- up_weight_grad: float32 [2048, 8192], P('row', 'col')
- up_bias_grad: float32 [8192], P('col')
- down_weight_grad: float32 [8192, 2048], P('col', 'row')
Inputs may be any that keep to these rules, and one draw needn't show every extreme that they name: `lengths`: some slot holds exactly 1024 valid tokens and some exactly 256.
All inputs are finite; a program needn't handle non-finite values.
Results may differ from a plain program's by a relative error of at most 0.01.
Values may be sent and summed in bfloat16 or wider, within the bound.
No kernel may reach another device: no remote copies, remote signals or barrier semaphores. Data moves between devices by JAX's collectives and lax.ppermute only.
A program may use at most 448 MiB of HBM per device.

v0:
```python
from functools import partial

import jax
import jax.numpy as jnp
from jax import lax
from jax.sharding import PartitionSpec as P

SLOT_LEN = 1024


eps_norm = 1e-05
neg_big = -1e30


def for_sending(x):

    def short(part):
        return part.astype(jnp.bfloat16) if part.dtype == jnp.float32 else part

    return jax.tree.map(short, x)


def rotary_tables(rows_count, slot_len, rot_dims):
    half_rot = rot_dims // 2
    position = (jnp.arange(rows_count) % slot_len).astype(jnp.float32)
    frequency = 10000.0 ** (-jnp.arange(half_rot).astype(jnp.float32) * 2.0 / rot_dims)
    angles = position[:, None] * frequency[None, :]
    return (jnp.cos(angles), jnp.sin(angles))


def rotate(values, cosine, sine_table, rot_dims):
    half_rot = rot_dims // 2
    front_half = values[..., :half_rot]
    back_half = values[..., half_rot:rot_dims]
    cos_rows = cosine[:, None, :]
    sin_rows = sine_table[:, None, :]
    return jnp.concatenate(
        [
            front_half * cos_rows - back_half * sin_rows,
            back_half * cos_rows + front_half * sin_rows,
            values[..., rot_dims:],
        ],
        axis=-1,
    )


def rotate_back(gradient, cosine, sine_table, rot_dims):
    half_rot = rot_dims // 2
    front_half = gradient[..., :half_rot]
    back_half = gradient[..., half_rot:rot_dims]
    cos_rows = cosine[:, None, :]
    sin_rows = sine_table[:, None, :]
    return jnp.concatenate(
        [
            front_half * cos_rows + back_half * sin_rows,
            back_half * cos_rows - front_half * sin_rows,
            gradient[..., rot_dims:],
        ],
        axis=-1,
    )


def allowed_mask(start, block_rows, slot_len, limit):
    query_pos = start + jnp.arange(block_rows)
    key_pos = jnp.arange(slot_len)
    return (key_pos[None, :] <= query_pos[:, None]) & (key_pos[None, :] < limit)


def block_scores(query_blk, slot_keys, start, limit):
    scale = query_blk.shape[2] ** (-0.5)
    scores = (
        jnp.einsum("qhd,khd->hqk", query_blk, slot_keys, preferred_element_type=jnp.float32) * scale
    )
    allowed = allowed_mask(start, query_blk.shape[0], slot_keys.shape[0], limit)
    return jnp.where(allowed[None], scores, neg_big)


def attend(query, keys, values, lens):
    total_rows, heads_local, head_dim = query.shape
    slot_shape = (total_rows // SLOT_LEN, SLOT_LEN, heads_local, head_dim)
    block_rows = min(512, SLOT_LEN)

    def one_slot(items):
        slot_query, slot_keys, slot_values, limit = items
        out_blocks = []
        norm_blocks = []
        for start in range(0, SLOT_LEN, block_rows):
            query_blk = slot_query[start : start + block_rows]
            scores = block_scores(query_blk, slot_keys, start, limit)
            top_score = jnp.max(scores, -1)
            expo = jnp.exp(scores - top_score[..., None])
            total_weight = jnp.sum(expo, -1)
            probs = (expo / total_weight[..., None]).astype(jnp.bfloat16)
            out_blk = jnp.einsum(
                "hqk,khd->qhd", probs, slot_values, preferred_element_type=jnp.float32
            )
            out_blocks.append(out_blk.astype(jnp.bfloat16))
            norm_blocks.append(jnp.transpose(top_score + jnp.log(total_weight)))
        return (jnp.concatenate(out_blocks, 0), jnp.concatenate(norm_blocks, 0))

    attn_out, log_norm = lax.map(
        one_slot,
        (query.reshape(slot_shape), keys.reshape(slot_shape), values.reshape(slot_shape), lens),
    )
    return (
        attn_out.reshape(total_rows, heads_local, head_dim),
        log_norm.reshape(total_rows, heads_local),
    )


def attend_back(query, keys, values, grad_out, log_norm, lens):
    total_rows, heads_local, head_dim = query.shape
    slot_shape = (total_rows // SLOT_LEN, SLOT_LEN, heads_local, head_dim)
    block_rows = min(512, SLOT_LEN)
    scale = head_dim ** (-0.5)

    def one_slot(items):
        slot_query, slot_keys, slot_values, slot_grad, slot_norm, limit = items
        grad_keys = jnp.zeros(slot_keys.shape, jnp.float32)
        grad_values = jnp.zeros(slot_values.shape, jnp.float32)
        query_grads = []
        for start in range(0, SLOT_LEN, block_rows):
            query_blk = slot_query[start : start + block_rows]
            grad_blk = slot_grad[start : start + block_rows]
            norm_blk = jnp.transpose(slot_norm[start : start + block_rows])
            scores = block_scores(query_blk, slot_keys, start, limit)
            probs = jnp.exp(scores - norm_blk[..., None])
            grad_probs = jnp.einsum(
                "qhd,khd->hqk", grad_blk, slot_values, preferred_element_type=jnp.float32
            )
            row_delta = jnp.sum(grad_probs * probs, -1, keepdims=True)
            grad_scores = (probs * (grad_probs - row_delta)).astype(jnp.bfloat16)
            query_grads.append(
                jnp.einsum(
                    "hqk,khd->qhd", grad_scores, slot_keys, preferred_element_type=jnp.float32
                )
                * scale
            )
            grad_keys = (
                grad_keys
                + jnp.einsum(
                    "hqk,qhd->khd", grad_scores, query_blk, preferred_element_type=jnp.float32
                )
                * scale
            )
            grad_values = grad_values + jnp.einsum(
                "hqk,qhd->khd",
                probs.astype(jnp.bfloat16),
                grad_blk,
                preferred_element_type=jnp.float32,
            )
        return (jnp.concatenate(query_grads, 0), grad_keys, grad_values)

    flat_shape = (total_rows // SLOT_LEN, SLOT_LEN, heads_local)
    grad_query, grad_keys, grad_values = lax.map(
        one_slot,
        (
            query.reshape(slot_shape),
            keys.reshape(slot_shape),
            values.reshape(slot_shape),
            grad_out.reshape(slot_shape),
            log_norm.reshape(flat_shape),
            lens,
        ),
    )
    row_shape = (total_rows, heads_local, head_dim)
    return (
        grad_query.reshape(row_shape),
        grad_keys.reshape(row_shape),
        grad_values.reshape(row_shape),
    )


def on_device(
    inputs,
    lengths,
    norm_gain,
    norm_bias,
    qkv_weight,
    qkv_bias,
    out_weight,
    out_bias,
    up_weight,
    up_bias,
    down_weight,
    cotangent,
):
    rows_local = inputs.shape[1]
    rows_total = rows_local * lax.axis_size("col")
    model_width = norm_gain.shape[0] * lax.axis_size("row")
    heads_local = qkv_weight.shape[1] // lax.axis_size("row")
    head_dim = qkv_weight.shape[3]
    rot_dims = head_dim // 2
    ff_local = up_weight.shape[1] // lax.axis_size("row")
    row_index = lax.axis_index("row")
    col_index = lax.axis_index("col")
    bias_heads = lax.dynamic_slice_in_dim(qkv_bias, row_index * heads_local, heads_local, 0)
    bias_up = lax.dynamic_slice_in_dim(up_bias, row_index * ff_local, ff_local, 0)
    qkv_flat = qkv_weight.reshape(qkv_weight.shape[0], -1)
    cosine, sine_table = rotary_tables(rows_total, SLOT_LEN, rot_dims)
    gelu_tanh = partial(jax.nn.gelu, approximate=True)
    own_qkv, own_up = (
        lax.all_to_all(qkv_flat, "row", split_axis=1, concat_axis=0, tiled=True),
        lax.all_to_all(up_weight, "row", split_axis=1, concat_axis=0, tiled=True),
    )
    own_out, own_down = (
        lax.all_to_all(out_weight, "row", split_axis=0, concat_axis=1, tiled=True),
        lax.all_to_all(down_weight, "row", split_axis=0, concat_axis=1, tiled=True),
    )
    grad_totals = (
        jnp.zeros(qkv_flat.shape, jnp.float32),
        jnp.zeros((qkv_flat.shape[1],), jnp.float32),
        jnp.zeros(out_weight.shape, jnp.float32),
        jnp.zeros(out_bias.shape, jnp.float32),
        jnp.zeros(up_weight.shape, jnp.float32),
        jnp.zeros(up_bias.shape, jnp.float32),
        jnp.zeros(down_weight.shape, jnp.float32),
    )
    gain_total = jnp.zeros(norm_gain.shape, jnp.float32)
    nbias_total = jnp.zeros(norm_bias.shape, jnp.float32)
    block_outs = []
    input_grads = []
    for micro_index in range(inputs.shape[0]):
        lens = lengths[micro_index]
        x_local = inputs[micro_index].astype(jnp.float32)
        feature_sums = lax.psum((jnp.sum(x_local, 1), jnp.sum(x_local * x_local, 1)), "row")
        mean_row = feature_sums[0] / model_width
        inv_std = lax.rsqrt(feature_sums[1] / model_width - mean_row * mean_row + eps_norm)
        x_hat = (x_local - mean_row[:, None]) * inv_std[:, None]
        normed = (x_hat * norm_gain + norm_bias).astype(jnp.bfloat16)
        norm_all = lax.all_gather(normed, "col", axis=0, tiled=True)
        norm_full = lax.all_gather(norm_all, "row", axis=1, tiled=True)
        head_part = jnp.dot(norm_full, own_qkv, preferred_element_type=jnp.float32)
        up_part = jnp.dot(norm_full, own_up, preferred_element_type=jnp.float32)
        qkv_vals = head_part.reshape(rows_total, heads_local, 3, head_dim) + bias_heads
        query = rotate(qkv_vals[:, :, 0], cosine, sine_table, rot_dims).astype(jnp.bfloat16)
        keys = rotate(qkv_vals[:, :, 1], cosine, sine_table, rot_dims).astype(jnp.bfloat16)
        values = qkv_vals[:, :, 2].astype(jnp.bfloat16)
        pre_up = up_part + bias_up
        activ, gelu_pull = jax.vjp(gelu_tanh, pre_up)
        attn_out, log_norm = attend(query, keys, values, lens)
        head_all, act_all = (
            lax.all_gather(
                for_sending(attn_out.reshape(rows_total, heads_local * head_dim)),
                "row",
                axis=1,
                tiled=True,
            ),
            lax.all_gather(activ.astype(jnp.bfloat16), "row", axis=1, tiled=True),
        )
        branch = jnp.dot(head_all, out_weight, preferred_element_type=jnp.float32)
        branch = branch + jnp.dot(act_all, down_weight, preferred_element_type=jnp.float32)
        branch_mine = lax.psum_scatter(branch, "col", scatter_dimension=0, tiled=True)
        block_outs.append((x_local + (branch_mine + out_bias)).astype(jnp.bfloat16))
        valid_all = (jnp.arange(SLOT_LEN)[None, :] < lens[:, None]).reshape(rows_total)
        valid_mine = lax.dynamic_slice_in_dim(valid_all, col_index * rows_local, rows_local, 0)
        grad_mine = jnp.where(
            valid_mine[:, None], cotangent[micro_index], jnp.zeros((), jnp.bfloat16)
        )
        grad_all = lax.all_gather(grad_mine, "col", axis=0, tiled=True)
        grad_out_w = jnp.einsum("td,te->de", head_all, grad_all, preferred_element_type=jnp.float32)
        grad_down_w = jnp.einsum("tf,te->fe", act_all, grad_all, preferred_element_type=jnp.float32)
        grad_out_b = jnp.sum(grad_all, 0, dtype=jnp.float32)
        grad_full = lax.all_gather(grad_all, "row", axis=1, tiled=True)
        grad_head = jnp.einsum("te,de->td", grad_full, own_out, preferred_element_type=jnp.float32)
        grad_act = jnp.einsum("te,fe->tf", grad_full, own_down, preferred_element_type=jnp.float32)
        grad_attn = grad_head.astype(jnp.bfloat16).reshape(rows_total, heads_local, head_dim)
        grad_pre = gelu_pull(grad_act)[0].astype(jnp.bfloat16)
        grad_query, grad_keys, grad_values = attend_back(
            query, keys, values, grad_attn, log_norm, lens
        )
        grad_qkv = (
            jnp.stack(
                [
                    rotate_back(grad_query, cosine, sine_table, rot_dims),
                    rotate_back(grad_keys, cosine, sine_table, rot_dims),
                    grad_values,
                ],
                axis=2,
            )
            .astype(jnp.bfloat16)
            .reshape(rows_total, -1)
        )
        qkv_all, pre_all = (
            lax.all_gather(grad_qkv, "row", axis=1, tiled=True),
            lax.all_gather(grad_pre, "row", axis=1, tiled=True),
        )
        grad_qkv_w = jnp.einsum("td,tf->df", norm_all, qkv_all, preferred_element_type=jnp.float32)
        grad_qkv_b = jnp.sum(qkv_all, 0, dtype=jnp.float32)
        grad_up_w = jnp.einsum("td,tf->df", norm_all, pre_all, preferred_element_type=jnp.float32)
        grad_up_b = jnp.sum(pre_all, 0, dtype=jnp.float32)
        norm_part = jnp.einsum("tf,df->td", qkv_all, qkv_flat, preferred_element_type=jnp.float32)
        norm_part = norm_part + jnp.einsum(
            "tf,df->td", pre_all, up_weight, preferred_element_type=jnp.float32
        )
        grad_normed = lax.psum_scatter(norm_part, "col", scatter_dimension=0, tiled=True)
        gain_total = gain_total + jnp.sum(grad_normed * x_hat, 0)
        nbias_total = nbias_total + jnp.sum(grad_normed, 0)
        grad_hat = grad_normed * norm_gain
        back_sums = lax.psum((jnp.sum(grad_hat, 1), jnp.sum(grad_hat * x_hat, 1)), "row")
        grad_x = inv_std[:, None] * (
            grad_hat
            - back_sums[0][:, None] / model_width
            - x_hat * (back_sums[1][:, None] / model_width)
        )
        input_grads.append((grad_mine.astype(jnp.float32) + grad_x).astype(jnp.bfloat16))
        micro_grads = (
            grad_qkv_w,
            grad_qkv_b,
            grad_out_w,
            grad_out_b,
            grad_up_w,
            grad_up_b,
            grad_down_w,
        )
        grad_totals = tuple((total + piece for total, piece in zip(grad_totals, micro_grads)))
    grad_totals = jax.tree.map(
        lambda part: part.astype(jnp.float32), lax.psum(for_sending(grad_totals), "dp")
    )
    gain_grad, nbias_grad = lax.psum((gain_total, nbias_total), ("dp", "col"))
    return (
        jnp.stack(block_outs, 0),
        jnp.stack(input_grads, 0),
        gain_grad,
        nbias_grad,
        grad_totals[0].reshape(qkv_weight.shape),
        grad_totals[1].reshape(qkv_bias.shape),
        grad_totals[2],
        grad_totals[3],
        grad_totals[4],
        grad_totals[5],
        grad_totals[6],
    )


def solution(mesh):
    in_specs = (
        P(None, ("dp", "col"), "row"),
        P(None, "dp"),
        P("row"),
        P("row"),
        P("row", "col", None, None),
        P("col", None, None),
        P("col", "row"),
        P("row"),
        P("row", "col"),
        P("col"),
        P("col", "row"),
        P(None, ("dp", "col"), "row"),
    )
    out_specs = (
        P(None, ("dp", "col"), "row"),
        P(None, ("dp", "col"), "row"),
        P("row"),
        P("row"),
        P("row", "col", None, None),
        P("col", None, None),
        P("col", "row"),
        P("row"),
        P("row", "col"),
        P("col"),
        P("col", "row"),
    )
    return jax.shard_map(
        on_device, mesh=mesh, in_specs=in_specs, out_specs=out_specs, check_vma=False
    )
```

profile of v0, /device:TPU:0, one launch (start us, length us, event | category | flops | bytes accessed | tf_op | source)
XLA Modules:
  0.0 2123.7 jit_solution(2631360146051825620)
XLA Ops:
  31.0 28.6 %all-gather.17.cloned.1.call-done = bf16[2048,512]{1,0:T(8,128)(2,1)} async-done(((bf16[1024,512]{1,0:T(8,128)(2,1)}), bf16[2048,512]{1,0:T(8,128)(2,1)}) %all-gather.17.cloned.1.call-update) | async-done | bytes 2097168 | tf_op jit(solution)/shard_map/all_gather | solution.py:231
  59.7 34.6 %all-gather.33.cloned.1.call-done = bf16[2048,512]{1,0:T(8,128)(2,1)} async-done(((bf16[1024,512]{1,0:T(8,128)(2,1)}), bf16[2048,512]{1,0:T(8,128)(2,1)}) %all-gather.33.cloned.1.call-update) | async-done | bytes 2097168 | tf_op jit(solution)/shard_map/all_gather | solution.py:260
  94.4 35.2 %all-gather.25.cloned.1.call-done = bf16[2048,512]{1,0:T(8,128)(2,1)} async-done(((bf16[1024,512]{1,0:T(8,128)(2,1)}), bf16[2048,512]{1,0:T(8,128)(2,1)}) %all-gather.25.cloned.1.call-update) | async-done | bytes 2097168 | tf_op jit(solution)/shard_map/all_gather | solution.py:231
  164.1 34.9 %all-to-all-done = bf16[512,4,768]{0,2,1:T(8,128)(2,1)S(1)} async-done(((bf16[512,4,768]{0,2,1:T(8,128)(2,1)}), bf16[512,4,768]{0,2,1:T(8,128)(2,1)S(1)}, u32[]{:S(2)}, u32[]{:S(2)}) %all-to-all-start) | async-done | bytes 3145760 | tf_op jit(solution)/shard_map/all_to_all | solution.py:203
  206.0 54.0 %all-gather.19.cloned.1.call-done = bf16[2048,2048]{1,0:T(8,128)(2,1)} async-done(((bf16[2048,512]{1,0:T(8,128)(2,1)}), bf16[2048,2048]{1,0:T(8,128)(2,1)}) %all-gather.19.cloned.1.call-update) | async-done | bytes 8388624 | tf_op jit(solution)/shard_map/all_gather | solution.py:232
  280.7 33.6 %while.52 = (s32[]{:T(128)}, bf16[2,1024,4,64]{1,3,2,0:T(8,128)(2,1)}, f32[2,1024,4]{1,2,0:T(4,128)S(1)}, bf16[2,1024,4,64]{1,3,2,0:T(8,128)(2,1)}, s32[2]{0:T(1...) while((s32[]{:T(128)}, ...), condition=%wide.region_9.10_spmd, body=%wide.region_4.9_spmd.sunk | while | flops 1127482880 | bytes 71475944 | solution.py:101
  341.6 173.5 %while.54 = (s32[]{:T(128)}, f32[2,1024,4,64]{1,0,3,2:T(2,128)}, f32[2,1024,4,64]{1,0,3,2:T(2,128)}, bf16[2,1024,4,64]{1,3,2,0:T(8,128)(2,1)}, bf16[2,1024,4,64]...) while((s32[]{:T(128)}, f32[2,1024,4,64]{1,0,3,2:T(2,128)}, ...), condition=%wide.region_25.26_spmd, body=%wide.region_22.25_spmd.sunk | while | flops 2750674432 | bytes 295825888 | solution.py:155
  370.9 18.8 dynamic_update_slice.54
  397.4 18.8 dynamic_update_slice.55
  559.7 83.0 %all-to-all-done.3 = bf16[4,1024,512]{2,1,0:T(8,128)(2,1)} async-done(((bf16[4,1024,512]{2,1,0:T(8,128)(2,1)}), bf16[4,1024,512]{2,1,0:T(8,128)(2,1)}, u32[]{:S(2)}, u32[]{:S(2)}) %all-to-all-start.3) | async-done | bytes 4194336 | tf_op jit(solution)/shard_map/all_to_all | solution.py:208
  706.5 28.6 %fusion.178 = (bf16[2048,1024]{1,0:T(8,128)(2,1)}, bf16[2048,1024]{1,0:T(8,128)(2,1)}, bf16[2048,1024]{1,0:T(8,128)(2,1)}, bf16[2048,1024]{1,0:T(8,128)(2,1)}) fusion(f32[2048,1024]{1,0:T(8,128)} %fusion.242, f32[1024]{0:T(1024)S(1)} %dynamic-slice-done, f32[2048,1024]{1,0:T(8,128)} %fusion.244, f32[2048,1024]{1,0:T(8,128)} %fusion.247, ...), kind=kOutput, calls=%fused_computation.242 | convolution fusion | flops 8686403584 | bytes 54530048 | tf_op jit(solution)/shard_map/te,fe->tf/dot_general | solution.py:266
  737.5 33.7 %while.53 = (s32[]{:T(128)}, bf16[2,1024,4,64]{1,3,2,0:T(8,128)(2,1)}, f32[2,1024,4]{1,2,0:T(4,128)S(1)}, bf16[2,1024,4,64]{1,3,2,0:T(8,128)(2,1)}, s32[2]{0:T(1...) while((s32[]{:T(128)}, ...), condition=%wide.region_20.21_spmd, body=%wide.region_15.20_spmd.sunk | while | flops 1127482880 | bytes 71475944 | solution.py:101
  776.3 172.3 %while.55 = (s32[]{:T(128)}, f32[2,1024,4,64]{1,0,3,2:T(2,128)}, f32[2,1024,4,64]{1,0,3,2:T(2,128)}, bf16[2,1024,4,64]{1,3,2,0:T(8,128)(2,1)}, bf16[2,1024,4,64]...) while((s32[]{:T(128)}, f32[2,1024,4,64]{1,0,3,2:T(2,128)}, ...), condition=%wide.region_34.35_spmd, body=%wide.region_31.34_spmd.sunk | while | flops 2750674432 | bytes 295825888 | solution.py:155
  1002.4 45.4 %all-gather.45.cloned.1.call-done = bf16[2048,3072]{0,1:T(8,128)(2,1)} async-done(((bf16[2048,768]{0,1:T(8,128)(2,1)}), bf16[2048,3072]{0,1:T(8,128)(2,1)}) %all-gather.45.cloned.1.call-update) | async-done | bytes 12582928 | tf_op jit(solution)/shard_map/all_gather | solution.py:285
  1058.9 96.2 %all-gather.47.cloned.1.call-done = bf16[2048,4096]{1,0:T(8,128)(2,1)} async-done(((bf16[2048,1024]{1,0:T(8,128)(2,1)}), bf16[2048,4096]{1,0:T(8,128)(2,1)}) %all-gather.47.cloned.1.call-update) | async-done | bytes 16777232 | tf_op jit(solution)/shard_map/all_gather | solution.py:286
  1170.7 21.0 all-gather.29.cloned.1.call-done
  1198.3 100.8 %all-gather.31.cloned.1.call-done = bf16[2048,4096]{1,0:T(8,128)(2,1)} async-done(((bf16[2048,1024]{1,0:T(8,128)(2,1)}), bf16[2048,4096]{1,0:T(8,128)(2,1)}) %all-gather.31.cloned.1.call-update) | async-done | bytes 16777232 | tf_op jit(solution)/shard_map/all_gather | solution.py:249
  1315.0 20.5 all-gather.21.cloned.1.call-done
  1380.6 62.2 %all-gather.23.cloned.1.call-done = bf16[2048,4096]{1,0:T(8,128)(2,1)} async-done(((bf16[2048,1024]{1,0:T(8,128)(2,1)}), bf16[2048,4096]{1,0:T(8,128)(2,1)}) %all-gather.23.cloned.1.call-update) | async-done | bytes 16777232 | tf_op jit(solution)/shard_map/all_gather | solution.py:249
  1542.4 19.0 all-reduce.3
  1563.2 50.6 %reduce-scatter.7.cloned.1.call-done = f32[1024,512]{1,0:T(8,128)} async-done(((f32[2048,512]{1,0:T(8,128)}), f32[1024,512]{1,0:T(8,128)}) %reduce-scatter.7.cloned.1.call-update) | async-done | bytes 2097168 | tf_op jit(solution)/shard_map/reduce_scatter | solution.py:253
  1613.8 57.1 %reduce-scatter.5.cloned.1.call-done = f32[1024,512]{1,0:T(8,128)} async-done(((f32[2048,512]{1,0:T(8,128)}), f32[1024,512]{1,0:T(8,128)}) %reduce-scatter.5.cloned.1.call-update) | async-done | bytes 2097168 | tf_op jit(solution)/shard_map/reduce_scatter | solution.py:253
  1676.6 22.5 %all-reduce = (f32[512]{0:T(512)}, f32[512]{0:T(512)}) all-reduce(f32[512]{0:T(512)S(1)} %add.407, f32[512]{0:T(512)S(1)} %add.408), channel_id=1, replica_groups=mesh['dp'=4,'row'=4,'col'=2] {'dp','col'}, use_global_device_ids=true, to_apply=%region_42.43 | all-reduce | flops 1024 | bytes 8192 | tf_op jit(solution)/shard_map/psum | solution.py:320
  1718.4 381.9 %all-reduce.7.cloned.1.call-done = (bf16[512,16,3,64]{0,3,2,1:T(8,128)(2,1)}, bf16[1024,512]{1,0:T(8,128)(2,1)}, bf16[512,4096]{1,0:T(8,128)(2,1)}, bf16[4096,512]{1,0:T(8,128)(2,1)}) async-done(((bf16[512,16,3,64]{0,3,2,1:T(8,128)(2,1)}, bf16[1024,512]{1,0:T(8,128)(2,1)}, bf16[512,4096]{1,0:T(8,128)(2,1)}, bf16[4096,512]{1,0:T(8,128)(2,1)}), (bf16[512,16,3,64]{0,3,2,1:T(8,128)(2,1)}, ...) | async-done | bytes 12582928 | tf_op jit(solution)/shard_map/psum | solution.py:318
  (572 shorter events, 891.3 us)
Async XLA Ops:
  7.2 52.4 %all-gather.17.cloned.1.call-start = ((), (), s32[]{:S(2)}) async-start(), calls=%async_computation.8 | async-start | bytes 3145728 | tf_op jit(solution)/shard_map/all_gather | solution.py:231
  26.1 68.2 %all-gather.33.cloned.1.call-start = ((), (), s32[]{:S(2)}) async-start(), calls=%async_computation.18 | async-start | bytes 3145728 | tf_op jit(solution)/shard_map/all_gather | solution.py:260
  29.7 99.9 %all-gather.25.cloned.1.call-start = ((), (), s32[]{:S(2)}) async-start(), calls=%async_computation.13 | async-start | bytes 3145728 | tf_op jit(solution)/shard_map/all_gather | solution.py:231
  30.4 133.7 %all-gather.41.cloned.1.call-start = ((), (), s32[]{:S(2)}) async-start(), calls=%async_computation.23 | async-start | bytes 3145728 | tf_op jit(solution)/shard_map/all_gather | solution.py:260
  31.0 229.0 %all-gather.19.cloned.1.call-start = ((), (), s32[]{:S(2)}) async-start(), calls=%async_computation.9 | async-start | bytes 10485760 | tf_op jit(solution)/shard_map/all_gather | solution.py:232
  59.7 264.7 %all-gather.35.cloned.1.call-start = ((), (), s32[]{:S(2)}) async-start(), calls=%async_computation.19 | async-start | bytes 10485760 | tf_op jit(solution)/shard_map/all_gather | solution.py:264
  94.3 434.1 %all-gather.27.cloned.1.call-start = ((), (), s32[]{:S(2)}) async-start(), calls=%async_computation.14 | async-start | bytes 10485760 | tf_op jit(solution)/shard_map/all_gather | solution.py:232
  147.2 51.8 %all-to-all-start = ((bf16[512,4,768]{0,2,1:T(8,128)(2,1)}), bf16[512,4,768]{0,2,1:T(8,128)(2,1)S(1)}, u32[]{:S(2)}, u32[]{:S(2)}) async-start(bf16[512,4,768]{0,2,1:T(8,128)(2,1)} %bitcast.647), calls=%async_computation | async-start | bytes 6291456 | tf_op jit(solution)/shard_map/all_to_all | solution.py:203
  150.9 504.9 %all-gather.43.cloned.1.call-start = ((), (), s32[]{:S(2)}) async-start(), calls=%async_computation.24 | async-start | bytes 10485760 | tf_op jit(solution)/shard_map/all_gather | solution.py:264
  199.0 349.0 %all-to-all-start.1 = ((bf16[512,4,1024]{0,2,1:T(8,128)(2,1)}), bf16[512,4,1024]{0,2,1:T(8,128)(2,1)}, u32[]{:S(2)}, u32[]{:S(2)}) async-start(bf16[512,4,1024]{0,2,1:T(8,128)(2,1)} %bitcast.630), calls=%async_computation.1 | async-start | bytes 8388608 | tf_op jit(solution)/shard_map/all_to_all | solution.py:204
  203.8 770.1 %all-gather.37.cloned.1.call-start = ((), (), s32[]{:S(2)}) async-start(), calls=%async_computation.20 | async-start | bytes 15728640 | tf_op jit(solution)/shard_map/all_gather | solution.py:285
  547.9 94.7 %all-to-all-start.3 = ((bf16[4,1024,512]{2,1,0:T(8,128)(2,1)}), bf16[4,1024,512]{2,1,0:T(8,128)(2,1)}, u32[]{:S(2)}, u32[]{:S(2)}) async-start(bf16[4,1024,512]{2,1,0:T(8,128)(2,1)} %bitcast.637), calls=%async_computation.5 | async-start | bytes 8388608 | tf_op jit(solution)/shard_map/all_to_all | solution.py:208
  552.8 433.8 %all-gather.39.cloned.1.call-start = ((), (), s32[]{:S(2)}) async-start(), calls=%async_computation.21 | async-start | bytes 20971520 | tf_op jit(solution)/shard_map/all_gather | solution.py:286
  735.1 312.6 %all-gather.45.cloned.1.call-start = ((), (), s32[]{:S(2)}) async-start(), calls=%async_computation.25 | async-start | bytes 15728640 | tf_op jit(solution)/shard_map/all_gather | solution.py:285
  966.7 188.4 %all-gather.47.cloned.1.call-start = ((), (), s32[]{:S(2)}) async-start(), calls=%async_computation.26 | async-start | bytes 20971520 | tf_op jit(solution)/shard_map/all_gather | solution.py:286
  967.2 224.5 %all-gather.29.cloned.1.call-start = ((), (), s32[]{:S(2)}) async-start(), calls=%async_computation.15 | async-start | bytes 5242880 | tf_op jit(solution)/shard_map/all_gather | solution.py:243
  970.2 328.8 %all-gather.31.cloned.1.call-start = ((), (), s32[]{:S(2)}) async-start(), calls=%async_computation.16 | async-start | bytes 20971520 | tf_op jit(solution)/shard_map/all_gather | solution.py:249
  970.8 364.7 %all-gather.21.cloned.1.call-start = ((), (), s32[]{:S(2)}) async-start(), calls=%async_computation.10 | async-start | bytes 5242880 | tf_op jit(solution)/shard_map/all_gather | solution.py:243
  973.2 469.6 %all-gather.23.cloned.1.call-start = ((), (), s32[]{:S(2)}) async-start(), calls=%async_computation.11 | async-start | bytes 20971520 | tf_op jit(solution)/shard_map/all_gather | solution.py:249
  973.8 589.4 %reduce-scatter.9.cloned.1.call-start = ((), (), s32[]{:S(2)}) async-start(), calls=%async_computation.22 | async-start | bytes 6291456 | tf_op jit(solution)/shard_map/reduce_scatter | solution.py:296
  1002.3 560.9 %reduce-scatter.11.cloned.1.call-start = ((), (), s32[]{:S(2)}) async-start(), calls=%async_computation.27 | async-start | bytes 6291456 | tf_op jit(solution)/shard_map/reduce_scatter | solution.py:296
  1170.7 443.2 %reduce-scatter.7.cloned.1.call-start = ((), (), s32[]{:S(2)}) async-start(), calls=%async_computation.17 | async-start | bytes 6291456 | tf_op jit(solution)/shard_map/reduce_scatter | solution.py:253
  1314.5 356.4 %reduce-scatter.5.cloned.1.call-start = ((), (), s32[]{:S(2)}) async-start(), calls=%async_computation.12 | async-start | bytes 6291456 | tf_op jit(solution)/shard_map/reduce_scatter | solution.py:253
  1458.4 642.0 %all-reduce.7.cloned.1.call-start = ((), (), s32[]{:S(2)}) async-start(), calls=%async_computation.28 | async-start | bytes 25165824 | tf_op jit(solution)/shard_map/psum | solution.py:318
  (121 other events, 2117.5 us)
Sparse Core Ops, SparseCore 0:
  26.2 33.4 all-gather.16
  61.2 33.0 all-gather.32
  96.4 33.0 all-gather.24
  130.9 33.0 all-gather.40
  165.5 94.4 all-gather.18
  261.4 62.9 all-gather.34
  325.9 57.3 all-gather.26
  384.9 58.2 all-gather.42
  548.1 122.1 all-gather.36
  735.2 104.7 all-gather.38
  966.8 80.9 all-gather.44
  1049.1 105.8 all-gather.46
  1157.2 34.4 all-gather.28
  1193.1 105.8 all-gather.30
  1301.0 34.4 all-gather.20
  1336.9 105.8 all-gather.22
  1445.6 54.3 reduce-scatter.8
  1502.7 54.3 reduce-scatter.10
  1559.4 54.3 reduce-scatter.6
  1616.5 54.3 reduce-scatter.4
  1673.8 426.4 all-reduce.6
where the time goes:
time: 2140 us; the launch traced here: 2120 us
  waiting for transfers between devices  1120 us (52%)
  matrix products  452 us (21%)
  local copies, waits for them, and re-layouts  294 us (14%)
  other arithmetic  139 us (6%)
  blocking collectives  82.6 us (4%)
    psum x1, waiting for transfers between devices, on_device(): lax.psum(for_sending(grad_totals), 'dp')  382 us
    all_gather x2, waiting for transfers between devices, on_device(): lax.all_gather(activ.astype(jnp.bfloat16), 'row', axis=1, tiled=True)  163 us
    dynamic_update_slice x16, local copies, waits for them, and re-layouts, attend_back(): lax.map(one_slot, (query.reshape(slot_shape), keys.reshape(slot_shape), v...  159 us
    reduce_scatter x2, waiting for transfers between devices, on_device(): lax.psum_scatter(branch, 'col', scatter_dimension=0, tiled=True)  108 us
    all_gather x2, waiting for transfers between devices, on_device(): lax.all_gather(grad_pre, 'row', axis=1, tiled=True)  96.2 us
    all_to_all x1, waiting for transfers between devices, on_device(): lax.all_to_all(down_weight, 'row', split_axis=0, concat_axis=1, tiled=True)  83 us
    all_gather x2, waiting for transfers between devices, on_device(): norm_all = lax.all_gather(normed, 'col', axis=0, tiled=True)  63.8 us
    all_gather x2, waiting for transfers between devices, on_device(): norm_full = lax.all_gather(norm_all, 'row', axis=1, tiled=True)  54 us
  transfers between devices with their start and end apart: 24, of which 17 were waited for; matrix products, arithmetic and copies ran while one was open for 39% of the time, Pallas kernels for 0%

commit v1 on v0

v1 whole, which is shorter than its diff:
```python
from functools import partial

import jax
import jax.numpy as jnp
from jax import lax
from jax.experimental import pallas as pl
from jax.experimental.pallas import tpu as pltpu
from jax.sharding import PartitionSpec as P

SLOT_LEN = 1024
eps_norm = 1e-05
neg_big = -1e30
bf16 = jnp.bfloat16
f32 = jnp.float32

NN = (((1,), (0,)), ((), ()))
NT = (((1,), (1,)), ((), ()))
TN = (((0,), (0,)), ((), ()))


def mm(a, b, dims):
    return lax.dot_general(a, b, dims, preferred_element_type=f32)


def params(mib=56):
    return pltpu.CompilerParams(vmem_limit_bytes=mib << 20)


def whole(shape):
    return pl.BlockSpec(shape, lambda *_: (0,) * len(shape), pipeline_mode=pl.Buffered(1))


def cost(flops, *arrays):
    size = sum(a.size * a.dtype.itemsize for a in arrays)
    return pl.CostEstimate(flops=int(flops), transcendentals=0, bytes_accessed=int(size))


def sds(shape, dtype):
    return jax.ShapeDtypeStruct(shape, dtype)


def norm_kernel(x_ref, gain_ref, bias_ref, out_ref, mean_ref, inv_ref, width):
    parts = x_ref.shape[1]
    total = 0.0
    square = 0.0
    for r in range(parts):
        x = x_ref[0, r].astype(f32)
        total = total + jnp.sum(x, -1, keepdims=True)
        square = square + jnp.sum(x * x, -1, keepdims=True)
    mean = total / width
    inv = lax.rsqrt(square / width - mean * mean + eps_norm)
    mean_ref[0] = mean
    inv_ref[0] = inv
    for r in range(parts):
        x = x_ref[0, r].astype(f32)
        hat = (x - mean) * inv
        out_ref[0, r] = (hat * gain_ref[r] + bias_ref[r]).astype(bf16)


def norm_call(x_all, gain, bias):
    cols, rows, toks, feats = x_all.shape
    tb = min(512, toks)
    return pl.pallas_call(
        partial(norm_kernel, width=rows * feats),
        grid=(cols, toks // tb),
        in_specs=[
            pl.BlockSpec((1, rows, tb, feats), lambda c, t: (c, 0, t, 0)),
            whole((rows, 1, feats)),
            whole((rows, 1, feats)),
        ],
        out_specs=[
            pl.BlockSpec((1, rows, tb, feats), lambda c, t: (c, 0, t, 0)),
            pl.BlockSpec((1, tb, 1), lambda c, t: (c, t, 0)),
            pl.BlockSpec((1, tb, 1), lambda c, t: (c, t, 0)),
        ],
        out_shape=[sds(x_all.shape, bf16), sds((cols, toks, 1), f32), sds((cols, toks, 1), f32)],
        compiler_params=params(),
        cost_estimate=cost(8 * x_all.size, x_all, x_all),
        name="norm",
    )(x_all, gain.reshape(rows, 1, feats), bias.reshape(rows, 1, feats))


def project_kernel(x_ref, w_ref, out_ref):
    acc = mm(x_ref[0, 0], w_ref[0], NT)
    for r in range(1, x_ref.shape[1]):
        acc = acc + mm(x_ref[0, r], w_ref[r], NT)
    out_ref[...] = acc.astype(out_ref.dtype)


def project_call(x_all, weight, dtype, name):
    cols, rows, toks, feats = x_all.shape
    width = weight.shape[1]
    tb = min(512, toks)
    per = toks // tb
    out = sds((cols * toks, width), dtype)
    return pl.pallas_call(
        project_kernel,
        grid=(cols, per),
        in_specs=[
            pl.BlockSpec((1, rows, tb, feats), lambda c, t: (c, 0, t, 0)),
            whole(weight.shape),
        ],
        out_specs=pl.BlockSpec((tb, width), lambda c, t: (c * per + t, 0)),
        out_shape=out,
        compiler_params=params(),
        cost_estimate=cost(2 * x_all.size * width, x_all, weight, out),
        name=name,
    )(x_all, weight)


def gelu_both(v):
    k = 0.7978845608028654
    square = v * v
    th = jnp.tanh(k * v * (1.0 + 0.044715 * square))
    half = 0.5 * (1.0 + th)
    slope = half + (0.5 * k) * v * (1.0 - th * th) * (1.0 + 0.134145 * square)
    return v * half, slope


def hidden_kernel(n_ref, g_ref, up_ref, down_ref, bias_ref, act_ref, dpre_ref, sum_ref, chunk):
    @pl.when((pl.program_id(0) == 0) & (pl.program_id(1) == 0))
    def _():
        sum_ref[...] = jnp.zeros_like(sum_ref)

    rows = n_ref.shape[1]
    tb = n_ref.shape[2]
    for c in range(act_ref.shape[1] // chunk):
        cut = pl.ds(c * chunk, chunk)
        pre = mm(n_ref[0, 0], up_ref[0, :, cut], NN)
        dact = mm(g_ref[0, 0], down_ref[0, cut, :], NT)
        for r in range(1, rows):
            pre = pre + mm(n_ref[0, r], up_ref[r, :, cut], NN)
            dact = dact + mm(g_ref[0, r], down_ref[r, cut, :], NT)
        act, slope = gelu_both(pre + bias_ref[:, cut])
        dpre = (dact * slope).astype(bf16)
        act_ref[:, cut] = act.astype(bf16)
        dpre_ref[:, cut] = dpre
        sum_ref[:, cut] += jnp.sum(dpre.astype(f32).reshape(tb // 8, 8, chunk), 0)


def hidden_call(normed, grad, up, down, bias):
    cols, rows, toks, feats = normed.shape
    width = up.shape[2]
    tb = min(512, toks)
    per = toks // tb
    out = sds((cols * toks, width), bf16)
    tok_spec = pl.BlockSpec((1, rows, tb, feats), lambda c, t: (c, 0, t, 0))
    out_spec = pl.BlockSpec((tb, width), lambda c, t: (c * per + t, 0))
    return pl.pallas_call(
        partial(hidden_kernel, chunk=min(256, width)),
        grid=(cols, per),
        in_specs=[tok_spec, tok_spec, whole(up.shape), whole(down.shape), whole((1, width))],
        out_specs=[out_spec, out_spec, pl.BlockSpec((8, width), lambda c, t: (0, 0))],
        out_shape=[out, out, sds((8, width), f32)],
        compiler_params=params(),
        cost_estimate=cost(4 * normed.size * width, normed, grad, up, down, out, out),
        name="hidden",
    )(normed, grad, up, down, bias.reshape(1, width))


def combine_kernel(core_ref, a_ref, b_ref, wa_ref, wb_ref, keep_ref, send_ref, dims_b):
    core = core_ref[0]
    for j in range(keep_ref.shape[1]):
        for out_ref, r in ((send_ref, 2 * j + 1 - core), (keep_ref, 2 * j + core)):
            acc = mm(a_ref[...], wa_ref[r], NN) + mm(b_ref[...], wb_ref[r], dims_b)
            out_ref[0, j] = acc.astype(bf16)


def combine_call(core, a, b, wa, wb, dims_b, cols, feats, name):
    toks = a.shape[0] // cols
    rows = wa.shape[0]
    tb = min(512, toks)
    per = toks // tb
    out = sds((cols, rows // 2, toks, feats), bf16)
    flops = 2 * a.shape[0] * (a.shape[1] + b.shape[1]) * rows * feats
    out_spec = pl.BlockSpec((1, rows // 2, tb, feats), lambda c, t, core: (c, 0, t, 0))
    return pl.pallas_call(
        partial(combine_kernel, dims_b=dims_b),
        grid_spec=pltpu.PrefetchScalarGridSpec(
            num_scalar_prefetch=1,
            grid=(cols, per),
            in_specs=[
                pl.BlockSpec((tb, a.shape[1]), lambda c, t, core: (c * per + t, 0)),
                pl.BlockSpec((tb, b.shape[1]), lambda c, t, core: (c * per + t, 0)),
                whole(wa.shape),
                whole(wb.shape),
            ],
            out_specs=[out_spec, out_spec],
        ),
        out_shape=[out, out],
        compiler_params=params(),
        cost_estimate=cost(flops, a, b, wa, wb, out, out),
        name=name,
    )(core, a, b, wa, wb)


def wgrad_kernel(*refs, count, token_major):
    xs, ys = refs[:count], refs[count : 2 * count]
    out_ref, acc_ref = refs[2 * count :]
    step = pl.program_id(0)
    first = step == 0
    rows = out_ref.shape[0]

    for r in range(rows):
        part = 0.0
        for x_ref, y_ref in zip(xs, ys):
            x = x_ref[0, r]
            y = y_ref[...]
            part = part + (mm(x, y, TN) if token_major else mm(y, x, TN))

        @pl.when(first)
        def _():
            acc_ref[r] = part

        @pl.when(step > 0)
        def _():
            acc_ref[r] += part

    @pl.when(step == pl.num_programs(0) - 1)
    def _():
        out_ref[...] = acc_ref[...].astype(out_ref.dtype)


def wgrad_call(xs, ys, token_major, name):
    cols, rows, toks, feats = xs[0].shape
    width = ys[0].shape[1]
    tb = min(512, toks)
    per = toks // tb
    count = len(xs)
    shape = (rows, feats, width) if token_major else (rows, width, feats)
    out = sds(shape, bf16)
    return pl.pallas_call(
        partial(wgrad_kernel, count=count, token_major=token_major),
        grid=(cols * per,),
        in_specs=[pl.BlockSpec((1, rows, tb, feats), lambda t: (t // per, 0, t % per, 0))] * count
        + [pl.BlockSpec((tb, width), lambda t: (t, 0))] * count,
        out_specs=whole(shape),
        out_shape=out,
        scratch_shapes=[pltpu.VMEM(shape, f32)],
        compiler_params=params(),
        cost_estimate=cost(2 * count * xs[0].size * width, *xs, *ys, out),
        name=name,
    )(*xs, *ys)


def rotary_tables(head_dim, lanes):
    rot = head_dim // 2
    half = rot // 2
    position = jnp.arange(SLOT_LEN).astype(f32)
    frequency = 10000.0 ** (-jnp.arange(half).astype(f32) * 2.0 / rot)
    angles = position[:, None] * frequency[None, :]
    cos, sin = jnp.cos(angles), jnp.sin(angles)
    one = jnp.ones((SLOT_LEN, head_dim - rot), f32)
    zero = jnp.zeros((SLOT_LEN, half), f32)
    rest = jnp.zeros((SLOT_LEN, head_dim - rot), f32)
    keep = jnp.concatenate([cos, cos, one], 1)
    from_back = jnp.concatenate([-sin, zero, rest], 1)
    from_front = jnp.concatenate([zero, sin, rest], 1)
    return tuple(jnp.tile(t, (1, lanes // head_dim)) for t in (keep, from_back, from_front))


def attention_call(qkv, bias, datt, lens, tables, heads, head_dim):
    lanes = tables[0].shape[1]
    toks = qkv.shape[0]
    slots = toks // SLOT_LEN
    pairs = datt.shape[1] // lanes
    width = 3 * lanes

    def kernel(
        lens_ref, qkv_ref, bias_ref, datt_ref, keep_ref, back_ref, front_ref,
        attn_ref, dqkv_ref, sum_ref,
        q_s, km_s, vm_s, dq_s, dk_s, dv_s,
    ):
        half = head_dim // 4
        block = 256
        limit = lens_ref[pl.program_id(0)]
        scale = head_dim ** (-0.5)
        lane = lax.broadcasted_iota(jnp.int32, (1, lanes), 1)
        mine = [(lane >= h * head_dim) & (lane < (h + 1) * head_dim) for h in range(heads)]

        def turn(x, sign):
            back = pltpu.roll(x, lanes - half, 1)
            front = pltpu.roll(x, half, 1)
            return x * keep_ref[...] + sign * (back * back_ref[...] + front * front_ref[...])

        def head_only(x, h):
            return jnp.where(mine[h], x, jnp.zeros_like(x)) if heads > 1 else x

        def part(j):
            cut = pl.ds(j * lanes, lanes)
            return qkv_ref[:, cut] + bias_ref[:, cut]

        q_s[...] = (turn(part(0), 1.0).astype(bf16).astype(f32) * scale).astype(bf16)
        keys = turn(part(1), 1.0).astype(bf16)
        values = part(2).astype(bf16)
        for h in range(heads):
            km_s[h] = head_only(keys, h)
            vm_s[h] = head_only(values, h)
        dk_s[...] = jnp.zeros_like(dk_s)
        dv_s[...] = jnp.zeros_like(dv_s)

        for i in range(SLOT_LEN // block):
            extent = (i + 1) * block
            rows = pl.ds(i * block, block)
            seen = pl.ds(0, extent)
            q = q_s[rows, :]
            do = datt_ref[rows, :]
            row = i * block + lax.broadcasted_iota(jnp.int32, (block, 1), 0)
            last = jnp.minimum(row, limit - 1)
            col = lax.broadcasted_iota(jnp.int32, (block, extent), 1)
            allowed = col <= last
            out = jnp.zeros((block, lanes), f32)
            dq = jnp.zeros((block, lanes), f32)
            for h in range(heads):
                k = km_s[h, seen, :]
                v = vm_s[h, seen, :]
                scores = jnp.where(allowed, mm(q, k, NT), neg_big)
                top = jnp.max(scores, -1, keepdims=True)
                expo = jnp.exp(scores - top)
                probs = expo * (1.0 / jnp.sum(expo, -1, keepdims=True))
                low = probs.astype(bf16)
                out = out + mm(low, v, NN)
                dprobs = mm(do, v, NT)
                weighted = dprobs * probs
                delta = jnp.sum(weighted, -1, keepdims=True)
                dscores = (weighted - probs * delta).astype(bf16)
                dq = dq + mm(dscores, k, NN)
                dk_s[seen, :] += mm(dscores, head_only(q, h), TN)
                dv_s[seen, :] += mm(low, head_only(do, h), TN)
            attn_ref[rows, :] = out.astype(bf16)
            dq_s[rows, :] = dq * scale

        for j, value in enumerate((turn(dq_s[...], -1.0), turn(dk_s[...], -1.0), dv_s[...])):
            cut = pl.ds(j * lanes, lanes)
            rounded = value.astype(bf16)
            dqkv_ref[:, cut] = rounded
            sum_ref[:, cut] = jnp.sum(rounded.astype(f32).reshape(SLOT_LEN // 8, 8, lanes), 0)

    spec = lambda w: pl.BlockSpec((SLOT_LEN, w), lambda s, p, lens: (s, p))
    table_spec = pl.BlockSpec((SLOT_LEN, lanes), lambda s, p, lens: (0, 0), pipeline_mode=pl.Buffered(1))
    slot_lanes = lambda dt: pltpu.VMEM((SLOT_LEN, lanes), dt)
    flops = 6 * 2 * slots * pairs * heads * SLOT_LEN * SLOT_LEN * lanes
    return pl.pallas_call(
        kernel,
        grid_spec=pltpu.PrefetchScalarGridSpec(
            num_scalar_prefetch=1,
            grid=(slots, pairs),
            in_specs=[
                spec(width),
                pl.BlockSpec((1, width), lambda s, p, lens: (0, p)),
                spec(lanes),
                table_spec,
                table_spec,
                table_spec,
            ],
            out_specs=[spec(lanes), spec(width), pl.BlockSpec((8, width), lambda s, p, lens: (s, p))],
            scratch_shapes=[
                slot_lanes(bf16),
                pltpu.VMEM((heads, SLOT_LEN, lanes), bf16),
                pltpu.VMEM((heads, SLOT_LEN, lanes), bf16),
                slot_lanes(f32),
                slot_lanes(f32),
                slot_lanes(f32),
            ],
        ),
        out_shape=[
            sds(datt.shape, bf16),
            sds(qkv.shape, bf16),
            sds((8 * slots, qkv.shape[1]), f32),
        ],
        compiler_params=params(),
        cost_estimate=cost(flops, qkv, datt, datt, qkv),
        name="attention",
    )(lens, qkv, bias, datt, *tables)


def swap(value, axis, mask):
    return lax.ppermute(value, axis, [(i, i ^ mask) for i in range(lax.axis_size(axis))])


def small_sum(value, axes):
    for axis in axes:
        for bit in range(lax.axis_size(axis).bit_length() - 1):
            value = value + swap(value, axis, 1 << bit)
    return value


def small_gather(value, axis):
    size = lax.axis_size(axis)
    own = lax.axis_index(axis)
    near = jnp.stack([value] + [swap(value, axis, k) for k in range(1, size)])
    return jnp.stack([lax.dynamic_index_in_dim(near, own ^ k, 0, False) for k in range(size)])


def halve(value, dim, bit_value):
    keep = lax.dynamic_index_in_dim(value, bit_value, dim, False)
    send = lax.dynamic_index_in_dim(value, 1 - bit_value, dim, False)
    return keep, send


def scatter_sum(keep, send, row_first):
    row_index, col_index = lax.axis_index("row"), lax.axis_index("col")
    cols, half_rows, toks, feats = keep.shape
    steps = []
    for bit in range(half_rows.bit_length() - 2, -1, -1):
        steps.append(("row", 1 << (bit + 1), 1))
    col_steps = [("col", 1 << bit, 0) for bit in range(cols.bit_length() - 2, -1, -1)]
    steps = steps + col_steps if row_first else col_steps + steps
    received = swap(send, "row", 1)
    value = (keep, received)
    for axis, mask, dim in steps:
        index = lax.axis_index(axis)
        bit_value = (index // mask) % 2
        halves = []
        for part in value:
            shape = part.shape
            cut = shape[:dim] + (2, shape[dim] // 2) + shape[dim + 1 :]
            halves.append(halve(part.reshape(cut), dim, bit_value))
        (keep_a, send_a), (keep_b, send_b) = halves
        keep = keep_a.astype(f32) + keep_b.astype(f32)
        send = (send_a.astype(f32) + send_b.astype(f32)).astype(bf16)
        last = (axis, mask, dim) == steps[-1]
        value = (keep if last else keep.astype(bf16), swap(send, axis, mask))
    return value[0].reshape(toks, feats).astype(f32) + value[1].reshape(toks, feats).astype(f32)


def exchange(pieces):
    return lax.all_to_all(pieces, "row", split_axis=0, concat_axis=0, tiled=True)


def on_device(
    inputs,
    lengths,
    norm_gain,
    norm_bias,
    qkv_weight,
    qkv_bias,
    out_weight,
    out_bias,
    up_weight,
    up_bias,
    down_weight,
    cotangent,
):
    micros, toks, feats = inputs.shape
    rows, cols = lax.axis_size("row"), lax.axis_size("col")
    width = rows * feats
    row_index, col_index = lax.axis_index("row"), lax.axis_index("col")
    col_heads, _, head_dim = qkv_weight.shape[1:]
    heads_local = col_heads // rows
    group = 2 if heads_local % 2 == 0 else 1
    pairs = heads_local // group
    lanes = max(128, group * head_dim)
    spare = lanes - group * head_dim
    ff_local = up_weight.shape[1] // rows
    core = (row_index % 2).astype(jnp.int32).reshape(1)

    up_own = exchange(up_weight.reshape(feats, rows, ff_local).transpose(1, 0, 2))
    down_own = exchange(down_weight.reshape(rows, ff_local, feats))
    qkv_own = qkv_weight.transpose(1, 2, 3, 0).reshape(rows, pairs, group, 3, head_dim, feats)
    qkv_own = qkv_own.transpose(0, 1, 3, 2, 4, 5).reshape(rows, pairs, 3, group * head_dim, feats)
    qkv_own = jnp.pad(qkv_own, ((0, 0),) * 3 + ((0, spare), (0, 0)))
    qkv_own = exchange(qkv_own.reshape(rows, pairs * 3 * lanes, feats))
    out_own = out_weight.reshape(rows, pairs, group * head_dim, feats)
    out_own = jnp.pad(out_own, ((0, 0),) * 2 + ((0, spare), (0, 0)))
    out_own = exchange(out_own.reshape(rows, pairs * lanes, feats))
    bias_up = lax.dynamic_slice_in_dim(up_bias, row_index * ff_local, ff_local, 0)
    bias_qkv = lax.dynamic_slice_in_dim(qkv_bias, row_index * heads_local, heads_local, 0)
    bias_qkv = bias_qkv.reshape(pairs, group, 3, head_dim).transpose(0, 2, 1, 3)
    bias_qkv = bias_qkv.reshape(pairs, 3, group * head_dim)
    bias_qkv = jnp.pad(bias_qkv, ((0, 0),) * 2 + ((0, spare),)).reshape(1, -1)
    tables = rotary_tables(head_dim, lanes)

    norm_full = small_gather(jnp.stack([norm_gain, norm_bias]), "row")
    token = col_index * toks + jnp.arange(toks)
    x_alls, g_alls, g_mines = [], [], []
    for m in range(micros):
        valid = (token % SLOT_LEN) < lengths[m][(col_index * toks) // SLOT_LEN]
        g_mine = jnp.where(valid[:, None], cotangent[m], jnp.zeros((), bf16))
        g_mines.append(g_mine)
        shape = (cols, rows, toks, feats)
        x_alls.append(lax.all_gather(inputs[m], ("col", "row"), axis=0).reshape(shape))
        g_alls.append(lax.all_gather(g_mine, ("col", "row"), axis=0).reshape(shape))

    normeds, stats, acts, dpres, attns, dqkvs = [], [], [], [], [], []
    sums_up, sums_qkv = 0.0, 0.0
    block_outs, dnorms = [], []
    for m in range(micros):
        normed, mean, inv = norm_call(x_alls[m], norm_full[:, 0], norm_full[:, 1])
        normeds.append(normed)
        stats.append(
            tuple(lax.dynamic_index_in_dim(v, col_index, 0, False) for v in (mean, inv))
        )
        act, dpre, sum_up = hidden_call(normed, g_alls[m], up_own, down_own, bias_up)
        qkv = project_call(normed, qkv_own, f32, "qkv")
        datt = project_call(g_alls[m], out_own, bf16, "datt")
        attn, dqkv, sum_qkv = attention_call(
            qkv, bias_qkv, datt, lengths[m], tables, group, head_dim
        )
        acts.append(act)
        dpres.append(dpre)
        attns.append(attn)
        dqkvs.append(dqkv)
        sums_up = sums_up + jnp.sum(sum_up, 0)
        sums_qkv = sums_qkv + jnp.sum(sum_qkv, 0)
        keep, send = combine_call(core, attn, act, out_own, down_own, NN, cols, feats, "branch")
        branch = scatter_sum(keep, send, m % 2 == 1)
        block_outs.append((inputs[m].astype(f32) + (branch + out_bias)).astype(bf16))
        keep, send = combine_call(core, dqkv, dpre, qkv_own, up_own, NT, cols, feats, "dnormed")
        dnorms.append(scatter_sum(keep, send, m % 2 == 1))

    totals = []
    for xs, ys, token_major, name in (
        (normeds, dpres, True, "grad_up"),
        (g_alls, acts, False, "grad_down"),
        (normeds, dqkvs, False, "grad_qkv"),
        (g_alls, attns, False, "grad_out"),
    ):
        total = lax.psum(exchange(wgrad_call(xs, ys, token_major, name)), "dp")
        totals.append(total.astype(f32))
    up_grad = totals[0].transpose(1, 0, 2).reshape(up_weight.shape)
    down_grad = totals[1].reshape(down_weight.shape)
    qkv_grad = totals[2].reshape(rows, pairs, 3, lanes, feats)[:, :, :, : group * head_dim]
    qkv_grad = qkv_grad.reshape(rows, pairs, 3, group, head_dim, feats)
    qkv_grad = qkv_grad.transpose(0, 1, 3, 2, 4, 5).reshape(col_heads, 3, head_dim, feats)
    qkv_grad = qkv_grad.transpose(3, 0, 1, 2)
    out_grad = totals[3].reshape(rows, pairs, lanes, feats)[:, :, : group * head_dim]
    out_grad = out_grad.reshape(out_weight.shape)

    bias_sums = small_gather(small_sum(jnp.concatenate([sums_up, sums_qkv]), ("dp",)), "row")
    up_bias_grad = bias_sums[:, :ff_local].reshape(-1)
    qkv_bias_grad = bias_sums[:, ff_local:].reshape(rows, pairs, 3, lanes)
    qkv_bias_grad = qkv_bias_grad[..., : group * head_dim]
    qkv_bias_grad = qkv_bias_grad.reshape(rows, pairs, 3, group, head_dim).transpose(0, 1, 3, 2, 4)
    qkv_bias_grad = qkv_bias_grad.reshape(qkv_bias.shape)

    gain_sum = nbias_sum = obias_sum = 0.0
    input_grads = []
    for m in range(micros):
        mean, inv = stats[m]
        hat = (inputs[m].astype(f32) - mean) * inv
        dnormed = dnorms[m]
        gain_sum = gain_sum + jnp.sum(dnormed * hat, 0)
        nbias_sum = nbias_sum + jnp.sum(dnormed, 0)
        obias_sum = obias_sum + jnp.sum(g_mines[m].astype(f32), 0)
        dhat = dnormed * norm_gain
        row_sums = small_sum(jnp.stack([jnp.sum(dhat, 1), jnp.sum(dhat * hat, 1)]), ("row",))
        dx = inv * (dhat - row_sums[0][:, None] / width - hat * (row_sums[1][:, None] / width))
        input_grads.append((g_mines[m].astype(f32) + dx).astype(bf16))
    feature_sums = small_sum(jnp.stack([gain_sum, nbias_sum, obias_sum]), ("col", "dp"))

    return (
        jnp.stack(block_outs, 0),
        jnp.stack(input_grads, 0),
        feature_sums[0],
        feature_sums[1],
        qkv_grad,
        qkv_bias_grad,
        out_grad,
        feature_sums[2],
        up_grad,
        up_bias_grad,
        down_grad,
    )


def solution(mesh):
    in_specs = (
        P(None, ("dp", "col"), "row"),
        P(None, "dp"),
        P("row"),
        P("row"),
        P("row", "col", None, None),
        P("col", None, None),
        P("col", "row"),
        P("row"),
        P("row", "col"),
        P("col"),
        P("col", "row"),
        P(None, ("dp", "col"), "row"),
    )
    out_specs = (
        P(None, ("dp", "col"), "row"),
        P(None, ("dp", "col"), "row"),
        P("row"),
        P("row"),
        P("row", "col", None, None),
        P("col", None, None),
        P("col", "row"),
        P("row"),
        P("row", "col"),
        P("col"),
        P("col", "row"),
    )
    return jax.shard_map(
        on_device, mesh=mesh, in_specs=in_specs, out_specs=out_specs, check_vma=False
    )
```

time: 2140 us -> 1110 us (0.52)
  waiting for transfers between devices: 1120 us -> 550 us
  matrix products: 452 us -> 0 us
  Pallas kernels: 0 us -> 360 us
  local copies, waits for them, and re-layouts: 294 us -> 49.8 us
  blocking collectives: 82.6 us -> 0 us
  other arithmetic: 139 us -> 62.9 us
  starting transfers between devices: 14.7 us -> 63.9 us
    dot_general x80 -> x0, matrix products: 452 us -> none  [the longest x8 46.9 us: one_slot(): jnp.einsum('hqk,qhd->khd', probs.astype(jnp.bfloat16), grad_blk, preferre...]
    all_gather x16 -> x4, waiting for transfers between devices: 512 us -> 76.6 us  [the longest x2 76.6 us: on_device(): g_alls.append(lax.all_gather(g_mine, ('col', 'row'), axis=0).reshape(shape))]
    pallas_call x0 -> x18, Pallas kernels: none -> 360 us  [the longest x4 92.2 us: wgrad_call(): pl.pallas_call(partial(wgrad_kernel, count=count, token_major=token_major...]
    ppermute x0 -> x27, waiting for transfers between devices: none -> 164 us  [swap(): lax.ppermute(value, axis, [(i, i ^ mask) for i in range(lax.axis_size(axi...]
    dynamic_update_slice x16 -> x0, local copies, waits for them, and re-layouts: 159 us -> none  [attend_back(): lax.map(one_slot, (query.reshape(slot_shape), keys.reshape(slot_shape), v...]
    psum x1, waiting for transfers between devices: 382 us -> 223 us  [on_device(): total = lax.psum(exchange(wgrad_call(xs, ys, token_major, name)), 'dp')]
    reduce_scatter x4 -> x0, waiting for transfers between devices: 108 us -> none  [the longest x2 108 us: on_device(): lax.psum_scatter(branch, 'col', scatter_dimension=0, tiled=True)]
    psum x4 -> x0, blocking collectives: 65 us -> none  [the longest x1 22.5 us: on_device(): gain_grad, nbias_grad = lax.psum((gain_total, nbias_total), ('dp', 'col'))]
  transfers between devices with their start and end apart: 24 -> 40, of which waited for: 17 -> 14; matrix products, arithmetic and copies ran while one was open for 39% -> 8% of each run, Pallas kernels for 0% -> 33%
where the time goes in v1:
time: 1110 us; the launch traced here: 1100 us
  waiting for transfers between devices  550 us (50%)
  Pallas kernels  360 us (32%)
  starting transfers between devices  63.9 us (6%)
  other arithmetic  62.9 us (6%)
  local copies, waits for them, and re-layouts  49.8 us (4%)
  between operations  14.8 us (1%)
    psum x1, waiting for transfers between devices, on_device(): total = lax.psum(exchange(wgrad_call(xs, ys, token_major, name)), 'dp')  223 us
    ppermute x27, waiting for transfers between devices, swap(): lax.ppermute(value, axis, [(i, i ^ mask) for i in range(lax.axis_size(axi...  164 us
    pallas_call x4, Pallas kernels, wgrad_call(): pl.pallas_call(partial(wgrad_kernel, count=count, token_major=token_major...  92.2 us
    all_to_all x8, waiting for transfers between devices, exchange(): lax.all_to_all(pieces, 'row', split_axis=0, concat_axis=0, tiled=True)  85.6 us
    pallas_call x2, Pallas kernels, attention_call(): pl.pallas_call(kernel, grid_spec=pltpu.PrefetchScalarGridSpec(num_scalar_...  79.6 us
    all_gather x2, waiting for transfers between devices, on_device(): g_alls.append(lax.all_gather(g_mine, ('col', 'row'), axis=0).reshape(shape))  76.6 us
    pallas_call x4, Pallas kernels, combine_call(): pl.pallas_call(partial(combine_kernel, dims_b=dims_b), grid_spec=pltpu.Pr...  74.4 us
    pallas_call x2, Pallas kernels, hidden_call(): pl.pallas_call(partial(hidden_kernel, chunk=min(256, width)), grid=(cols,...  55.3 us
  transfers between devices with their start and end apart: 40, of which 14 were waited for; matrix products, arithmetic and copies ran while one was open for 8% of the time, Pallas kernels for 33%

profile of v1, /device:TPU:0, one launch (start us, length us, event | category | flops | bytes accessed | tf_op | source)
XLA Modules:
  0.0 1101.9 jit_solution(1147426445095738530)
XLA Ops:
  24.8 21.3 %all-to-all-done.1.w_ref.wa_ref = bf16[4,256,512]{2,1,0:T(8,128)(2,1)S(1)} async-done(((bf16[4,256,512]{2,1,0:T(8,128)(2,1)}), bf16[4,256,512]{2,1,0:T(8,128)(2,1)S(1)}, u32[]{:S(2)}, u32[]{:S(2)}) %all-to-all-start.1) | async-done | bytes 1048608 | tf_op jit(solution)/shard_map/all_to_all | solution.py:428
  64.5 44.8 %all-to-all-done.w_ref.wa_ref = bf16[4,768,512]{2,1,0:T(8,128)(2,1)} async-done(((bf16[4,768,512]{2,1,0:T(8,128)(2,1)}), bf16[4,768,512]{2,1,0:T(8,128)(2,1)}, u32[]{:S(2)}, u32[]{:S(2)}) %all-to-all-start) | async-done | bytes 3145760 | tf_op jit(solution)/shard_map/all_to_all | solution.py:428
  122.2 67.4 %collective-permute-done.1 = f32[2,512]{1,0:T(2,128)S(1)} collective-permute-done((f32[2,512]{1,0:T(2,128)S(1)}, f32[2,512]{1,0:T(2,128)S(1)}, u32[]{:S(2)}, u32[]{:S(2)}) %collective-permute-start.1) | collective-permute-done | bytes 4128 | tf_op jit(solution)/shard_map/ppermute | solution.py:378
  201.2 10.9 norm.2
  212.2 11.9 %qkv.3.qkv_ref = f32[2048,768]{1,0:T(8,128)} custom-call(bf16[2,4,1024,512]{3,2,1,0:T(8,128)(2,1)} %get-tuple-element.42.x_ref.n_ref.refs_1_, bf16[4,768,512]{2,1,0:T(8,128)(2,1)} %all-to-all-done.w_ref.wa_ref), custom_call_target="tpu_custom_call" | custom-call | flops 6442450944 | bytes 17825792 | tf_op jit(solution)/shard_map/qkv/pallas_call | solution.py:96
  224.0 11.6 %qkv.2.qkv_ref = f32[2048,768]{1,0:T(8,128)} custom-call(bf16[2,4,1024,512]{3,2,1,0:T(8,128)(2,1)} %get-tuple-element.37.x_ref.n_ref.refs_0_, bf16[4,768,512]{2,1,0:T(8,128)(2,1)} %all-to-all-done.w_ref.wa_ref), custom_call_target="tpu_custom_call" | custom-call | flops 6442450944 | bytes 17825792 | tf_op jit(solution)/shard_map/qkv/pallas_call | solution.py:96
  247.5 76.6 %all-gather.7.cloned.1.call-done = bf16[8,1024,512]{2,1,0:T(8,128)(2,1)} async-done(((bf16[1,1024,512]{2,1,0:T(8,128)(2,1)}), bf16[8,1024,512]{2,1,0:T(8,128)(2,1)}) %all-gather.7.cloned.1.call-update) | async-done | bytes 8388624 | tf_op jit(solution)/shard_map/all_gather | solution.py:483
  330.8 39.6 %attention.3 = (bf16[2048,256]{1,0:T(8,128)(2,1)}, bf16[2048,768]{1,0:T(8,128)(2,1)}, f32[16,768]{1,0:T(8,128)}) custom-call(s32[2]{0:T(128)} %get-tuple-element.156.lens_ref, f32[2048,768]{1,0:T(8,128)} %qkv.3.qkv_ref, f32[1,768]{1,0:T(1,128)} %reshape.717.bias_ref, bf16[2048,256]{1,0:T(8,128)(2,1)} %datt.3.datt_ref, f32[1024,128]{1,0:T(8,128)} %copy.54.keep_ref, ...), custom_call_target="tpu_custom_call" | custom-call | flops 12884901888 | bytes 14680064 | tf_op jit(solution)/shard_map/attention/pallas_call | solution.py:343
  370.4 40.0 %attention.2 = (bf16[2048,256]{1,0:T(8,128)(2,1)}, bf16[2048,768]{1,0:T(8,128)(2,1)}, f32[16,768]{1,0:T(8,128)}) custom-call(s32[2]{0:T(128)} %get-tuple-element.155.lens_ref, f32[2048,768]{1,0:T(8,128)} %qkv.2.qkv_ref, f32[1,768]{1,0:T(1,128)} %reshape.717.bias_ref, bf16[2048,256]{1,0:T(8,128)(2,1)} %datt.2.datt_ref, f32[1024,128]{1,0:T(8,128)} %copy.54.keep_ref, ...), custom_call_target="tpu_custom_call" | custom-call | flops 12884901888 | bytes 14680064 | tf_op jit(solution)/shard_map/attention/pallas_call | solution.py:343
  410.4 11.8 %grad_out.1 = bf16[4,256,512]{2,1,0:T(8,128)(2,1)} custom-call(bf16[2,4,1024,512]{3,2,1,0:T(8,128)(2,1)} %bitcast.141, bf16[2,4,1024,512]{3,2,1,0:T(8,128)(2,1)} %bitcast.137, bf16[2048,256]{1,0:T(8,128)(2,1)} %get-tuple-element.38.a_ref.refs_2_, bf16[2048,256]{1,0:T(8,128)(2,1)} %get-tuple-element.43.a_ref.refs_3_), custom_call_target="tpu_custom_call" | custom-call | flops 4294967296 | bytes 19922944 | tf_op jit(solution)/shard_map/grad_out/pallas_call | solution.py:232
  425.9 27.7 %hidden.3 = (bf16[2048,1024]{1,0:T(8,128)(2,1)}, bf16[2048,1024]{1,0:T(8,128)(2,1)}, f32[8,1024]{1,0:T(8,128)}) custom-call(bf16[2,4,1024,512]{3,2,1,0:T(8,128)(2,1)} %get-tuple-element.42.x_ref.n_ref.refs_1_, bf16[2,4,1024,512]{3,2,1,0:T(8,128)(2,1)} %bitcast.138, bf16[4,512,1024]{2,1,0:T(8,128)(2,1)} %all-to-all-done.2.up_ref.wb_ref, ...), custom_call_target="tpu_custom_call" | custom-call | flops 17179869184 | bytes 33554432 | tf_op jit(solution)/shard_map/hidden/pallas_call | solution.py:149
  453.6 23.0 %grad_qkv.1 = bf16[4,768,512]{2,1,0:T(8,128)(2,1)} custom-call(bf16[2,4,1024,512]{3,2,1,0:T(8,128)(2,1)} %get-tuple-element.37.x_ref.n_ref.refs_0_, bf16[2,4,1024,512]{3,2,1,0:T(8,128)(2,1)} %get-tuple-element.42.x_ref.n_ref.refs_1_, bf16[2048,768]{1,0:T(8,128)(2,1)} %get-tuple-element.48.a_ref.refs_2_, bf16[2048,768]{1,0:T(8,128)(2,1)} %get-tuple-element.54.a_ref.refs_3_), custom_call_target="tpu_custom_call" | custom-call | flops 12884901888 | bytes 26214400 | tf_op jit(solution)/shard_map/grad_qkv/pallas_call | solution.py:232
  481.5 27.7 %hidden.2 = (bf16[2048,1024]{1,0:T(8,128)(2,1)}, bf16[2048,1024]{1,0:T(8,128)(2,1)}, f32[8,1024]{1,0:T(8,128)}) custom-call(bf16[2,4,1024,512]{3,2,1,0:T(8,128)(2,1)} %get-tuple-element.37.x_ref.n_ref.refs_0_, bf16[2,4,1024,512]{3,2,1,0:T(8,128)(2,1)} %bitcast.142, bf16[4,512,1024]{2,1,0:T(8,128)(2,1)} %all-to-all-done.2.up_ref.wb_ref, ...), custom_call_target="tpu_custom_call" | custom-call | flops 17179869184 | bytes 33554432 | tf_op jit(solution)/shard_map/hidden/pallas_call | solution.py:149
  509.1 28.7 %grad_up.1 = bf16[4,512,1024]{2,1,0:T(8,128)(2,1)} custom-call(bf16[2,4,1024,512]{3,2,1,0:T(8,128)(2,1)} %get-tuple-element.37.x_ref.n_ref.refs_0_, bf16[2,4,1024,512]{3,2,1,0:T(8,128)(2,1)} %get-tuple-element.42.x_ref.n_ref.refs_1_, bf16[2048,1024]{1,0:T(8,128)(2,1)} %get-tuple-element.49.b_ref.refs_2_, bf16[2048,1024]{1,0:T(8,128)(2,1)} %get-tuple-element.55.b_ref.refs_3_), custom_call_target="tpu_custom_call" | custom-call | flops 17179869184 | bytes 29360128 | tf_op jit(solution)/shard_map/grad_up/pallas_call | solution.py:232
  543.2 28.7 %grad_down.1 = bf16[4,1024,512]{2,1,0:T(8,128)(2,1)} custom-call(bf16[2,4,1024,512]{3,2,1,0:T(8,128)(2,1)} %bitcast.143, bf16[2,4,1024,512]{3,2,1,0:T(8,128)(2,1)} %bitcast.139, bf16[2048,1024]{1,0:T(8,128)(2,1)} %get-tuple-element.39.b_ref.refs_2_, bf16[2048,1024]{1,0:T(8,128)(2,1)} %get-tuple-element.44.b_ref.refs_3_), custom_call_target="tpu_custom_call" | custom-call | flops 17179869184 | bytes 29360128 | tf_op jit(solution)/shard_map/grad_down/pallas_call | solution.py:232
  571.9 19.5 %all-to-all-done.6 = bf16[4,512,1024]{2,1,0:T(8,128)(2,1)} async-done(((bf16[4,512,1024]{2,1,0:T(8,128)(2,1)}), bf16[4,512,1024]{2,1,0:T(8,128)(2,1)}, u32[]{:S(2)}, u32[]{:S(2)}) %all-to-all-start.6) | async-done | bytes 4194336 | tf_op jit(solution)/shard_map/all_to_all | solution.py:428
  596.4 21.2 %dnormed.3 = (bf16[2,2,1024,512]{3,2,1,0:T(8,128)(2,1)}, bf16[2,2,1024,512]{3,2,1,0:T(8,128)(2,1)}) custom-call(s32[1]{0:T(128)} %bitcast.core_ref, bf16[2048,768]{1,0:T(8,128)(2,1)} %get-tuple-element.54.a_ref.refs_3_, bf16[2048,1024]{1,0:T(8,128)(2,1)} %get-tuple-element.55.b_ref.refs_3_, bf16[4,768,512]{2,1,0:T(8,128)(2,1)} %all-to-all-done.w_ref.wa_ref, ...), custom_call_target="tpu_custom_call" | custom-call | flops 15032385536 | bytes 23068672 | tf_op jit(solution)/shard_map/dnormed/pallas_call | solution.py:177
  618.0 21.2 %dnormed.2 = (bf16[2,2,1024,512]{3,2,1,0:T(8,128)(2,1)}, bf16[2,2,1024,512]{3,2,1,0:T(8,128)(2,1)}) custom-call(s32[1]{0:T(128)} %bitcast.core_ref, bf16[2048,768]{1,0:T(8,128)(2,1)} %get-tuple-element.48.a_ref.refs_2_, bf16[2048,1024]{1,0:T(8,128)(2,1)} %get-tuple-element.49.b_ref.refs_2_, bf16[4,768,512]{2,1,0:T(8,128)(2,1)} %all-to-all-done.w_ref.wa_ref, ...), custom_call_target="tpu_custom_call" | custom-call | flops 15032385536 | bytes 23068672 | tf_op jit(solution)/shard_map/dnormed/pallas_call | solution.py:177
  647.5 15.9 %branch.3 = (bf16[2,2,1024,512]{3,2,1,0:T(8,128)(2,1)}, bf16[2,2,1024,512]{3,2,1,0:T(8,128)(2,1)}) custom-call(s32[1]{0:T(128)} %bitcast.core_ref, bf16[2048,256]{1,0:T(8,128)(2,1)} %get-tuple-element.43.a_ref.refs_3_, bf16[2048,1024]{1,0:T(8,128)(2,1)} %get-tuple-element.44.b_ref.refs_3_, bf16[4,256,512]{2,1,0:T(8,128)(2,1)} %copy-done.3, ...), custom_call_target="tpu_custom_call" | custom-call | flops 10737418240 | bytes 18874368 | tf_op jit(solution)/shard_map/branch/pallas_call | solution.py:177
  663.8 16.0 %branch.2 = (bf16[2,2,1024,512]{3,2,1,0:T(8,128)(2,1)}, bf16[2,2,1024,512]{3,2,1,0:T(8,128)(2,1)}) custom-call(s32[1]{0:T(128)} %bitcast.core_ref, bf16[2048,256]{1,0:T(8,128)(2,1)} %get-tuple-element.38.a_ref.refs_2_, bf16[2048,1024]{1,0:T(8,128)(2,1)} %get-tuple-element.39.b_ref.refs_2_, bf16[4,256,512]{2,1,0:T(8,128)(2,1)} %copy-done.3, ...), custom_call_target="tpu_custom_call" | custom-call | flops 10737418240 | bytes 18874368 | tf_op jit(solution)/shard_map/branch/pallas_call | solution.py:177
  726.1 54.1 %collective-permute-done.25 = f32[1792]{0:T(1024)S(1)} collective-permute-done((f32[1792]{0:T(1024)S(1)}, f32[1792]{0:T(1024)S(1)}, u32[]{:S(2)}, u32[]{:S(2)}) %collective-permute-start.25) | collective-permute-done | bytes 7200 | tf_op jit(solution)/shard_map/ppermute | solution.py:378
  797.1 14.9 %collective-permute-done.16 = bf16[1,1,1024,512]{3,2,1,0:T(8,128)(2,1)S(1)} collective-permute-done((bf16[1,1,1024,512]{3,2,1,0:T(8,128)(2,1)}, bf16[1,1,1024,512]{3,2,1,0:T(8,128)(2,1)S(1)}, u32[]{:S(2)}, u32[]{:S(2)}) %collective-permute-start.16) | collective-permute-done | bytes 1048608 | tf_op jit(solution)/shard_map/ppermute | solution.py:378
  821.8 12.3 %collective-permute-done.8 = bf16[1,1,1024,512]{3,2,1,0:T(8,128)(2,1)S(1)} collective-permute-done((bf16[1,1,1024,512]{3,2,1,0:T(8,128)(2,1)S(1)}, bf16[1,1,1024,512]{3,2,1,0:T(8,128)(2,1)S(1)}, u32[]{:S(2)}, u32[]{:S(2)}) %collective-permute-start.8) | collective-permute-done | bytes 1048608 | tf_op jit(solution)/shard_map/ppermute | solution.py:378
  853.0 223.0 %all-reduce.3.cloned.1.call-done = (bf16[512,4096]{0,1:T(8,128)(2,1)}, bf16[512,16,3,64]{0,3,2,1:T(8,128)(2,1)}, bf16[1024,512]{1,0:T(8,128)(2,1)}, bf16[4096,512]{1,0:T(8,128)(2,1)}) async-done(((bf16[512,4096]{0,1:T(8,128)(2,1)}, bf16[512,16,3,64]{0,3,2,1:T(8,128)(2,1)}, bf16[1024,512]{1,0:T(8,128)(2,1)}, bf16[4096,512]{1,0:T(8,128)(2,1)}), (bf16[512,4096]{0,1:T(8,128)(2,1)}, ...) | async-done | bytes 12582928 | tf_op jit(solution)/shard_map/psum | solution.py:519
  (236 shorter events, 217.4 us)
Async XLA Ops:
  7.2 183.2 %all-gather.9.cloned.1.call-start = ((), (), s32[]{:S(2)}) async-start(), calls=%async_computation.10 | async-start | bytes 9437184 | tf_op jit(solution)/shard_map/all_gather | solution.py:482
  10.3 191.0 %all-gather.5.cloned.1.call-start = ((), (), s32[]{:S(2)}) async-start(), calls=%async_computation.8 | async-start | bytes 9437184 | tf_op jit(solution)/shard_map/all_gather | solution.py:482
  11.0 229.7 %all-gather.11.cloned.1.call-start = ((), (), s32[]{:S(2)}) async-start(), calls=%async_computation.11 | async-start | bytes 9437184 | tf_op jit(solution)/shard_map/all_gather | solution.py:483
  15.9 308.2 %all-gather.7.cloned.1.call-start = ((), (), s32[]{:S(2)}) async-start(), calls=%async_computation.9 | async-start | bytes 9437184 | tf_op jit(solution)/shard_map/all_gather | solution.py:483
  47.1 62.1 %all-to-all-start = ((bf16[4,768,512]{2,1,0:T(8,128)(2,1)}), bf16[4,768,512]{2,1,0:T(8,128)(2,1)}, u32[]{:S(2)}, u32[]{:S(2)}) async-start(bf16[4,768,512]{2,1,0:T(8,128)(2,1)} %bitcast.12), calls=%async_computation | async-start | bytes 6291456 | tf_op jit(solution)/shard_map/all_to_all | solution.py:428
  109.2 126.4 %all-to-all-start.2 = ((bf16[4,512,1024]{2,1,0:T(8,128)(2,1)}), bf16[4,512,1024]{2,1,0:T(8,128)(2,1)}, u32[]{:S(2)}, u32[]{:S(2)}) async-start(bf16[4,512,1024]{2,1,0:T(8,128)(2,1)} %bitcast.145), calls=%async_computation.2 | async-start | bytes 8388608 | tf_op jit(solution)/shard_map/all_to_all | solution.py:428
  114.8 74.9 %collective-permute-start.1 = (f32[2,512]{1,0:T(2,128)S(1)}, f32[2,512]{1,0:T(2,128)S(1)}, u32[]{:S(2)}, u32[]{:S(2)}) collective-permute-start(f32[2,512]{1,0:T(2,128)S(1)} %get-tuple-element.153), channel_id=1, source_target_pairs={{0,4},{2,6},{4,0},{6,2},{1,5},{3,7},{5,1},{7,3},{8,12},{10,14},{12... | collective-permute-start | bytes 12296 | tf_op jit(solution)/shard_map/ppermute | solution.py:378
  116.5 73.2 %collective-permute-start.2 = (f32[2,512]{1,0:T(2,128)S(1)}, f32[2,512]{1,0:T(2,128)S(1)}, u32[]{:S(2)}, u32[]{:S(2)}) collective-permute-start(f32[2,512]{1,0:T(2,128)S(1)} %get-tuple-element.153), channel_id=1, source_target_pairs={{0,6},{2,4},{4,2},{6,0},{1,7},{3,5},{5,3},{7,1},{8,14},{10,12},{12... | collective-permute-start | bytes 12296 | tf_op jit(solution)/shard_map/ppermute | solution.py:378
  235.6 186.6 %all-to-all-start.3 = ((bf16[4,1024,512]{2,1,0:T(8,128)(2,1)}), bf16[4,1024,512]{2,1,0:T(8,128)(2,1)}, u32[]{:S(2)}, u32[]{:S(2)}) async-start(bf16[4,1024,512]{2,1,0:T(8,128)(2,1)} %bitcast.152), calls=%async_computation.3 | async-start | bytes 8388608 | tf_op jit(solution)/shard_map/all_to_all | solution.py:428
  422.2 54.3 %all-to-all-start.5 = ((bf16[4,256,512]{2,1,0:T(8,128)(2,1)}), bf16[4,256,512]{2,1,0:T(8,128)(2,1)S(1)}, u32[]{:S(2)}, u32[]{:S(2)}) async-start(bf16[4,256,512]{2,1,0:T(8,128)(2,1)} %grad_out.1), calls=%async_computation.5 | async-start | bytes 2097152 | tf_op jit(solution)/shard_map/all_to_all | solution.py:428
  477.6 60.3 %all-to-all-start.4 = ((bf16[4,768,512]{2,1,0:T(8,128)(2,1)}), bf16[4,768,512]{2,1,0:T(8,128)(2,1)S(1)}, u32[]{:S(2)}, u32[]{:S(2)}) async-start(bf16[4,768,512]{2,1,0:T(8,128)(2,1)} %grad_qkv.1), calls=%async_computation.4 | async-start | bytes 6291456 | tf_op jit(solution)/shard_map/all_to_all | solution.py:428
  537.9 53.5 %all-to-all-start.6 = ((bf16[4,512,1024]{2,1,0:T(8,128)(2,1)}), bf16[4,512,1024]{2,1,0:T(8,128)(2,1)}, u32[]{:S(2)}, u32[]{:S(2)}) async-start(bf16[4,512,1024]{2,1,0:T(8,128)(2,1)} %grad_up.1), calls=%async_computation.6 | async-start | bytes 8388608 | tf_op jit(solution)/shard_map/all_to_all | solution.py:428
  591.4 56.1 %all-to-all-start.7 = ((bf16[4,1024,512]{2,1,0:T(8,128)(2,1)}), bf16[4,1024,512]{2,1,0:T(8,128)(2,1)}, u32[]{:S(2)}, u32[]{:S(2)}) async-start(bf16[4,1024,512]{2,1,0:T(8,128)(2,1)} %grad_down.1), calls=%async_computation.7 | async-start | bytes 8388608 | tf_op jit(solution)/shard_map/all_to_all | solution.py:428
  596.3 479.7 %all-reduce.3.cloned.1.call-start = ((), (), s32[]{:S(2)}) async-start(), calls=%async_computation.12 | async-start | bytes 25165824 | tf_op jit(solution)/shard_map/psum | solution.py:519
  617.6 62.4 %collective-permute-start.14 = (bf16[2,2,1024,512]{3,2,1,0:T(8,128)(2,1)}, bf16[2,2,1024,512]{3,2,1,0:T(8,128)(2,1)}, u32[]{:S(2)}, u32[]{:S(2)}) collective-permute-start(bf16[2,2,1024,512]{3,2,1,0:T(8,128)(2,1)} %get-tuple-element.57), channel_id=1, source_target_pairs={{0,2},{2,0},{4,6},{6,4},{1,3},{3,1},{5,7},{7,5},{8,10},{10,8},{12,... | collective-permute-start | bytes 12582920 | tf_op jit(solution)/shard_map/ppermute | solution.py:378
  639.2 49.7 %collective-permute-start.9 = (bf16[2,2,1024,512]{3,2,1,0:T(8,128)(2,1)}, bf16[2,2,1024,512]{3,2,1,0:T(8,128)(2,1)}, u32[]{:S(2)}, u32[]{:S(2)}) collective-permute-start(bf16[2,2,1024,512]{3,2,1,0:T(8,128)(2,1)} %get-tuple-element.51), channel_id=1, source_target_pairs={{0,2},{2,0},{4,6},{6,4},{1,3},{3,1},{5,7},{7,5},{8,10},{10,8},{12,... | collective-permute-start | bytes 12582920 | tf_op jit(solution)/shard_map/ppermute | solution.py:378
  663.4 32.7 %collective-permute-start.6 = (bf16[2,2,1024,512]{3,2,1,0:T(8,128)(2,1)}, bf16[2,2,1024,512]{3,2,1,0:T(8,128)(2,1)}, u32[]{:S(2)}, u32[]{:S(2)}) collective-permute-start(bf16[2,2,1024,512]{3,2,1,0:T(8,128)(2,1)} %get-tuple-element.46), channel_id=1, source_target_pairs={{0,2},{2,0},{4,6},{6,4},{1,3},{3,1},{5,7},{7,5},{8,10},{10,8},{12,... | collective-permute-start | bytes 12582920 | tf_op jit(solution)/shard_map/ppermute | solution.py:378
  686.9 96.4 %collective-permute-start.15 = (bf16[2,1,1024,512]{3,2,1,0:T(8,128)(2,1)}, bf16[2,1,1024,512]{3,2,1,0:T(8,128)(2,1)}, u32[]{:S(2)}, u32[]{:S(2)}) collective-permute-start(bf16[2,1,1024,512]{3,2,1,0:T(8,128)(2,1)} %get-tuple-element.117), channel_id=1, source_target_pairs={{0,4},{2,6},{4,0},{6,2},{1,5},{3,7},{5,1},{7,3},{8,12},{10,14},{12... | collective-permute-start | bytes 6291464 | tf_op jit(solution)/shard_map/ppermute | solution.py:378
  694.5 92.9 %collective-permute-start.10 = (bf16[1,2,1024,512]{3,2,1,0:T(8,128)(2,1)}, bf16[1,2,1024,512]{3,2,1,0:T(8,128)(2,1)}, u32[]{:S(2)}, u32[]{:S(2)}) collective-permute-start(bf16[1,2,1024,512]{3,2,1,0:T(8,128)(2,1)} %get-tuple-element.115), channel_id=1, source_target_pairs={{0,1},{1,0},{2,3},{3,2},{4,5},{5,4},{6,7},{7,6},{8,9},{9,8},{10,11... | collective-permute-start | bytes 6291464 | tf_op jit(solution)/shard_map/ppermute | solution.py:378
  701.3 91.7 %collective-permute-start.7 = (bf16[2,1,1024,512]{3,2,1,0:T(8,128)(2,1)}, bf16[2,1,1024,512]{3,2,1,0:T(8,128)(2,1)}, u32[]{:S(2)}, u32[]{:S(2)}) collective-permute-start(bf16[2,1,1024,512]{3,2,1,0:T(8,128)(2,1)} %get-tuple-element.121), channel_id=1, source_target_pairs={{0,4},{2,6},{4,0},{6,2},{1,5},{3,7},{5,1},{7,3},{8,12},{10,14},{12... | collective-permute-start | bytes 6291464 | tf_op jit(solution)/shard_map/ppermute | solution.py:378
  706.9 88.2 %collective-permute-start.4 = (bf16[1,2,1024,512]{3,2,1,0:T(8,128)(2,1)}, bf16[1,2,1024,512]{3,2,1,0:T(8,128)(2,1)}, u32[]{:S(2)}, u32[]{:S(2)}) collective-permute-start(bf16[1,2,1024,512]{3,2,1,0:T(8,128)(2,1)} %get-tuple-element.119), channel_id=1, source_target_pairs={{0,1},{1,0},{2,3},{3,2},{4,5},{5,4},{6,7},{7,6},{8,9},{9,8},{10,11... | collective-permute-start | bytes 6291464 | tf_op jit(solution)/shard_map/ppermute | solution.py:378
  724.4 55.8 %collective-permute-start.25 = (f32[1792]{0:T(1024)S(1)}, f32[1792]{0:T(1024)S(1)}, u32[]{:S(2)}, u32[]{:S(2)}) collective-permute-start(f32[1792]{0:T(1024)S(1)} %add.457), channel_id=1, source_target_pairs={{0,4},{2,6},{4,0},{6,2},{1,5},{3,7},{5,1},{7,3},{8,12},{10,14},{12... | collective-permute-start | bytes 21512 | tf_op jit(solution)/shard_map/ppermute | solution.py:378
  794.5 39.5 %collective-permute-start.8 = (bf16[1,1,1024,512]{3,2,1,0:T(8,128)(2,1)S(1)}, bf16[1,1,1024,512]{3,2,1,0:T(8,128)(2,1)S(1)}, u32[]{:S(2)}, u32[]{:S(2)}) collective-permute-start(bf16[1,1,1024,512]{3,2,1,0:T(8,128)(2,1)S(1)} %add_convert_fusion.10), channel_id=1, source_target_pairs={{0,1},{1,0},{2,3},{3,2},{4,5},{5,4},{6,7},{7,6},{8,9},{9,8},{10,11... | collective-permute-start | bytes 3145736 | tf_op jit(solution)/shard_map/ppermute | solution.py:378
  796.7 41.1 %collective-permute-start.5 = (bf16[1,1,1024,512]{3,2,1,0:T(8,128)(2,1)S(1)}, bf16[1,1,1024,512]{3,2,1,0:T(8,128)(2,1)S(1)}, u32[]{:S(2)}, u32[]{:S(2)}) collective-permute-start(bf16[1,1,1024,512]{3,2,1,0:T(8,128)(2,1)S(1)} %add_convert_fusion.11), channel_id=1, source_target_pairs={{0,4},{2,6},{4,0},{6,2},{1,5},{3,7},{5,1},{7,3},{8,12},{10,14},{12... | collective-permute-start | bytes 3145736 | tf_op jit(solution)/shard_map/ppermute | solution.py:378
  (48 other events, 676.8 us)
Sparse Core Ops, SparseCore 0:
  10.5 87.0 all-gather.8
  100.0 81.2 all-gather.4
  183.2 54.2 all-gather.10
  239.3 84.8 all-gather.6
  647.6 428.3 all-reduce.2

commit v2 on v1

--- a/solution.py
+++ b/solution.py
@@ -32,7 +32,7 @@
 
 def cost(flops, *arrays):
     size = sum(a.size * a.dtype.itemsize for a in arrays)
-    return pl.CostEstimate(flops=int(flops), transcendentals=0, bytes_accessed=int(size))
+    return pl.CostEstimate(flops=int(flops) // 64, transcendentals=0, bytes_accessed=int(size) // 64)
 
 
 def sds(shape, dtype):
@@ -80,6 +80,11 @@
     )(x_all, gain.reshape(rows, 1, feats), bias.reshape(rows, 1, feats))
 
 
+def rows_of(weight, width, index):
+    shape = (weight.shape[0], width, weight.shape[2])
+    return pl.BlockSpec(shape, lambda *_: (0, index, 0), pipeline_mode=pl.Buffered(1))
+
+
 def project_kernel(x_ref, w_ref, out_ref):
     acc = mm(x_ref[0, 0], w_ref[0], NT)
     for r in range(1, x_ref.shape[1]):
@@ -87,9 +92,8 @@
     out_ref[...] = acc.astype(out_ref.dtype)
 
 
-def project_call(x_all, weight, dtype, name):
+def project_call(x_all, weight, width, index, dtype, name):
     cols, rows, toks, feats = x_all.shape
-    width = weight.shape[1]
     tb = min(512, toks)
     per = toks // tb
     out = sds((cols * toks, width), dtype)
@@ -98,7 +102,7 @@
         grid=(cols, per),
         in_specs=[
             pl.BlockSpec((1, rows, tb, feats), lambda c, t: (c, 0, t, 0)),
-            whole(weight.shape),
+            rows_of(weight, width, index),
         ],
         out_specs=pl.BlockSpec((tb, width), lambda c, t: (c * per + t, 0)),
         out_shape=out,
@@ -158,31 +162,33 @@
     )(normed, grad, up, down, bias.reshape(1, width))
 
 
-def combine_kernel(core_ref, a_ref, b_ref, wa_ref, wb_ref, keep_ref, send_ref, dims_b):
-    core = core_ref[0]
+def combine_kernel(own_ref, a_ref, b_ref, wa_ref, wb_ref, keep_ref, send_ref, dims_b):
+    own = own_ref[0]
     for j in range(keep_ref.shape[1]):
-        for out_ref, r in ((send_ref, 2 * j + 1 - core), (keep_ref, 2 * j + core)):
+        for out_ref, k in ((send_ref, 2 * j + 1), (keep_ref, 2 * j)):
+            r = jnp.bitwise_xor(own, k)
             acc = mm(a_ref[...], wa_ref[r], NN) + mm(b_ref[...], wb_ref[r], dims_b)
             out_ref[0, j] = acc.astype(bf16)
 
 
-def combine_call(core, a, b, wa, wb, dims_b, cols, feats, name):
+def combine_call(own, a, b, wa, index, wb, dims_b, cols, feats, name):
     toks = a.shape[0] // cols
     rows = wa.shape[0]
     tb = min(512, toks)
     per = toks // tb
     out = sds((cols, rows // 2, toks, feats), bf16)
     flops = 2 * a.shape[0] * (a.shape[1] + b.shape[1]) * rows * feats
-    out_spec = pl.BlockSpec((1, rows // 2, tb, feats), lambda c, t, core: (c, 0, t, 0))
+    in_map = lambda c, t, own: (jnp.bitwise_xor(c, own[1]) * per + t, 0)
+    out_spec = pl.BlockSpec((1, rows // 2, tb, feats), lambda c, t, own: (c, 0, t, 0))
     return pl.pallas_call(
         partial(combine_kernel, dims_b=dims_b),
         grid_spec=pltpu.PrefetchScalarGridSpec(
             num_scalar_prefetch=1,
             grid=(cols, per),
             in_specs=[
-                pl.BlockSpec((tb, a.shape[1]), lambda c, t, core: (c * per + t, 0)),
-                pl.BlockSpec((tb, b.shape[1]), lambda c, t, core: (c * per + t, 0)),
-                whole(wa.shape),
+                pl.BlockSpec((tb, a.shape[1]), in_map),
+                pl.BlockSpec((tb, b.shape[1]), in_map),
+                rows_of(wa, a.shape[1], index),
                 whole(wb.shape),
             ],
             out_specs=[out_spec, out_spec],
@@ -191,56 +197,166 @@
         compiler_params=params(),
         cost_estimate=cost(flops, a, b, wa, wb, out, out),
         name=name,
-    )(core, a, b, wa, wb)
-
-
-def wgrad_kernel(*refs, count, token_major):
-    xs, ys = refs[:count], refs[count : 2 * count]
-    out_ref, acc_ref = refs[2 * count :]
+    )(own, a, b, wa, wb)
+
+
+def wgrad_kernel(own_ref, *refs, terms, count):
+    outs, acc_ref = refs[2 * terms * count : -1], refs[-1]
     step = pl.program_id(0)
-    first = step == 0
-    rows = out_ref.shape[0]
-
-    for r in range(rows):
-        part = 0.0
-        for x_ref, y_ref in zip(xs, ys):
-            x = x_ref[0, r]
-            y = y_ref[...]
-            part = part + (mm(x, y, TN) if token_major else mm(y, x, TN))
-
-        @pl.when(first)
-        def _():
-            acc_ref[r] = part
-
-        @pl.when(step > 0)
-        def _():
-            acc_ref[r] += part
+    for r in range(acc_ref.shape[0]):
+        start = 0
+        for i in range(terms):
+            xs = refs[2 * i * count : (2 * i + 1) * count]
+            ys = refs[(2 * i + 1) * count : (2 * i + 2) * count]
+            part = 0.0
+            for x_ref, y_ref in zip(xs, ys):
+                part = part + mm(y_ref[...], x_ref[0, r], TN)
+            cut = pl.ds(start, part.shape[0])
+            start += part.shape[0]
+
+            @pl.when(step == 0)
+            def _():
+                acc_ref[r, cut] = part
+
+            @pl.when(step > 0)
+            def _():
+                acc_ref[r, cut] += part
 
     @pl.when(step == pl.num_programs(0) - 1)
     def _():
-        out_ref[...] = acc_ref[...].astype(out_ref.dtype)
-
-
-def wgrad_call(xs, ys, token_major, name):
-    cols, rows, toks, feats = xs[0].shape
-    width = ys[0].shape[1]
+        per = acc_ref.shape[0] // len(outs)
+        for i, out_ref in enumerate(outs):
+            for j in range(per):
+                r = jnp.bitwise_xor(own_ref[0], i * per + j)
+                out_ref[j] = acc_ref[r].astype(bf16)
+
+
+def wgrad_call(own, pairs, chunks, name):
+    cols, rows, toks, feats = pairs[0][0][0].shape
+    width = sum(ys[0].shape[1] for _, ys in pairs)
     tb = min(512, toks)
     per = toks // tb
-    count = len(xs)
-    shape = (rows, feats, width) if token_major else (rows, width, feats)
-    out = sds(shape, bf16)
+    count = len(pairs[0][0])
+    shape = (width, feats)
+    outs = [sds((rows // chunks,) + shape, bf16)] * chunks
+    specs, arrays = [], []
+    for xs, ys in pairs:
+        specs += [pl.BlockSpec((1, rows, tb, feats), lambda t, own: (t // per, 0, t % per, 0))] * count
+        specs += [pl.BlockSpec((tb, ys[0].shape[1]), lambda t, own: (t, 0))] * count
+        arrays += xs + ys
     return pl.pallas_call(
-        partial(wgrad_kernel, count=count, token_major=token_major),
-        grid=(cols * per,),
-        in_specs=[pl.BlockSpec((1, rows, tb, feats), lambda t: (t // per, 0, t % per, 0))] * count
-        + [pl.BlockSpec((tb, width), lambda t: (t, 0))] * count,
-        out_specs=whole(shape),
+        partial(wgrad_kernel, terms=len(pairs), count=count),
+        grid_spec=pltpu.PrefetchScalarGridSpec(
+            num_scalar_prefetch=1,
+            grid=(cols * per,),
+            in_specs=specs,
+            out_specs=[whole(o.shape) for o in outs],
+            scratch_shapes=[pltpu.VMEM((rows,) + shape, f32)],
+        ),
+        out_shape=outs,
+        compiler_params=params(),
+        cost_estimate=cost(2 * count * pairs[0][0][0].size * width, *arrays, *outs),
+        name=name,
+    )(own, *arrays)
+
+
+def assemble_kernel(own_ref, *refs):
+    step, part = pl.program_id(0), pl.program_id(1)
+    out_ref = refs[-1]
+    for k in range(2):
+
+        @pl.when(step == k)
+        def _():
+            out_ref[0] = refs[k][...]
+
+    for k in range(2, len(refs) // 2 + 1):
+        near_ref, far_ref = refs[2 * k - 2 : 2 * k]
+
+        @pl.when((step == k) & (part == own_ref[1]))
+        def _():
+            out_ref[0] = near_ref[...]
+
+        @pl.when((step == k) & (part != own_ref[1]))
+        def _():
+            out_ref[0] = far_ref[...]
+
+
+def assemble_call(place, pieces, halves, name):
+    rows = len(pieces) + len(halves)
+    height, width = pieces[0].shape
+    half = height // 2
+    flat = list(pieces) + [h for pair in halves for h in pair]
+    out = sds((rows, height, width), bf16)
+
+    def in_map(k):
+        def at(i, b, place):
+            return (jnp.where(i == k, b, jnp.where(i < k, 0, 1)), 0)
+
+        return at
+
+    return pl.pallas_call(
+        assemble_kernel,
+        grid_spec=pltpu.PrefetchScalarGridSpec(
+            num_scalar_prefetch=1,
+            grid=(rows, 2),
+            in_specs=[pl.BlockSpec((half, width), in_map(k)) for k in range(2)]
+            + [pl.BlockSpec((half, width), lambda i, b, place: (0, 0))] * (len(flat) - 2),
+            out_specs=pl.BlockSpec(
+                (1, half, width), lambda i, b, place: (jnp.bitwise_xor(place[0], i), b, 0)
+            ),
+        ),
         out_shape=out,
-        scratch_shapes=[pltpu.VMEM(shape, f32)],
         compiler_params=params(),
-        cost_estimate=cost(2 * count * xs[0].size * width, *xs, *ys, out),
+        cost_estimate=cost(out.size, out, out),
         name=name,
-    )(*xs, *ys)
+    )(place, *flat)
+
+
+def place_kernel(own_ref, *refs, turned):
+    step = pl.program_id(0)
+    out_ref = refs[-1]
+    for k, piece_ref in enumerate(refs[:-1]):
+
+        @pl.when(step == k)
+        def _():
+            piece = piece_ref[...].astype(f32)
+            out_ref[...] = piece.T if turned else piece
+
+
+def place_call(own, pieces, size, index, turned, name):
+    rows = len(pieces)
+    height, width = pieces[0].shape
+    height = size
+    parts = max(1, height // 512)
+    cut = height // parts
+
+    def in_map(k):
+        def at(i, b, own):
+            return (index * parts + jnp.where(i == k, b, jnp.where(i < k, 0, parts - 1)), 0)
+
+        return at
+
+    if turned:
+        out = sds((width, rows * height), f32)
+        block = (width, cut)
+        out_map = lambda i, b, own: (0, jnp.bitwise_xor(own[0], i) * parts + b)
+    else:
+        out = sds((rows * height, width), f32)
+        block = (cut, width)
+        out_map = lambda i, b, own: (jnp.bitwise_xor(own[0], i) * parts + b, 0)
+    return pl.pallas_call(
+        partial(place_kernel, turned=turned),
+        grid_spec=pltpu.PrefetchScalarGridSpec(
+            num_scalar_prefetch=1,
+            grid=(rows, parts),
+            in_specs=[pl.BlockSpec((cut, width), in_map(k)) for k in range(rows)],
+            out_specs=pl.BlockSpec(block, out_map),
+        ),
+        out_shape=out,
+        compiler_params=params(),
+        cost_estimate=cost(out.size, out, out),
+        name=name,
+    )(own, *pieces)
 
 
 def rotary_tables(head_dim, lanes):
@@ -374,58 +490,159 @@
     )(lens, qkv, bias, datt, *tables)
 
 
+def after(value, *others):
+    return lax.optimization_barrier((value,) + others)[0]
+
+
 def swap(value, axis, mask):
     return lax.ppermute(value, axis, [(i, i ^ mask) for i in range(lax.axis_size(axis))])
 
 
-def small_sum(value, axes):
-    for axis in axes:
-        for bit in range(lax.axis_size(axis).bit_length() - 1):
-            value = value + swap(value, axis, 1 << bit)
-    return value
-
-
 def small_gather(value, axis):
+    own = lax.axis_index(axis)
     size = lax.axis_size(axis)
-    own = lax.axis_index(axis)
     near = jnp.stack([value] + [swap(value, axis, k) for k in range(1, size)])
     return jnp.stack([lax.dynamic_index_in_dim(near, own ^ k, 0, False) for k in range(size)])
 
 
-def halve(value, dim, bit_value):
-    keep = lax.dynamic_index_in_dim(value, bit_value, dim, False)
-    send = lax.dynamic_index_in_dim(value, 1 - bit_value, dim, False)
-    return keep, send
-
-
-def scatter_sum(keep, send, row_first):
-    row_index, col_index = lax.axis_index("row"), lax.axis_index("col")
-    cols, half_rows, toks, feats = keep.shape
-    steps = []
-    for bit in range(half_rows.bit_length() - 2, -1, -1):
-        steps.append(("row", 1 << (bit + 1), 1))
-    col_steps = [("col", 1 << bit, 0) for bit in range(cols.bit_length() - 2, -1, -1)]
-    steps = steps + col_steps if row_first else col_steps + steps
-    received = swap(send, "row", 1)
-    value = (keep, received)
-    for axis, mask, dim in steps:
-        index = lax.axis_index(axis)
-        bit_value = (index // mask) % 2
-        halves = []
-        for part in value:
-            shape = part.shape
-            cut = shape[:dim] + (2, shape[dim] // 2) + shape[dim + 1 :]
-            halves.append(halve(part.reshape(cut), dim, bit_value))
-        (keep_a, send_a), (keep_b, send_b) = halves
-        keep = keep_a.astype(f32) + keep_b.astype(f32)
-        send = (send_a.astype(f32) + send_b.astype(f32)).astype(bf16)
-        last = (axis, mask, dim) == steps[-1]
-        value = (keep if last else keep.astype(bf16), swap(send, axis, mask))
-    return value[0].reshape(toks, feats).astype(f32) + value[1].reshape(toks, feats).astype(f32)
-
-
-def exchange(pieces):
-    return lax.all_to_all(pieces, "row", split_axis=0, concat_axis=0, tiled=True)
+def fetch(make, name, *others):
+    rows = lax.axis_size("row")
+    own = lax.axis_index("row")
+    odd = lax.axis_index("dp") % 2
+    pieces = [make(own), swap(make(own ^ 1), "row", 1)]
+    halves = []
+    for k in range(2, rows):
+        piece = make(own ^ k)
+        half = piece.shape[0] // 2
+        out = lax.dynamic_slice_in_dim(piece, odd * half, half, 0)
+        near = swap(after(out, *others), "row", k)
+        halves.append((near, swap(near, "dp", 1)))
+    place = jnp.stack([own, odd]).astype(jnp.int32)
+
+    def assemble(dep):
+        return assemble_call(place, [after(pieces[0], dep)] + pieces[1:], halves, name)
+
+    return assemble, halves[-1][0]
+
+
+def add_low(*values):
+    return sum(v.astype(f32) for v in values).astype(bf16)
+
+
+def flips(axis, mask):
+    return axis, [(i, i ^ mask) for i in range(lax.axis_size(axis))]
+
+
+class LineSum:
+    def __init__(self):
+        self.coming, self.inner, self.middle, self.summed = [], None, None, []
+
+    def start(self):
+        self.entering = self.coming.pop(0) if self.coming else None
+        index = lax.axis_index("dp")
+        self.end = (index == 0) | (index == 3)
+        inward, outward = [(0, 1), (3, 2)], [(1, 0), (2, 3)]
+        enter, leave = self.entering, self.middle
+        self.joined = enter is not None and leave is not None and enter.shape == leave.shape
+        moves = []
+        if self.joined:
+            moves.append((jnp.where(self.end, enter, leave), "dp", inward + outward))
+        else:
+            moves += [(enter, "dp", inward)] if enter is not None else []
+            moves += [(leave, "dp", outward)] if leave is not None else []
+        if self.inner is not None:
+            moves.append((self.inner, "dp", [(1, 2), (2, 1)]))
+        return moves
+
+    def done(self, received):
+        received = list(received)
+        middle = add_low(self.inner, received.pop()) if self.inner is not None else None
+        if self.middle is not None:
+            self.summed.append(jnp.where(self.end, received[-1], self.middle))
+        inner = add_low(self.entering, received[0]) if self.entering is not None else None
+        self.inner, self.middle = inner, middle
+        return [v for v in (inner, middle) if v is not None] or [self.summed[-1]]
+
+    def finished(self):
+        return not self.coming and self.inner is None and self.middle is None
+
+
+class SmallSum:
+    def __init__(self, value, axes, gather=False):
+        self.value, self.gathered = value, []
+        bits = lambda axis: [1 << b for b in range(lax.axis_size(axis).bit_length() - 1)]
+        self.steps = [(axis, mask, False) for axis in axes for mask in bits(axis)]
+        self.steps += [("row", mask, True) for mask in bits("row")] if gather else []
+
+    def start(self):
+        return [(self.value,) + flips(*self.steps[0][:2])]
+
+    def done(self, received):
+        if self.steps[0][2]:
+            self.value = jnp.stack([self.value, received[0]])
+        else:
+            self.value = self.value + received[0]
+        self.steps = self.steps[1:]
+        return [self.value]
+
+    def finished(self):
+        return not self.steps
+
+
+class Deliver:
+    def __init__(self, line, index, first):
+        self.line, self.index, self.first = line, index, first
+        self.steps = ([first] if first else []) + [1]
+        self.value = None
+
+    def start(self):
+        if self.value is None:
+            self.value = self.line.summed[self.index]
+        if self.steps[0] == 1:
+            return [(self.value[1],) + flips("row", 1)]
+        return [(self.value,) + flips("row", self.steps[0])]
+
+    def done(self, received):
+        if self.steps[0] == 1:
+            self.pieces = [self.value[0], received[0]]
+        else:
+            self.value = received[0]
+        self.steps = self.steps[1:]
+        return received
+
+    def finished(self):
+        return not self.steps
+
+
+class ScatterSum:
+    def __init__(self, keep, send, row_first):
+        self.parts, self.out = (keep,), send
+        cols, half_rows = keep.shape[:2]
+        col_steps = [("col", 1 << bit, 0) for bit in range(cols.bit_length() - 2, -1, -1)]
+        row_steps = [("row", 2 << bit, 1) for bit in range(half_rows.bit_length() - 2, -1, -1)]
+        self.steps = [("row", 1, None)]
+        self.steps += row_steps + col_steps if row_first else col_steps + row_steps
+
+    def start(self):
+        return [(self.out,) + flips(*self.steps[0][:2])]
+
+    def done(self, received):
+        self.parts = self.parts + tuple(received)
+        self.steps = self.steps[1:]
+        if self.finished():
+            return received
+        dim = self.steps[0][2]
+        half = self.parts[0].shape[dim] // 2
+        low, high = ([lax.slice_in_dim(p, i, i + half, axis=dim) for p in self.parts] for i in (0, half))
+        self.out = add_low(*high)
+        self.parts = tuple(low)
+        return [self.out]
+
+    def finished(self):
+        return not self.steps
+
+    def total(self):
+        return sum(p[0, 0].astype(f32) for p in self.parts)
 
 
 def on_device(
@@ -452,102 +669,235 @@
     pairs = heads_local // group
     lanes = max(128, group * head_dim)
     spare = lanes - group * head_dim
+    out_width = pairs * lanes
+    qkv_width = 3 * out_width
     ff_local = up_weight.shape[1] // rows
-    core = (row_index % 2).astype(jnp.int32).reshape(1)
-
-    up_own = exchange(up_weight.reshape(feats, rows, ff_local).transpose(1, 0, 2))
-    down_own = exchange(down_weight.reshape(rows, ff_local, feats))
-    qkv_own = qkv_weight.transpose(1, 2, 3, 0).reshape(rows, pairs, group, 3, head_dim, feats)
-    qkv_own = qkv_own.transpose(0, 1, 3, 2, 4, 5).reshape(rows, pairs, 3, group * head_dim, feats)
-    qkv_own = jnp.pad(qkv_own, ((0, 0),) * 3 + ((0, spare), (0, 0)))
-    qkv_own = exchange(qkv_own.reshape(rows, pairs * 3 * lanes, feats))
-    out_own = out_weight.reshape(rows, pairs, group * head_dim, feats)
-    out_own = jnp.pad(out_own, ((0, 0),) * 2 + ((0, spare), (0, 0)))
-    out_own = exchange(out_own.reshape(rows, pairs * lanes, feats))
+    own = jnp.stack([row_index, col_index]).astype(jnp.int32)
+
+    token = col_index * toks + jnp.arange(toks)
+    g_mines, x_alls, g_alls = [], [], []
+    for m in range(micros):
+        valid = (token % SLOT_LEN) < lengths[m][(col_index * toks) // SLOT_LEN]
+        g_mines.append(jnp.where(valid[:, None], cotangent[m], jnp.zeros((), bf16)))
+        shape = (cols, rows, toks, feats)
+        x_alls.append(lax.all_gather(inputs[m], ("col", "row"), axis=0).reshape(shape))
+        g_alls.append(lax.all_gather(g_mines[m], ("col", "row"), axis=0).reshape(shape))
+
+    up_own, arrived = fetch(
+        lambda q: lax.dynamic_slice_in_dim(up_weight, q * ff_local, ff_local, 1), "up_own"
+    )
+    down_own, arrived = fetch(
+        lambda q: lax.dynamic_slice_in_dim(down_weight, q * ff_local, ff_local, 0),
+        "down_own",
+        arrived,
+    )
+    qkv_all = qkv_weight.transpose(1, 2, 3, 0).reshape(rows, pairs, group, 3, head_dim, feats)
+    qkv_all = qkv_all.transpose(0, 1, 3, 2, 4, 5).reshape(rows, pairs, 3, group * head_dim, feats)
+    qkv_all = jnp.pad(qkv_all, ((0, 0),) * 3 + ((0, spare), (0, 0)))
+    out_all = out_weight.reshape(rows, pairs, group * head_dim, feats)
+    out_all = jnp.pad(out_all, ((0, 0),) * 2 + ((0, spare), (0, 0)))
+    heads_all = jnp.concatenate(
+        [qkv_all.reshape(rows, qkv_width, feats), out_all.reshape(rows, out_width, feats)], 1
+    )
+    heads_own, _ = fetch(
+        lambda q: lax.dynamic_index_in_dim(heads_all, q, 0, False), "heads_own", arrived
+    )
     bias_up = lax.dynamic_slice_in_dim(up_bias, row_index * ff_local, ff_local, 0)
     bias_qkv = lax.dynamic_slice_in_dim(qkv_bias, row_index * heads_local, heads_local, 0)
     bias_qkv = bias_qkv.reshape(pairs, group, 3, head_dim).transpose(0, 2, 1, 3)
     bias_qkv = bias_qkv.reshape(pairs, 3, group * head_dim)
     bias_qkv = jnp.pad(bias_qkv, ((0, 0),) * 2 + ((0, spare),)).reshape(1, -1)
     tables = rotary_tables(head_dim, lanes)
-
     norm_full = small_gather(jnp.stack([norm_gain, norm_bias]), "row")
-    token = col_index * toks + jnp.arange(toks)
-    x_alls, g_alls, g_mines = [], [], []
-    for m in range(micros):
-        valid = (token % SLOT_LEN) < lengths[m][(col_index * toks) // SLOT_LEN]
-        g_mine = jnp.where(valid[:, None], cotangent[m], jnp.zeros((), bf16))
-        g_mines.append(g_mine)
-        shape = (cols, rows, toks, feats)
-        x_alls.append(lax.all_gather(inputs[m], ("col", "row"), axis=0).reshape(shape))
-        g_alls.append(lax.all_gather(g_mine, ("col", "row"), axis=0).reshape(shape))
-
-    normeds, stats, acts, dpres, attns, dqkvs = [], [], [], [], [], []
-    sums_up, sums_qkv = 0.0, 0.0
-    block_outs, dnorms = [], []
-    for m in range(micros):
-        normed, mean, inv = norm_call(x_alls[m], norm_full[:, 0], norm_full[:, 1])
+
+    normeds, stats, acts, dpres = [], [], [], []
+    weights = {}
+    qkvs, datts, attns, dqkvs = {}, {}, {}, {}
+    sums_up, sums_qkv = [], []
+    line, order = LineSum(), []
+    flows, grads = {"z": line}, {}
+
+    def norm_m(m, dep):
+        normed, mean, inv = norm_call(after(x_alls[m], dep), norm_full[:, 0], norm_full[:, 1])
         normeds.append(normed)
         stats.append(
             tuple(lax.dynamic_index_in_dim(v, col_index, 0, False) for v in (mean, inv))
         )
-        act, dpre, sum_up = hidden_call(normed, g_alls[m], up_own, down_own, bias_up)
-        qkv = project_call(normed, qkv_own, f32, "qkv")
-        datt = project_call(g_alls[m], out_own, bf16, "datt")
-        attn, dqkv, sum_qkv = attention_call(
-            qkv, bias_qkv, datt, lengths[m], tables, group, head_dim
+        return inv
+
+    def hidden_m(m, dep):
+        if not m:
+            weights["up"], weights["down"] = up_own(dep), down_own(dep)
+        normed = after(normeds[m], dep)
+        act, dpre, sum_up = hidden_call(
+            normed, g_alls[m], weights["up"], weights["down"], bias_up
         )
         acts.append(act)
         dpres.append(dpre)
-        attns.append(attn)
-        dqkvs.append(dqkv)
-        sums_up = sums_up + jnp.sum(sum_up, 0)
-        sums_qkv = sums_qkv + jnp.sum(sum_qkv, 0)
-        keep, send = combine_call(core, attn, act, out_own, down_own, NN, cols, feats, "branch")
-        branch = scatter_sum(keep, send, m % 2 == 1)
-        block_outs.append((inputs[m].astype(f32) + (branch + out_bias)).astype(bf16))
-        keep, send = combine_call(core, dqkv, dpre, qkv_own, up_own, NT, cols, feats, "dnormed")
-        dnorms.append(scatter_sum(keep, send, m % 2 == 1))
-
-    totals = []
-    for xs, ys, token_major, name in (
-        (normeds, dpres, True, "grad_up"),
-        (g_alls, acts, False, "grad_down"),
-        (normeds, dqkvs, False, "grad_qkv"),
-        (g_alls, attns, False, "grad_out"),
-    ):
-        total = lax.psum(exchange(wgrad_call(xs, ys, token_major, name)), "dp")
-        totals.append(total.astype(f32))
-    up_grad = totals[0].transpose(1, 0, 2).reshape(up_weight.shape)
-    down_grad = totals[1].reshape(down_weight.shape)
-    qkv_grad = totals[2].reshape(rows, pairs, 3, lanes, feats)[:, :, :, : group * head_dim]
+        sums_up.append(jnp.sum(sum_up, 0))
+        return sum_up
+
+    def qkv_m(m, dep):
+        if not m:
+            weights["heads"] = heads_own(dep)
+        normed = after(normeds[m], dep)
+        qkvs[m] = project_call(normed, weights["heads"], qkv_width, 0, f32, "qkv")
+        g_all = after(g_alls[m], qkvs[m])
+        datts[m] = project_call(g_all, weights["heads"], out_width, 3, bf16, "datt")
+        return datts[m]
+
+    def attention_m(m, dep):
+        datt = after(datts[m], dep)
+        attns[m], dqkvs[m], sum_qkv = attention_call(
+            qkvs[m], bias_qkv, datt, lengths[m], tables, group, head_dim
+        )
+        sums_qkv.append(jnp.sum(sum_qkv, 0))
+        return sum_qkv
+
+    def dnormed_m(m, dep):
+        dqkv = after(dqkvs[m], dep)
+        keep, send = combine_call(
+            own, dqkv, dpres[m], weights["heads"], 0, weights["up"], NT, cols, feats, "dnormed"
+        )
+        flows[f"n{m}"] = ScatterSum(keep, send, m == 0)
+        return send
+
+    def branch_m(m, dep):
+        attn = after(attns[m], dep)
+        keep, send = combine_call(
+            own, attn, acts[m], weights["heads"], 3, weights["down"], NN, cols, feats, "branch"
+        )
+        flows[f"b{m}"] = ScatterSum(keep, send, True)
+        return send
+
+    def grad_m(group_name, dep):
+        if group_name == "d":
+            terms = [(g_alls, [after(acts[0], dep)] + acts[1:])]
+        elif group_name == "u":
+            terms = [(normeds, [after(dpres[0], dep)] + dpres[1:])]
+        else:
+            dqkv = [after(dqkvs[0], dep)] + [dqkvs[m] for m in range(1, micros)]
+            terms = [(normeds, dqkv), (g_alls, [attns[m] for m in range(micros)])]
+        grads[group_name] = wgrad_call(own, terms, 2, "grad_" + group_name)
+        for i in (1, 0):
+            line.coming.append(grads[group_name][i])
+            flows[f"{group_name}{i}"] = Deliver(line, len(order), i * (rows // 2))
+            order.append(i)
+        return grads[group_name][0]
+
+    kernels = {
+        "norm": norm_m, "hidden": hidden_m, "qkv": qkv_m, "attention": attention_m,
+        "dnormed": dnormed_m, "branch": branch_m, "grad": grad_m,
+    }
+    placed = {}
+
+    def place(name):
+        parts = flows[name + "0"].pieces + flows[name + "1"].pieces
+        if name == "d":
+            placed["down"] = place_call(own, parts, ff_local, 0, False, "place_down")
+        elif name == "u":
+            placed["up"] = place_call(own, parts, ff_local, 0, True, "place_up")
+        else:
+            placed["qkv"] = place_call(own, parts, qkv_width, 0, False, "place_qkv")
+            placed["out"] = place_call(own, parts, out_width, 3, False, "place_out")
+
+    finals = {}
+
+    def sums():
+        row_parts, features = [], 0.0
+        for m in range(micros):
+            mean, inv = stats[m]
+            hat = (inputs[m].astype(f32) - mean) * inv
+            dnormed = flows[f"n{m}"].total()
+            dhat = dnormed * norm_gain
+            row_parts += [jnp.sum(dhat, 1), jnp.sum(dhat * hat, 1)]
+            finals[m] = (hat, dhat, inv)
+            features = features + jnp.stack(
+                [
+                    jnp.sum(dnormed * hat, 0),
+                    jnp.sum(dnormed, 0),
+                    jnp.sum(g_mines[m].astype(f32), 0),
+                ]
+            )
+        flows["r"] = SmallSum(jnp.stack(row_parts), ("row",))
+        flows["f"] = SmallSum(features, ("col", "dp"))
+
+    def biases_m(which, dep):
+        flows["s"] = SmallSum(jnp.concatenate([sum(sums_up), sum(sums_qkv)]), ("dp",), True)
+        return dep
+
+    def place_m(name, dep):
+        place(name)
+        return placed["down" if name == "d" else "up" if name == "u" else "out"]
+
+    kernels.update(biases=biases_m, place=place_m)
+
+    program = [
+        ((), ("norm0", "hidden0", "qkv0", "attention0")),
+        ((), ("norm1", "hidden1")),
+        ((), ("gradd",)),
+        (("z",), ("gradu", "dnormed0")),
+        (("z", "n0"), ("qkv1", "branch0")),
+        (("z", "n0", "b0"), ("attention1",)),
+        (("z", "n0", "b0"), ("gradh", "biases0")),
+        (("z", "b0", "d1", "s"), ("dnormed1", "branch1")),
+        (("z", "n1", "b1", "u1"), ()),
+        (("z", "n1", "b1", "d1", "d0", "u1", "u0"), ()),
+        (("z", "n1", "b1", "h1", "s"), ("placed", "placeu")),
+    ]
+    deps = [norm_full]
+    for names, work in program:
+        moved = []
+        for name in names:
+            if not flows[name].finished():
+                jobs = flows[name].start()
+                moved.append((flows[name], [lax.ppermute(after(v, *deps), *to) for v, *to in jobs]))
+        last = deps
+        ran = []
+        for item in work:
+            kind, which = item[:-1], item[-1]
+            dep = last[0] if len(last) == 1 else after(last[0], *last[1:])
+            last = [kernels[kind](int(which) if which.isdigit() else which, dep)]
+            ran = last
+        deps = [value for flow, values in moved for value in flow.done(values)] + ran
+    while True:
+        if "r" not in flows and all(flows[f"n{m}"].finished() for m in range(micros)):
+            sums()
+            deps = deps + [flows["r"].value]
+        left = [flow for flow in flows.values() if not flow.finished()]
+        if not left:
+            break
+        moved = [(flow, [lax.ppermute(after(v, *deps), *to) for v, *to in flow.start()]) for flow in left]
+        deps = [value for flow, values in moved for value in flow.done(values)]
+    for name in "duh":
+        if {"d": "down", "u": "up", "h": "out"}[name] not in placed:
+            place(name)
+    block_outs = [
+        (inputs[m].astype(f32) + (flows[f"b{m}"].total() + out_bias)).astype(bf16)
+        for m in range(micros)
+    ]
+    input_grads = []
+    for m in range(micros):
+        hat, dhat, inv = finals[m]
+        row_sums = flows["r"].value[2 * m : 2 * m + 2]
+        dx = inv * (dhat - row_sums[0][:, None] / width - hat * (row_sums[1][:, None] / width))
+        input_grads.append((g_mines[m].astype(f32) + dx).astype(bf16))
+    feature_sums = flows["f"].value
+    up_grad, down_grad = placed["up"], placed["down"]
+    qkv_grad, out_grad = placed["qkv"], placed["out"]
+    qkv_grad = qkv_grad.reshape(rows, pairs, 3, lanes, feats)[:, :, :, : group * head_dim]
     qkv_grad = qkv_grad.reshape(rows, pairs, 3, group, head_dim, feats)
-    qkv_grad = qkv_grad.transpose(0, 1, 3, 2, 4, 5).reshape(col_heads, 3, head_dim, feats)
-    qkv_grad = qkv_grad.transpose(3, 0, 1, 2)
-    out_grad = totals[3].reshape(rows, pairs, lanes, feats)[:, :, : group * head_dim]
+    qkv_grad = qkv_grad.transpose(5, 0, 1, 3, 2, 4).reshape(qkv_weight.shape)
+    out_grad = out_grad.reshape(rows, pairs, lanes, feats)[:, :, : group * head_dim]
     out_grad = out_grad.reshape(out_weight.shape)
 
-    bias_sums = small_gather(small_sum(jnp.concatenate([sums_up, sums_qkv]), ("dp",)), "row")
+    near = flows["s"].value.reshape(rows, -1)
+    bias_sums = jnp.take(near, row_index ^ jnp.arange(rows), axis=0)
     up_bias_grad = bias_sums[:, :ff_local].reshape(-1)
     qkv_bias_grad = bias_sums[:, ff_local:].reshape(rows, pairs, 3, lanes)
     qkv_bias_grad = qkv_bias_grad[..., : group * head_dim]
     qkv_bias_grad = qkv_bias_grad.reshape(rows, pairs, 3, group, head_dim).transpose(0, 1, 3, 2, 4)
     qkv_bias_grad = qkv_bias_grad.reshape(qkv_bias.shape)
-
-    gain_sum = nbias_sum = obias_sum = 0.0
-    input_grads = []
-    for m in range(micros):
-        mean, inv = stats[m]
-        hat = (inputs[m].astype(f32) - mean) * inv
-        dnormed = dnorms[m]
-        gain_sum = gain_sum + jnp.sum(dnormed * hat, 0)
-        nbias_sum = nbias_sum + jnp.sum(dnormed, 0)
-        obias_sum = obias_sum + jnp.sum(g_mines[m].astype(f32), 0)
-        dhat = dnormed * norm_gain
-        row_sums = small_sum(jnp.stack([jnp.sum(dhat, 1), jnp.sum(dhat * hat, 1)]), ("row",))
-        dx = inv * (dhat - row_sums[0][:, None] / width - hat * (row_sums[1][:, None] / width))
-        input_grads.append((g_mines[m].astype(f32) + dx).astype(bf16))
-    feature_sums = small_sum(jnp.stack([gain_sum, nbias_sum, obias_sum]), ("col", "dp"))
 
     return (
         jnp.stack(block_outs, 0),

time: 1110 us -> 885 us (0.80)
  waiting for transfers between devices: 550 us -> 230 us
  Pallas kernels: 360 us -> 413 us
  other arithmetic: 62.9 us -> 91.6 us
  starting transfers between devices: 63.9 us -> 77 us
    psum x1 -> x0, waiting for transfers between devices: 223 us -> none  [on_device(): total = lax.psum(exchange(wgrad_call(xs, ys, token_major, name)), 'dp')]
    ppermute x0 -> x44, waiting for transfers between devices: none -> 145 us  [on_device(): lax.ppermute(after(v, *deps), *to)]
    ppermute x27 -> x18, waiting for transfers between devices: 164 us -> 76.5 us  [swap(): lax.ppermute(value, axis, [(i, i ^ mask) for i in range(lax.axis_size(axi...]
    all_to_all x8 -> x0, waiting for transfers between devices: 85.6 us -> none  [exchange(): lax.all_to_all(pieces, 'row', split_axis=0, concat_axis=0, tiled=True)]
    all_gather x2, waiting for transfers between devices: 76.6 us -> 6.82 us  [on_device(): lax.all_gather(g_mines[m], ('col', 'row'), axis=0).reshape(shape)]
    ppermute x0 -> x44, starting transfers between devices: none -> 56.3 us  [on_device(): lax.ppermute(after(v, *deps), *to)]
    pallas_call x4 -> x10, Pallas kernels: 92.2 us -> 142 us  [the longest x3 92.8 us: wgrad_call(): pl.pallas_call(partial(wgrad_kernel, terms=len(pairs), count=count), grid...]
    all_to_all x8 -> x0, starting transfers between devices: 36.9 us -> none  [exchange(): lax.all_to_all(pieces, 'row', split_axis=0, concat_axis=0, tiled=True)]
  transfers between devices with their start and end apart: 40 -> 66, of which waited for: 14 -> 21; matrix products, arithmetic and copies ran while one was open for 8% -> 14% of each run, Pallas kernels for 33% -> 41%
where the time goes in v2:
time: 885 us; the launch traced here: 878 us
  Pallas kernels  413 us (47%)
  waiting for transfers between devices  230 us (26%)
  other arithmetic  91.6 us (10%)
  starting transfers between devices  77 us (9%)
  local copies, waits for them, and re-layouts  52 us (6%)
  between operations  15.1 us (2%)
    ppermute x44, waiting for transfers between devices, on_device(): lax.ppermute(after(v, *deps), *to)  145 us
    pallas_call x3, Pallas kernels, wgrad_call(): pl.pallas_call(partial(wgrad_kernel, terms=len(pairs), count=count), grid...  92.8 us
    pallas_call x2, Pallas kernels, attention_call(): pl.pallas_call(kernel, grid_spec=pltpu.PrefetchScalarGridSpec(num_scalar_...  79.7 us
    pallas_call x4, Pallas kernels, combine_call(): pl.pallas_call(partial(combine_kernel, dims_b=dims_b), grid_spec=pltpu.Pr...  77.5 us
    ppermute x18, waiting for transfers between devices, swap(): lax.ppermute(value, axis, [(i, i ^ mask) for i in range(lax.axis_size(axi...  76.5 us
    ppermute x44, starting transfers between devices, on_device(): lax.ppermute(after(v, *deps), *to)  56.3 us
    pallas_call x2, Pallas kernels, hidden_call(): pl.pallas_call(partial(hidden_kernel, chunk=min(256, width)), grid=(cols,...  55.6 us
    pallas_call x4, Pallas kernels, project_call(): pl.pallas_call(project_kernel, grid=(cols, per), in_specs=[pl.BlockSpec((...  36.5 us
  transfers between devices with their start and end apart: 66, of which 21 were waited for; matrix products, arithmetic and copies ran while one was open for 14% of the time, Pallas kernels for 41%

profile of v2, /device:TPU:0, one launch (start us, length us, event | category | flops | bytes accessed | tf_op | source)
XLA Modules:
  0.0 878.5 jit_solution(13013128832938201683)
XLA Ops:
  29.3 15.3 %collective-permute-done.6.refs_4_ = bf16[256,1024]{1,0:T(8,128)(2,1)} collective-permute-done((bf16[256,1024]{1,0:T(8,128)(2,1)}, bf16[256,1024]{1,0:T(8,128)(2,1)}, u32[]{:S(2)}, u32[]{:S(2)}) %collective-permute-start.6) | collective-permute-done | bytes 524320 | tf_op jit(solution)/shard_map/ppermute | solution.py:498
  63.7 18.8 %collective-permute-done.11.refs_4_ = bf16[512,512]{1,0:T(8,128)(2,1)} collective-permute-done((bf16[512,512]{1,0:T(8,128)(2,1)}, bf16[512,512]{1,0:T(8,128)(2,1)}, u32[]{:S(2)}, u32[]{:S(2)}) %collective-permute-start.11) | collective-permute-done | bytes 524320 | tf_op jit(solution)/shard_map/ppermute | solution.py:498
  90.8 11.4 %collective-permute-done.9.refs_2_ = bf16[512,512]{1,0:T(8,128)(2,1)} collective-permute-done((bf16[512,512]{1,0:T(8,128)(2,1)}, bf16[512,512]{1,0:T(8,128)(2,1)}, u32[]{:S(2)}, u32[]{:S(2)}) %collective-permute-start.9) | collective-permute-done | bytes 524320 | tf_op jit(solution)/shard_map/ppermute | solution.py:498
  120.3 15.7 %collective-permute-done.16.refs_4_ = bf16[512,512]{1,0:T(8,128)(2,1)S(1)} collective-permute-done((bf16[512,512]{1,0:T(8,128)(2,1)}, bf16[512,512]{1,0:T(8,128)(2,1)S(1)}, u32[]{:S(2)}, u32[]{:S(2)}) %collective-permute-start.16) | collective-permute-done | bytes 524320 | tf_op jit(solution)/shard_map/ppermute | solution.py:498
  138.2 10.9 %norm.2 = (bf16[2,4,1024,512]{3,2,1,0:T(8,128)(2,1)}, f32[2,1024,1]{2,1,0:T(8,128)}, f32[2,1024,1]{2,1,0:T(8,128)}) custom-call(bf16[2,4,1024,512]{3,2,1,0:T(8,128)(2,1)} %bitcast.180, f32[4,1,512]{2,1,0:T(1,128)} %get-tuple-element.262.gain_ref, f32[4,1,512]{2,1,0:T(1,128)} %get-tuple-element.261.bias_ref), custom_call_target="tpu_custom_call" | custom-call | flops 524288 | bytes 262144 | tf_op jit(solution)/shard_map/norm/pallas_call | solution.py:63
  163.9 27.6 %hidden.2 = (bf16[2048,1024]{1,0:T(8,128)(2,1)}, bf16[2048,1024]{1,0:T(8,128)(2,1)}, f32[8,1024]{1,0:T(8,128)}) custom-call(bf16[2,4,1024,512]{3,2,1,0:T(8,128)(2,1)} %get-tuple-element.115.n_ref.x_ref.refs_0_, bf16[2,4,1024,512]{3,2,1,0:T(8,128)(2,1)} %bitcast.169, bf16[4,512,1024]{2,1,0:T(8,128)(2,1)} %up_own.1.up_ref.wb_ref, ...), custom_call_target="tpu_custom_call" | custom-call | flops 268435456 | bytes 524288 | tf_op jit(solution)/shard_map/hidden/pallas_call | solution.py:153
  201.3 11.6 %qkv.2.qkv_ref = f32[2048,768]{1,0:T(8,128)} custom-call(bf16[2,4,1024,512]{3,2,1,0:T(8,128)(2,1)} %get-tuple-element.115.n_ref.x_ref.refs_0_, bf16[4,1024,512]{2,1,0:T(8,128)(2,1)} %heads_own.1.w_ref.wa_ref), custom_call_target="tpu_custom_call" | custom-call | flops 100663296 | bytes 294912 | tf_op jit(solution)/shard_map/qkv/pallas_call | solution.py:100
  219.6 39.8 %attention.2 = (bf16[2048,256]{1,0:T(8,128)(2,1)}, bf16[2048,768]{1,0:T(8,128)(2,1)}, f32[16,768]{1,0:T(8,128)}) custom-call(s32[2]{0:T(128)} %get-tuple-element.278.lens_ref, f32[2048,768]{1,0:T(8,128)} %qkv.2.qkv_ref, f32[1,768]{1,0:T(1,128)} %reshape.653.bias_ref, bf16[2048,256]{1,0:T(8,128)(2,1)} %datt.2.datt_ref, f32[1024,128]{1,0:T(8,128)} %copy.38.keep_ref, ...), custom_call_target="tpu_custom_call" | custom-call | flops 201326592 | bytes 229376 | tf_op jit(solution)/shard_map/attention/pallas_call | solution.py:459
  259.4 10.7 %norm.3 = (bf16[2,4,1024,512]{3,2,1,0:T(8,128)(2,1)}, f32[2,1024,1]{2,1,0:T(8,128)}, f32[2,1024,1]{2,1,0:T(8,128)}) custom-call(bf16[2,4,1024,512]{3,2,1,0:T(8,128)(2,1)} %bitcast.181, f32[4,1,512]{2,1,0:T(1,128)} %get-tuple-element.262.gain_ref, f32[4,1,512]{2,1,0:T(1,128)} %get-tuple-element.261.bias_ref), custom_call_target="tpu_custom_call" | custom-call | flops 524288 | bytes 262144 | tf_op jit(solution)/shard_map/norm/pallas_call | solution.py:63
  276.7 28.0 %hidden.3 = (bf16[2048,1024]{1,0:T(8,128)(2,1)}, bf16[2048,1024]{1,0:T(8,128)(2,1)}, f32[8,1024]{1,0:T(8,128)}) custom-call(bf16[2,4,1024,512]{3,2,1,0:T(8,128)(2,1)} %get-tuple-element.130.x_ref.n_ref.refs_1_, bf16[2,4,1024,512]{3,2,1,0:T(8,128)(2,1)} %bitcast.173, bf16[4,512,1024]{2,1,0:T(8,128)(2,1)} %up_own.1.up_ref.wb_ref, ...), custom_call_target="tpu_custom_call" | custom-call | flops 268435456 | bytes 524288 | tf_op jit(solution)/shard_map/hidden/pallas_call | solution.py:153
  304.7 29.3 %grad_d.1 = (bf16[2,1024,512]{2,1,0:T(8,128)(2,1)}, bf16[2,1024,512]{2,1,0:T(8,128)(2,1)}) custom-call(s32[2]{0:T(128)} %pad_add_fusion.own_ref, bf16[2,4,1024,512]{3,2,1,0:T(8,128)(2,1)} %bitcast.171, bf16[2,4,1024,512]{3,2,1,0:T(8,128)(2,1)} %bitcast.174, bf16[2048,1024]{1,0:T(8,128)(2,1)} %get-tuple-element.132.b_ref.refs_2_, ...), custom_call_target="tpu_custom_call" | custom-call | flops 268435456 | bytes 458752 | tf_op jit(solution)/shard_map/grad_d/pallas_call | solution.py:247
  337.6 29.5 %grad_u.1 = (bf16[2,1024,512]{2,1,0:T(8,128)(2,1)}, bf16[2,1024,512]{2,1,0:T(8,128)(2,1)}) custom-call(s32[2]{0:T(128)} %pad_add_fusion.own_ref, bf16[2,4,1024,512]{3,2,1,0:T(8,128)(2,1)} %get-tuple-element.115.n_ref.x_ref.refs_0_, bf16[2,4,1024,512]{3,2,1,0:T(8,128)(2,1)} %get-tuple-element.130.x_ref.n_ref.refs_1_, ...), custom_call_target="tpu_custom_call" | custom-call | flops 268435456 | bytes 458752 | tf_op jit(solution)/shard_map/grad_u/pallas_call | solution.py:247
  367.1 22.1 %dnormed.2 = (bf16[2,2,1024,512]{3,2,1,0:T(8,128)(2,1)}, bf16[2,2,1024,512]{3,2,1,0:T(8,128)(2,1)}) custom-call(s32[2]{0:T(128)} %pad_add_fusion.own_ref, bf16[2048,768]{1,0:T(8,128)(2,1)} %get-tuple-element.142.a_ref.refs_2_, bf16[2048,1024]{1,0:T(8,128)(2,1)} %get-tuple-element.139.refs_2_.b_ref, bf16[4,1024,512]{2,1,0:T(8,128)(2,1)} %heads_own.1.w_ref.wa_ref, ...), custom_call_target="tpu_custom_call" | custom-call | flops 234881024 | bytes 376832 | tf_op jit(solution)/shard_map/dnormed/pallas_call | solution.py:183
  395.8 11.4 %qkv.3.qkv_ref = f32[2048,768]{1,0:T(8,128)} custom-call(bf16[2,4,1024,512]{3,2,1,0:T(8,128)(2,1)} %get-tuple-element.130.x_ref.n_ref.refs_1_, bf16[4,1024,512]{2,1,0:T(8,128)(2,1)} %heads_own.1.w_ref.wa_ref), custom_call_target="tpu_custom_call" | custom-call | flops 100663296 | bytes 294912 | tf_op jit(solution)/shard_map/qkv/pallas_call | solution.py:100
  414.0 16.7 %branch.2 = (bf16[2,2,1024,512]{3,2,1,0:T(8,128)(2,1)}, bf16[2,2,1024,512]{3,2,1,0:T(8,128)(2,1)}) custom-call(s32[2]{0:T(128)} %pad_add_fusion.own_ref, bf16[2048,256]{1,0:T(8,128)(2,1)} %get-tuple-element.125.a_ref.refs_6_, bf16[2048,1024]{1,0:T(8,128)(2,1)} %get-tuple-element.132.b_ref.refs_2_, bf16[4,1024,512]{2,1,0:T(8,128)(2,1)} %heads_own.1.w_ref.wa_ref, ...), custom_call_target="tpu_custom_call" | custom-call | flops 167772160 | bytes 344064 | tf_op jit(solution)/shard_map/branch/pallas_call | solution.py:183
  456.3 39.9 %attention.3 = (bf16[2048,256]{1,0:T(8,128)(2,1)}, bf16[2048,768]{1,0:T(8,128)(2,1)}, f32[16,768]{1,0:T(8,128)}) custom-call(s32[2]{0:T(128)} %get-tuple-element.279.lens_ref, f32[2048,768]{1,0:T(8,128)} %qkv.3.qkv_ref, f32[1,768]{1,0:T(1,128)} %reshape.653.bias_ref, bf16[2048,256]{1,0:T(8,128)(2,1)} %datt.3.datt_ref, f32[1024,128]{1,0:T(8,128)} %copy.38.keep_ref, ...), custom_call_target="tpu_custom_call" | custom-call | flops 201326592 | bytes 229376 | tf_op jit(solution)/shard_map/attention/pallas_call | solution.py:459
  518.6 34.0 %grad_h.1 = (bf16[2,1024,512]{2,1,0:T(8,128)(2,1)}, bf16[2,1024,512]{2,1,0:T(8,128)(2,1)}) custom-call(s32[2]{0:T(128)} %pad_add_fusion.own_ref, bf16[2,4,1024,512]{3,2,1,0:T(8,128)(2,1)} %get-tuple-element.115.n_ref.x_ref.refs_0_, bf16[2,4,1024,512]{3,2,1,0:T(8,128)(2,1)} %get-tuple-element.130.x_ref.n_ref.refs_1_, ...), custom_call_target="tpu_custom_call" | custom-call | flops 268435456 | bytes 720896 | tf_op jit(solution)/shard_map/grad_h/pallas_call | solution.py:247
  582.6 22.1 %dnormed.3 = (bf16[2,2,1024,512]{3,2,1,0:T(8,128)(2,1)}, bf16[2,2,1024,512]{3,2,1,0:T(8,128)(2,1)}) custom-call(s32[2]{0:T(128)} %pad_add_fusion.own_ref, bf16[2048,768]{1,0:T(8,128)(2,1)} %get-tuple-element.158.refs_3_.a_ref, bf16[2048,1024]{1,0:T(8,128)(2,1)} %get-tuple-element.140.refs_3_.b_ref, bf16[4,1024,512]{2,1,0:T(8,128)(2,1)} %heads_own.1.w_ref.wa_ref, ...), custom_call_target="tpu_custom_call" | custom-call | flops 234881024 | bytes 376832 | tf_op jit(solution)/shard_map/dnormed/pallas_call | solution.py:183
  606.9 16.6 %branch.3 = (bf16[2,2,1024,512]{3,2,1,0:T(8,128)(2,1)}, bf16[2,2,1024,512]{3,2,1,0:T(8,128)(2,1)}) custom-call(s32[2]{0:T(128)} %pad_add_fusion.own_ref, bf16[2048,256]{1,0:T(8,128)(2,1)} %get-tuple-element.163.refs_7_.a_ref, bf16[2048,1024]{1,0:T(8,128)(2,1)} %get-tuple-element.133.refs_3_.b_ref, bf16[4,1024,512]{2,1,0:T(8,128)(2,1)} %heads_own.1.w_ref.wa_ref, ...), custom_call_target="tpu_custom_call" | custom-call | flops 167772160 | bytes 344064 | tf_op jit(solution)/shard_map/branch/pallas_call | solution.py:183
  630.5 15.1 %collective-permute-done.30 = bf16[1,1,1024,512]{3,2,1,0:T(8,128)(2,1)S(1)} collective-permute-done((bf16[1,1,1024,512]{3,2,1,0:T(8,128)(2,1)S(1)}, bf16[1,1,1024,512]{3,2,1,0:T(8,128)(2,1)S(1)}, u32[]{:S(2)}, u32[]{:S(2)}) %collective-permute-start.30) | collective-permute-done | bytes 1048608 | tf_op jit(solution)/shard_map/ppermute | solution.py:854
  650.7 43.0 %collective-permute-done.36 = bf16[2,1024,512]{2,1,0:T(8,128)(2,1)S(1)} collective-permute-done((bf16[2,1024,512]{2,1,0:T(8,128)(2,1)S(1)}, bf16[2,1024,512]{2,1,0:T(8,128)(2,1)S(1)}, u32[]{:S(2)}, u32[]{:S(2)}) %collective-permute-start.36) | collective-permute-done | bytes 2097184 | tf_op jit(solution)/shard_map/ppermute | solution.py:854
  714.5 34.5 %collective-permute-done.40 = bf16[2,1,1024,512]{3,2,1,0:T(8,128)(2,1)} collective-permute-done((bf16[2,1,1024,512]{3,2,1,0:T(8,128)(2,1)S(1)}, bf16[2,1,1024,512]{3,2,1,0:T(8,128)(2,1)}, u32[]{:S(2)}, u32[]{:S(2)}) %collective-permute-start.40) | collective-permute-done | bytes 2097184 | tf_op jit(solution)/shard_map/ppermute | solution.py:854
  800.5 10.6 %collective-permute-done.49 = bf16[2,1024,512]{2,1,0:T(8,128)(2,1)} collective-permute-done((bf16[2,1024,512]{2,1,0:T(8,128)(2,1)}, bf16[2,1024,512]{2,1,0:T(8,128)(2,1)}, u32[]{:S(2)}, u32[]{:S(2)}) %collective-permute-start.49) | collective-permute-done | bytes 2097184 | tf_op jit(solution)/shard_map/ppermute | solution.py:854
  819.5 9.8 %collective-permute-done.51 = bf16[2,1024,512]{2,1,0:T(8,128)(2,1)} collective-permute-done((bf16[2,1024,512]{2,1,0:T(8,128)(2,1)}, bf16[2,1024,512]{2,1,0:T(8,128)(2,1)}, u32[]{:S(2)}, u32[]{:S(2)}) %collective-permute-start.51) | collective-permute-done | bytes 2097184 | tf_op jit(solution)/shard_map/ppermute | solution.py:854
  (360 shorter events, 338.9 us)
Async XLA Ops:
  7.2 131.0 %all-gather.5.cloned.1.call-start = ((), (), s32[]{:S(2)}) async-start(), calls=%async_computation | async-start | bytes 9437184 | tf_op jit(solution)/shard_map/all_gather | solution.py:683
  10.4 153.5 %all-gather.7.cloned.1.call-start = ((), (), s32[]{:S(2)}) async-start(), calls=%async_computation.1 | async-start | bytes 9437184 | tf_op jit(solution)/shard_map/all_gather | solution.py:684
  15.4 244.0 %all-gather.11.cloned.1.call-start = ((), (), s32[]{:S(2)}) async-start(), calls=%async_computation.3 | async-start | bytes 9437184 | tf_op jit(solution)/shard_map/all_gather | solution.py:683
  16.1 260.6 %all-gather.9.cloned.1.call-start = ((), (), s32[]{:S(2)}) async-start(), calls=%async_computation.2 | async-start | bytes 9437184 | tf_op jit(solution)/shard_map/all_gather | solution.py:684
  87.5 48.5 %collective-permute-start.16 = (bf16[512,512]{1,0:T(8,128)(2,1)}, bf16[512,512]{1,0:T(8,128)(2,1)S(1)}, u32[]{:S(2)}, u32[]{:S(2)}) collective-permute-start(bf16[512,512]{1,0:T(8,128)(2,1)} %get-tuple-element.118), channel_id=1, source_target_pairs={{0,6},{2,4},{4,2},{6,0},{1,7},{3,5},{5,3},{7,1},{8,14},{10,12},{12... | collective-permute-start | bytes 1572872 | tf_op jit(solution)/shard_map/ppermute | solution.py:498
  102.2 89.3 %collective-permute-start.13 = (bf16[1024,512]{1,0:T(8,128)(2,1)}, bf16[1024,512]{1,0:T(8,128)(2,1)S(1)}, u32[]{:S(2)}, u32[]{:S(2)}) collective-permute-start(bf16[1024,512]{1,0:T(8,128)(2,1)} %get-tuple-element.225), channel_id=1, source_target_pairs={{0,2},{2,0},{4,6},{6,4},{1,3},{3,1},{5,7},{7,5},{8,10},{10,8},{12,... | collective-permute-start | bytes 3145736 | tf_op jit(solution)/shard_map/ppermute | solution.py:498
  107.1 49.2 %collective-permute-start.12 = (bf16[512,512]{1,0:T(8,128)(2,1)}, bf16[512,512]{1,0:T(8,128)(2,1)}, u32[]{:S(2)}, u32[]{:S(2)}) collective-permute-start(bf16[512,512]{1,0:T(8,128)(2,1)} %collective-permute-done.11.refs_4_), channel_id=1, source_target_pairs={{0,8},{8,0},{16,24},{24,16},{1,9},{9,1},{17,25},{25,17},{2,10},{10... | collective-permute-start | bytes 1572872 | tf_op jit(solution)/shard_map/ppermute | solution.py:498
  117.3 74.2 %collective-permute-start.15 = (bf16[512,512]{1,0:T(8,128)(2,1)S(1)}, bf16[512,512]{1,0:T(8,128)(2,1)S(1)}, u32[]{:S(2)}, u32[]{:S(2)}) collective-permute-start(bf16[512,512]{1,0:T(8,128)(2,1)S(1)} %collective-permute-done.14.refs_2_), channel_id=1, source_target_pairs={{0,8},{8,0},{16,24},{24,16},{1,9},{9,1},{17,25},{25,17},{2,10},{10... | collective-permute-start | bytes 1572872 | tf_op jit(solution)/shard_map/ppermute | solution.py:498
  135.9 55.6 %collective-permute-start.17 = (bf16[512,512]{1,0:T(8,128)(2,1)S(1)}, bf16[512,512]{1,0:T(8,128)(2,1)S(1)}, u32[]{:S(2)}, u32[]{:S(2)}) collective-permute-start(bf16[512,512]{1,0:T(8,128)(2,1)S(1)} %collective-permute-done.16.refs_4_), channel_id=1, source_target_pairs={{0,8},{8,0},{16,24},{24,16},{1,9},{9,1},{17,25},{25,17},{2,10},{10... | collective-permute-start | bytes 1572872 | tf_op jit(solution)/shard_map/ppermute | solution.py:498
  334.0 55.1 %collective-permute-start.18 = (bf16[2,1024,512]{2,1,0:T(8,128)(2,1)}, bf16[2,1024,512]{2,1,0:T(8,128)(2,1)S(1)}, u32[]{:S(2)}, u32[]{:S(2)}) collective-permute-start(bf16[2,1024,512]{2,1,0:T(8,128)(2,1)} %get-tuple-element.136), channel_id=1, source_target_pairs={{0,8},{24,16},{1,9},{25,17},{2,10},{26,18},{3,11},{27,19},{4,12},{... | collective-permute-start | bytes 6291464 | tf_op jit(solution)/shard_map/ppermute | solution.py:854
  391.0 57.0 %collective-permute-start.21 = (bf16[2,2,1024,512]{3,2,1,0:T(8,128)(2,1)}, bf16[2,2,1024,512]{3,2,1,0:T(8,128)(2,1)}, u32[]{:S(2)}, u32[]{:S(2)}) collective-permute-start(bf16[2,2,1024,512]{3,2,1,0:T(8,128)(2,1)} %get-tuple-element.147), channel_id=1, source_target_pairs={{0,2},{2,0},{4,6},{6,4},{1,3},{3,1},{5,7},{7,5},{8,10},{10,8},{12,... | collective-permute-start | bytes 12582920 | tf_op jit(solution)/shard_map/ppermute | solution.py:854
  393.8 48.8 %collective-permute-start.20 = (bf16[2,1024,512]{2,1,0:T(8,128)(2,1)}, bf16[2,1024,512]{2,1,0:T(8,128)(2,1)}, u32[]{:S(2)}, u32[]{:S(2)}) collective-permute-start(bf16[2,1024,512]{2,1,0:T(8,128)(2,1)} %add_convert_fusion.15), channel_id=1, source_target_pairs={{8,16},{16,8},{9,17},{17,9},{10,18},{18,10},{11,19},{19,11},{12,20... | collective-permute-start | bytes 6291464 | tf_op jit(solution)/shard_map/ppermute | solution.py:854
  450.2 58.9 %collective-permute-start.22 = (bf16[2,2,1024,512]{3,2,1,0:T(8,128)(2,1)}, bf16[2,2,1024,512]{3,2,1,0:T(8,128)(2,1)}, u32[]{:S(2)}, u32[]{:S(2)}) collective-permute-start(bf16[2,2,1024,512]{3,2,1,0:T(8,128)(2,1)} %get-tuple-element.148), channel_id=1, source_target_pairs={{0,2},{2,0},{4,6},{6,4},{1,3},{3,1},{5,7},{7,5},{8,10},{10,8},{12,... | collective-permute-start | bytes 12582920 | tf_op jit(solution)/shard_map/ppermute | solution.py:854
  451.8 49.9 %collective-permute-start.23 = (bf16[2,1024,512]{2,1,0:T(8,128)(2,1)}, bf16[2,1024,512]{2,1,0:T(8,128)(2,1)S(1)}, u32[]{:S(2)}, u32[]{:S(2)}) collective-permute-start(bf16[2,1024,512]{2,1,0:T(8,128)(2,1)} %get-tuple-element.150), channel_id=1, source_target_pairs={{0,8},{24,16},{8,0},{16,24},{1,9},{25,17},{9,1},{17,25},{2,10},{26... | collective-permute-start | bytes 6291464 | tf_op jit(solution)/shard_map/ppermute | solution.py:854
  454.3 49.4 %collective-permute-start.24 = (bf16[2,1024,512]{2,1,0:T(8,128)(2,1)}, bf16[2,1024,512]{2,1,0:T(8,128)(2,1)}, u32[]{:S(2)}, u32[]{:S(2)}) collective-permute-start(bf16[2,1024,512]{2,1,0:T(8,128)(2,1)} %add_convert_fusion.14), channel_id=1, source_target_pairs={{8,16},{16,8},{9,17},{17,9},{10,18},{18,10},{11,19},{19,11},{12,20... | collective-permute-start | bytes 6291464 | tf_op jit(solution)/shard_map/ppermute | solution.py:854
  514.1 48.3 %collective-permute-start.27 = (bf16[2,1024,512]{2,1,0:T(8,128)(2,1)}, bf16[2,1024,512]{2,1,0:T(8,128)(2,1)S(1)}, u32[]{:S(2)}, u32[]{:S(2)}) collective-permute-start(bf16[2,1024,512]{2,1,0:T(8,128)(2,1)} %get-tuple-element.155), channel_id=1, source_target_pairs={{0,8},{24,16},{8,0},{16,24},{1,9},{25,17},{9,1},{17,25},{2,10},{26... | collective-permute-start | bytes 6291464 | tf_op jit(solution)/shard_map/ppermute | solution.py:854
  578.3 48.7 %collective-permute-start.32 = (bf16[2,1024,512]{2,1,0:T(8,128)(2,1)}, bf16[2,1024,512]{2,1,0:T(8,128)(2,1)}, u32[]{:S(2)}, u32[]{:S(2)}) collective-permute-start(bf16[2,1024,512]{2,1,0:T(8,128)(2,1)} %add_convert_fusion.8), channel_id=1, source_target_pairs={{8,16},{16,8},{9,17},{17,9},{10,18},{18,10},{11,19},{19,11},{12,20... | collective-permute-start | bytes 6291464 | tf_op jit(solution)/shard_map/ppermute | solution.py:854
  581.9 63.7 %collective-permute-start.33 = (bf16[2,1024,512]{2,1,0:T(8,128)(2,1)}, bf16[2,1024,512]{2,1,0:T(8,128)(2,1)}, u32[]{:S(2)}, u32[]{:S(2)}) collective-permute-start(bf16[2,1024,512]{2,1,0:T(8,128)(2,1)} %broadcast_select_fusion.6), channel_id=1, source_target_pairs={{0,4},{2,6},{4,0},{6,2},{1,5},{3,7},{5,1},{7,3},{8,12},{10,14},{12... | collective-permute-start | bytes 6291464 | tf_op jit(solution)/shard_map/ppermute | solution.py:854
  645.6 50.7 %collective-permute-start.35 = (bf16[2,2,1024,512]{3,2,1,0:T(8,128)(2,1)}, bf16[2,2,1024,512]{3,2,1,0:T(8,128)(2,1)S(1)}, u32[]{:S(2)}, u32[]{:S(2)}) collective-permute-start(bf16[2,2,1024,512]{3,2,1,0:T(8,128)(2,1)} %get-tuple-element.171), channel_id=1, source_target_pairs={{0,2},{2,0},{4,6},{6,4},{1,3},{3,1},{5,7},{7,5},{8,10},{10,8},{12,... | collective-permute-start | bytes 12582920 | tf_op jit(solution)/shard_map/ppermute | solution.py:854
  645.6 52.4 %collective-permute-start.38 = (bf16[2,2,1024,512]{3,2,1,0:T(8,128)(2,1)}, bf16[2,2,1024,512]{3,2,1,0:T(8,128)(2,1)S(1)}, u32[]{:S(2)}, u32[]{:S(2)}) collective-permute-start(bf16[2,2,1024,512]{3,2,1,0:T(8,128)(2,1)} %get-tuple-element.175), channel_id=1, source_target_pairs={{0,2},{2,0},{4,6},{6,4},{1,3},{3,1},{5,7},{7,5},{8,10},{10,8},{12,... | collective-permute-start | bytes 12582920 | tf_op jit(solution)/shard_map/ppermute | solution.py:854
  649.2 52.8 %collective-permute-start.39 = (bf16[2,1024,512]{2,1,0:T(8,128)(2,1)S(1)}, bf16[2,1024,512]{2,1,0:T(8,128)(2,1)}, u32[]{:S(2)}, u32[]{:S(2)}) collective-permute-start(bf16[2,1024,512]{2,1,0:T(8,128)(2,1)S(1)} %broadcast_select_fusion.4), channel_id=1, source_target_pairs={{0,4},{2,6},{4,0},{6,2},{1,5},{3,7},{5,1},{7,3},{8,12},{10,14},{12... | collective-permute-start | bytes 6291464 | tf_op jit(solution)/shard_map/ppermute | solution.py:854
  709.2 60.5 %collective-permute-start.50 = (bf16[2,1024,512]{2,1,0:T(8,128)(2,1)}, bf16[2,1024,512]{2,1,0:T(8,128)(2,1)}, u32[]{:S(2)}, u32[]{:S(2)}) collective-permute-start(bf16[2,1024,512]{2,1,0:T(8,128)(2,1)} %add_convert_fusion.2), channel_id=1, source_target_pairs={{8,0},{16,24},{9,1},{17,25},{10,2},{18,26},{11,3},{19,27},{12,4},{... | collective-permute-start | bytes 6291464 | tf_op jit(solution)/shard_map/ppermute | solution.py:854
  759.0 52.2 %collective-permute-start.49 = (bf16[2,1024,512]{2,1,0:T(8,128)(2,1)}, bf16[2,1024,512]{2,1,0:T(8,128)(2,1)}, u32[]{:S(2)}, u32[]{:S(2)}) collective-permute-start(bf16[2,1024,512]{2,1,0:T(8,128)(2,1)} %add_convert_fusion), channel_id=1, source_target_pairs={{8,0},{16,24},{9,1},{17,25},{10,2},{18,26},{11,3},{19,27},{12,4},{... | collective-permute-start | bytes 6291464 | tf_op jit(solution)/shard_map/ppermute | solution.py:854
  772.9 56.4 %collective-permute-start.51 = (bf16[2,1024,512]{2,1,0:T(8,128)(2,1)}, bf16[2,1024,512]{2,1,0:T(8,128)(2,1)}, u32[]{:S(2)}, u32[]{:S(2)}) collective-permute-start(bf16[2,1024,512]{2,1,0:T(8,128)(2,1)} %broadcast_select_fusion), channel_id=1, source_target_pairs={{0,4},{2,6},{4,0},{6,2},{1,5},{3,7},{5,1},{7,3},{8,12},{10,14},{12... | collective-permute-start | bytes 6291464 | tf_op jit(solution)/shard_map/ppermute | solution.py:854
  (96 other events, 1777.2 us)
Sparse Core Ops, SparseCore 0:
  10.5 86.4 all-gather.4
  98.9 64.9 all-gather.6
  166.4 54.2 all-gather.10
  222.4 54.2 all-gather.8

commit v3 on v2

--- a/solution.py
+++ b/solution.py
@@ -160,6 +160,37 @@
         cost_estimate=cost(4 * normed.size * width, normed, grad, up, down, out, out),
         name="hidden",
     )(normed, grad, up, down, bias.reshape(1, width))
+
+
+def combine_all_kernel(a_ref, b_ref, wa_ref, wb_ref, out_ref, dims_b):
+    for r in range(out_ref.shape[0]):
+        acc = mm(a_ref[...], wa_ref[r], NN) + mm(b_ref[...], wb_ref[r], dims_b)
+        out_ref[r] = acc.astype(bf16)
+
+
+def combine_all_call(a, b, wa, index, wb, dims_b, cols, feats, name):
+    toks = a.shape[0] // cols
+    rows = wa.shape[0]
+    tb = min(512, toks)
+    per = toks // tb
+    out = sds((cols * rows, toks, feats), bf16)
+    flops = 2 * a.shape[0] * (a.shape[1] + b.shape[1]) * rows * feats
+    in_map = lambda c, t: (c * per + t, 0)
+    return pl.pallas_call(
+        partial(combine_all_kernel, dims_b=dims_b),
+        grid=(cols, per),
+        in_specs=[
+            pl.BlockSpec((tb, a.shape[1]), in_map),
+            pl.BlockSpec((tb, b.shape[1]), in_map),
+            rows_of(wa, a.shape[1], index),
+            whole(wb.shape),
+        ],
+        out_specs=pl.BlockSpec((rows, tb, feats), lambda c, t: (c, t, 0)),
+        out_shape=out,
+        compiler_params=params(),
+        cost_estimate=cost(flops, a, b, wa, wb, out),
+        name=name,
+    )(a, b, wa, wb)
 
 
 def combine_kernel(own_ref, a_ref, b_ref, wa_ref, wb_ref, keep_ref, send_ref, dims_b):
@@ -319,20 +350,20 @@
 
         @pl.when(step == k)
         def _():
-            piece = piece_ref[...].astype(f32)
+            piece = piece_ref[0].astype(f32)
             out_ref[...] = piece.T if turned else piece
 
 
 def place_call(own, pieces, size, index, turned, name):
     rows = len(pieces)
-    height, width = pieces[0].shape
-    height = size
-    parts = max(1, height // 512)
+    height, width = size, pieces[0][0].shape[2]
+    parts = max(1, height // 1024)
     cut = height // parts
 
     def in_map(k):
         def at(i, b, own):
-            return (index * parts + jnp.where(i == k, b, jnp.where(i < k, 0, parts - 1)), 0)
+            row = index * parts + jnp.where(i == k, b, jnp.where(i < k, 0, parts - 1))
+            return (pieces[k][1], row, 0)
 
         return at
 
@@ -349,14 +380,14 @@
         grid_spec=pltpu.PrefetchScalarGridSpec(
             num_scalar_prefetch=1,
             grid=(rows, parts),
-            in_specs=[pl.BlockSpec((cut, width), in_map(k)) for k in range(rows)],
+            in_specs=[pl.BlockSpec((1, cut, width), in_map(k)) for k in range(rows)],
             out_specs=pl.BlockSpec(block, out_map),
         ),
         out_shape=out,
         compiler_params=params(),
         cost_estimate=cost(out.size, out, out),
         name=name,
-    )(own, *pieces)
+    )(own, *[array for array, _ in pieces])
 
 
 def rotary_tables(head_dim, lanes):
@@ -569,49 +600,63 @@
 
 class SmallSum:
     def __init__(self, value, axes, gather=False):
-        self.value, self.gathered = value, []
+        self.value = value
         bits = lambda axis: [1 << b for b in range(lax.axis_size(axis).bit_length() - 1)]
-        self.steps = [(axis, mask, False) for axis in axes for mask in bits(axis)]
-        self.steps += [("row", mask, True) for mask in bits("row")] if gather else []
+        self.steps = [(axis, mask) for axis in axes for mask in bits(axis)]
+        self.gather = gather
 
     def start(self):
-        return [(self.value,) + flips(*self.steps[0][:2])]
+        if not self.steps:
+            return [(self.value,) + flips("row", k) for k in range(1, lax.axis_size("row"))]
+        return [(self.value,) + flips(*self.steps[0])]
 
     def done(self, received):
-        if self.steps[0][2]:
-            self.value = jnp.stack([self.value, received[0]])
+        if self.steps:
+            self.value = self.value + received[0]
+            self.steps = self.steps[1:]
         else:
-            self.value = self.value + received[0]
+            self.value = jnp.stack([self.value] + list(received))
+            self.gather = False
+        return [self.value]
+
+    def finished(self):
+        return not self.steps and not self.gather
+
+
+class Deliver:
+    def __init__(self, line, near, far):
+        self.line, self.near, self.far = line, near, far
+        self.steps = [2, 1]
+        self.value = None
+
+    def start(self):
+        if self.steps[0] == 2:
+            return [(self.line.summed[self.far],) + flips("row", 2)]
+        other = jnp.stack([self.line.summed[self.near][1], self.value[1]])
+        return [(other,) + flips("row", 1)]
+
+    def done(self, received):
+        if self.steps[0] == 2:
+            self.value = received[0]
+        else:
+            near = self.line.summed[self.near]
+            self.pieces = [(near, 0), (received[0], 0), (self.value, 0), (received[0], 1)]
         self.steps = self.steps[1:]
-        return [self.value]
+        return received
 
     def finished(self):
         return not self.steps
 
 
-class Deliver:
-    def __init__(self, line, index, first):
-        self.line, self.index, self.first = line, index, first
-        self.steps = ([first] if first else []) + [1]
-        self.value = None
-
-    def start(self):
-        if self.value is None:
-            self.value = self.line.summed[self.index]
-        if self.steps[0] == 1:
-            return [(self.value[1],) + flips("row", 1)]
-        return [(self.value,) + flips("row", self.steps[0])]
-
-    def done(self, received):
-        if self.steps[0] == 1:
-            self.pieces = [self.value[0], received[0]]
-        else:
-            self.value = received[0]
-        self.steps = self.steps[1:]
-        return received
+class WholeSum:
+    def __init__(self, blocks):
+        self.value = lax.psum_scatter(blocks, ("col", "row"), scatter_dimension=0)
 
     def finished(self):
-        return not self.steps
+        return True
+
+    def total(self):
+        return self.value.astype(f32)
 
 
 class ScatterSum:
@@ -714,7 +759,7 @@
     weights = {}
     qkvs, datts, attns, dqkvs = {}, {}, {}, {}
     sums_up, sums_qkv = [], []
-    line, order = LineSum(), []
+    line = LineSum()
     flows, grads = {"z": line}, {}
 
     def norm_m(m, dep):
@@ -756,14 +801,26 @@
 
     def dnormed_m(m, dep):
         dqkv = after(dqkvs[m], dep)
+        if not m:
+            blocks = combine_all_call(
+                dqkv, dpres[m], weights["heads"], 0, weights["up"], NT, cols, feats, "dnormed"
+            )
+            flows["n0"] = WholeSum(blocks)
+            return blocks
         keep, send = combine_call(
             own, dqkv, dpres[m], weights["heads"], 0, weights["up"], NT, cols, feats, "dnormed"
         )
-        flows[f"n{m}"] = ScatterSum(keep, send, m == 0)
+        flows[f"n{m}"] = ScatterSum(keep, send, False)
         return send
 
     def branch_m(m, dep):
         attn = after(attns[m], dep)
+        if not m:
+            blocks = combine_all_call(
+                attn, acts[m], weights["heads"], 3, weights["down"], NN, cols, feats, "branch"
+            )
+            flows["b0"] = WholeSum(blocks)
+            return blocks
         keep, send = combine_call(
             own, attn, acts[m], weights["heads"], 3, weights["down"], NN, cols, feats, "branch"
         )
@@ -779,10 +836,8 @@
             dqkv = [after(dqkvs[0], dep)] + [dqkvs[m] for m in range(1, micros)]
             terms = [(normeds, dqkv), (g_alls, [attns[m] for m in range(micros)])]
         grads[group_name] = wgrad_call(own, terms, 2, "grad_" + group_name)
-        for i in (1, 0):
-            line.coming.append(grads[group_name][i])
-            flows[f"{group_name}{i}"] = Deliver(line, len(order), i * (rows // 2))
-            order.append(i)
+        line.coming += grads[group_name][::-1]
+        flows[group_name] = Deliver(line, 2 * len(grads) - 1, 2 * len(grads) - 2)
         return grads[group_name][0]
 
     kernels = {
@@ -791,8 +846,9 @@
     }
     placed = {}
 
-    def place(name):
-        parts = flows[name + "0"].pieces + flows[name + "1"].pieces
+    def place(name, deps=()):
+        parts = flows[name].pieces
+        parts = [(after(parts[0][0], *deps), parts[0][1])] + parts[1:]
         if name == "d":
             placed["down"] = place_call(own, parts, ff_local, 0, False, "place_down")
         elif name == "u":
@@ -827,7 +883,7 @@
         return dep
 
     def place_m(name, dep):
-        place(name)
+        place(name, [dep])
         return placed["down" if name == "d" else "up" if name == "u" else "out"]
 
     kernels.update(biases=biases_m, place=place_m)
@@ -837,13 +893,13 @@
         ((), ("norm1", "hidden1")),
         ((), ("gradd",)),
         (("z",), ("gradu", "dnormed0")),
-        (("z", "n0"), ("qkv1", "branch0")),
-        (("z", "n0", "b0"), ("attention1",)),
-        (("z", "n0", "b0"), ("gradh", "biases0")),
-        (("z", "b0", "d1", "s"), ("dnormed1", "branch1")),
-        (("z", "n1", "b1", "u1"), ()),
-        (("z", "n1", "b1", "d1", "d0", "u1", "u0"), ()),
-        (("z", "n1", "b1", "h1", "s"), ("placed", "placeu")),
+        (("z",), ("qkv1", "branch0")),
+        (("z",), ("attention1",)),
+        (("z", "d"), ("gradh", "biases0")),
+        (("z", "d"), ("dnormed1", "branch1")),
+        (("z", "n1", "b1", "u"), ("placed",)),
+        (("z", "n1", "b1", "u"), ()),
+        (("z", "n1", "b1", "h"), ("placeu",)),
     ]
     deps = [norm_full]
     for names, work in program:
@@ -891,7 +947,7 @@
     out_grad = out_grad.reshape(rows, pairs, lanes, feats)[:, :, : group * head_dim]
     out_grad = out_grad.reshape(out_weight.shape)
 
-    near = flows["s"].value.reshape(rows, -1)
+    near = flows["s"].value
     bias_sums = jnp.take(near, row_index ^ jnp.arange(rows), axis=0)
     up_bias_grad = bias_sums[:, :ff_local].reshape(-1)
     qkv_bias_grad = bias_sums[:, ff_local:].reshape(rows, pairs, 3, lanes)

time: 885 us -> 860 us (0.972)
  local copies, waits for them, and re-layouts: 52 us -> 42.2 us
    pallas_call x4 -> x2, Pallas kernels: 77.5 us -> 39.6 us  [combine_call(): pl.pallas_call(partial(combine_kernel, dims_b=dims_b), grid_spec=pltpu.Pr...]
    pallas_call x0 -> x2, Pallas kernels: none -> 37 us  [combine_all_call(): pl.pallas_call(partial(combine_all_kernel, dims_b=dims_b), grid=(cols, pe...]
    squeeze x6 -> x0, local copies, waits for them, and re-layouts: 11.4 us -> none  [done(): self.pieces = [self.value[0], received[0]]]
    ppermute x44 -> x36, starting transfers between devices: 56.3 us -> 44.9 us  [on_device(): lax.ppermute(after(v, *deps), *to)]
    convert_element_type x16 -> x12, other arithmetic: 34.4 us -> 28.6 us  [add_low(): return sum((v.astype(f32) for v in values)).astype(bf16)]
    ppermute x44 -> x36, waiting for transfers between devices: 145 us -> 147 us  [on_device(): lax.ppermute(after(v, *deps), *to)]
  transfers between devices with their start and end apart: 66 -> 60, of which waited for: 21 -> 19; matrix products, arithmetic and copies ran while one was open for 14% -> 14% of each run, Pallas kernels for 41% -> 41%
where the time goes in v3:
time: 860 us; the launch traced here: 853 us
  Pallas kernels  410 us (48%)
  waiting for transfers between devices  230 us (27%)
  other arithmetic  87.6 us (10%)
  starting transfers between devices  68.3 us (8%)
  local copies, waits for them, and re-layouts  42.2 us (5%)
  between operations  15.5 us (2%)
    ppermute x36, waiting for transfers between devices, on_device(): lax.ppermute(after(v, *deps), *to)  147 us
    pallas_call x3, Pallas kernels, wgrad_call(): pl.pallas_call(partial(wgrad_kernel, terms=len(pairs), count=count), grid...  92.8 us
    pallas_call x2, Pallas kernels, attention_call(): pl.pallas_call(kernel, grid_spec=pltpu.PrefetchScalarGridSpec(num_scalar_...  79.8 us
    ppermute x18, waiting for transfers between devices, swap(): lax.ppermute(value, axis, [(i, i ^ mask) for i in range(lax.axis_size(axi...  74.5 us
    pallas_call x2, Pallas kernels, hidden_call(): pl.pallas_call(partial(hidden_kernel, chunk=min(256, width)), grid=(cols,...  55.7 us
    ppermute x36, starting transfers between devices, on_device(): lax.ppermute(after(v, *deps), *to)  44.9 us
    pallas_call x2, Pallas kernels, combine_call(): pl.pallas_call(partial(combine_kernel, dims_b=dims_b), grid_spec=pltpu.Pr...  39.6 us
    pallas_call x4, Pallas kernels, project_call(): pl.pallas_call(project_kernel, grid=(cols, per), in_specs=[pl.BlockSpec((...  38.3 us
  transfers between devices with their start and end apart: 60, of which 19 were waited for; matrix products, arithmetic and copies ran while one was open for 14% of the time, Pallas kernels for 41%

profile of v3, /device:TPU:0, one launch (start us, length us, event | category | flops | bytes accessed | tf_op | source)
XLA Modules:
  0.0 853.4 jit_solution(5900274904188485420)
XLA Ops:
  28.7 15.5 %collective-permute-done.6.refs_4_ = bf16[256,1024]{1,0:T(8,128)(2,1)} collective-permute-done((bf16[256,1024]{1,0:T(8,128)(2,1)}, bf16[256,1024]{1,0:T(8,128)(2,1)}, u32[]{:S(2)}, u32[]{:S(2)}) %collective-permute-start.6) | collective-permute-done | bytes 524320 | tf_op jit(solution)/shard_map/ppermute | solution.py:529
  63.3 18.5 %collective-permute-done.11.refs_4_ = bf16[512,512]{1,0:T(8,128)(2,1)} collective-permute-done((bf16[512,512]{1,0:T(8,128)(2,1)}, bf16[512,512]{1,0:T(8,128)(2,1)}, u32[]{:S(2)}, u32[]{:S(2)}) %collective-permute-start.11) | collective-permute-done | bytes 524320 | tf_op jit(solution)/shard_map/ppermute | solution.py:529
  90.4 11.3 %collective-permute-done.9.refs_2_ = bf16[512,512]{1,0:T(8,128)(2,1)} collective-permute-done((bf16[512,512]{1,0:T(8,128)(2,1)}, bf16[512,512]{1,0:T(8,128)(2,1)}, u32[]{:S(2)}, u32[]{:S(2)}) %collective-permute-start.9) | collective-permute-done | bytes 524320 | tf_op jit(solution)/shard_map/ppermute | solution.py:529
  119.6 15.6 %collective-permute-done.16.refs_4_ = bf16[512,512]{1,0:T(8,128)(2,1)S(1)} collective-permute-done((bf16[512,512]{1,0:T(8,128)(2,1)}, bf16[512,512]{1,0:T(8,128)(2,1)S(1)}, u32[]{:S(2)}, u32[]{:S(2)}) %collective-permute-start.16) | collective-permute-done | bytes 524320 | tf_op jit(solution)/shard_map/ppermute | solution.py:529
  138.2 10.9 %norm.2 = (bf16[2,4,1024,512]{3,2,1,0:T(8,128)(2,1)}, f32[2,1024,1]{2,1,0:T(8,128)}, f32[2,1024,1]{2,1,0:T(8,128)}) custom-call(bf16[2,4,1024,512]{3,2,1,0:T(8,128)(2,1)} %bitcast.146, f32[4,1,512]{2,1,0:T(1,128)} %get-tuple-element.220.gain_ref, f32[4,1,512]{2,1,0:T(1,128)} %get-tuple-element.219.bias_ref), custom_call_target="tpu_custom_call" | custom-call | flops 524288 | bytes 262144 | tf_op jit(solution)/shard_map/norm/pallas_call | solution.py:63
  164.2 27.6 %hidden.2 = (bf16[2048,1024]{1,0:T(8,128)(2,1)}, bf16[2048,1024]{1,0:T(8,128)(2,1)}, f32[8,1024]{1,0:T(8,128)}) custom-call(bf16[2,4,1024,512]{3,2,1,0:T(8,128)(2,1)} %get-tuple-element.101.n_ref.x_ref.refs_0_, bf16[2,4,1024,512]{3,2,1,0:T(8,128)(2,1)} %bitcast.135, bf16[4,512,1024]{2,1,0:T(8,128)(2,1)} %up_own.1.up_ref.wb_ref, ...), custom_call_target="tpu_custom_call" | custom-call | flops 268435456 | bytes 524288 | tf_op jit(solution)/shard_map/hidden/pallas_call | solution.py:153
  201.6 11.6 %qkv.2.qkv_ref = f32[2048,768]{1,0:T(8,128)} custom-call(bf16[2,4,1024,512]{3,2,1,0:T(8,128)(2,1)} %get-tuple-element.101.n_ref.x_ref.refs_0_, bf16[4,1024,512]{2,1,0:T(8,128)(2,1)} %heads_own.1.w_ref.wa_ref), custom_call_target="tpu_custom_call" | custom-call | flops 100663296 | bytes 294912 | tf_op jit(solution)/shard_map/qkv/pallas_call | solution.py:100
  219.9 39.9 %attention.2 = (bf16[2048,256]{1,0:T(8,128)(2,1)}, bf16[2048,768]{1,0:T(8,128)(2,1)}, f32[16,768]{1,0:T(8,128)}) custom-call(s32[2]{0:T(128)} %get-tuple-element.234.lens_ref, f32[2048,768]{1,0:T(8,128)} %qkv.2.qkv_ref, f32[1,768]{1,0:T(1,128)} %reshape.481.bias_ref, bf16[2048,256]{1,0:T(8,128)(2,1)} %datt.2.datt_ref, f32[1024,128]{1,0:T(8,128)} %copy.38.keep_ref, ...), custom_call_target="tpu_custom_call" | custom-call | flops 201326592 | bytes 229376 | tf_op jit(solution)/shard_map/attention/pallas_call | solution.py:490
  259.8 10.7 %norm.3 = (bf16[2,4,1024,512]{3,2,1,0:T(8,128)(2,1)}, f32[2,1024,1]{2,1,0:T(8,128)}, f32[2,1024,1]{2,1,0:T(8,128)}) custom-call(bf16[2,4,1024,512]{3,2,1,0:T(8,128)(2,1)} %bitcast.147, f32[4,1,512]{2,1,0:T(1,128)} %get-tuple-element.220.gain_ref, f32[4,1,512]{2,1,0:T(1,128)} %get-tuple-element.219.bias_ref), custom_call_target="tpu_custom_call" | custom-call | flops 524288 | bytes 262144 | tf_op jit(solution)/shard_map/norm/pallas_call | solution.py:63
  277.0 28.0 %hidden.3 = (bf16[2048,1024]{1,0:T(8,128)(2,1)}, bf16[2048,1024]{1,0:T(8,128)(2,1)}, f32[8,1024]{1,0:T(8,128)}) custom-call(bf16[2,4,1024,512]{3,2,1,0:T(8,128)(2,1)} %get-tuple-element.116.x_ref.n_ref.refs_1_, bf16[2,4,1024,512]{3,2,1,0:T(8,128)(2,1)} %bitcast.139, bf16[4,512,1024]{2,1,0:T(8,128)(2,1)} %up_own.1.up_ref.wb_ref, ...), custom_call_target="tpu_custom_call" | custom-call | flops 268435456 | bytes 524288 | tf_op jit(solution)/shard_map/hidden/pallas_call | solution.py:153
  305.1 29.3 %grad_d.1 = (bf16[2,1024,512]{2,1,0:T(8,128)(2,1)}, bf16[2,1024,512]{2,1,0:T(8,128)(2,1)}) custom-call(s32[2]{0:T(128)} %pad_add_fusion.1.own_ref, bf16[2,4,1024,512]{3,2,1,0:T(8,128)(2,1)} %bitcast.137, bf16[2,4,1024,512]{3,2,1,0:T(8,128)(2,1)} %bitcast.140, bf16[2048,1024]{1,0:T(8,128)(2,1)} %get-tuple-element.127.b_ref.refs_2_, ...), custom_call_target="tpu_custom_call" | custom-call | flops 268435456 | bytes 458752 | tf_op jit(solution)/shard_map/grad_d/pallas_call | solution.py:278
  339.1 29.5 %grad_u.1 = (bf16[2,1024,512]{2,1,0:T(8,128)(2,1)}, bf16[2,1024,512]{2,1,0:T(8,128)(2,1)}) custom-call(s32[2]{0:T(128)} %pad_add_fusion.1.own_ref, bf16[2,4,1024,512]{3,2,1,0:T(8,128)(2,1)} %get-tuple-element.101.n_ref.x_ref.refs_0_, bf16[2,4,1024,512]{3,2,1,0:T(8,128)(2,1)} %get-tuple-element.116.x_ref.n_ref.refs_1_, ...), custom_call_target="tpu_custom_call" | custom-call | flops 268435456 | bytes 458752 | tf_op jit(solution)/shard_map/grad_u/pallas_call | solution.py:278
  368.6 21.1 %dnormed.3 = bf16[8,1024,512]{2,1,0:T(8,128)(2,1)} custom-call(bf16[2048,768]{1,0:T(8,128)(2,1)} %get-tuple-element.134.refs_2_.a_ref, bf16[2048,1024]{1,0:T(8,128)(2,1)} %get-tuple-element.129.refs_2_.b_ref, bf16[4,1024,512]{2,1,0:T(8,128)(2,1)} %heads_own.1.w_ref.wa_ref, bf16[4,512,1024]{2,1,0:T(8,128)(2,1)} %up_own.1.up_ref.wb_ref), custom_call_target="tpu_custom_call" | custom-call | flops 234881024 | bytes 376832 | tf_op jit(solution)/shard_map/dnormed/pallas_call | solution.py:179
  397.3 12.7 %qkv.3.qkv_ref = f32[2048,768]{1,0:T(8,128)} custom-call(bf16[2,4,1024,512]{3,2,1,0:T(8,128)(2,1)} %get-tuple-element.116.x_ref.n_ref.refs_1_, bf16[4,1024,512]{2,1,0:T(8,128)(2,1)} %heads_own.1.w_ref.wa_ref), custom_call_target="tpu_custom_call" | custom-call | flops 100663296 | bytes 294912 | tf_op jit(solution)/shard_map/qkv/pallas_call | solution.py:100
  417.3 15.9 %branch.2 = bf16[8,1024,512]{2,1,0:T(8,128)(2,1)} custom-call(bf16[2048,256]{1,0:T(8,128)(2,1)} %get-tuple-element.111.a_ref.refs_6_, bf16[2048,1024]{1,0:T(8,128)(2,1)} %get-tuple-element.127.b_ref.refs_2_, bf16[4,1024,512]{2,1,0:T(8,128)(2,1)} %heads_own.1.w_ref.wa_ref, bf16[4,1024,512]{2,1,0:T(8,128)(2,1)} %down_own.1.down_ref.wb_ref), custom_call_target="tpu_custom_call" | custom-call | flops 167772160 | bytes 344064 | tf_op jit(solution)/shard_map/branch/pallas_call | solution.py:179
  452.9 39.9 %attention.3 = (bf16[2048,256]{1,0:T(8,128)(2,1)}, bf16[2048,768]{1,0:T(8,128)(2,1)}, f32[16,768]{1,0:T(8,128)}) custom-call(s32[2]{0:T(128)} %get-tuple-element.235.lens_ref, f32[2048,768]{1,0:T(8,128)} %qkv.3.qkv_ref, f32[1,768]{1,0:T(1,128)} %reshape.481.bias_ref, bf16[2048,256]{1,0:T(8,128)(2,1)} %datt.3.datt_ref, f32[1024,128]{1,0:T(8,128)} %copy.38.keep_ref, ...), custom_call_target="tpu_custom_call" | custom-call | flops 201326592 | bytes 229376 | tf_op jit(solution)/shard_map/attention/pallas_call | solution.py:490
  510.3 34.0 %grad_h.1 = (bf16[2,1024,512]{2,1,0:T(8,128)(2,1)}, bf16[2,1024,512]{2,1,0:T(8,128)(2,1)}) custom-call(s32[2]{0:T(128)} %pad_add_fusion.1.own_ref, bf16[2,4,1024,512]{3,2,1,0:T(8,128)(2,1)} %get-tuple-element.101.n_ref.x_ref.refs_0_, bf16[2,4,1024,512]{3,2,1,0:T(8,128)(2,1)} %get-tuple-element.116.x_ref.n_ref.refs_1_, ...), custom_call_target="tpu_custom_call" | custom-call | flops 268435456 | bytes 720896 | tf_op jit(solution)/shard_map/grad_h/pallas_call | solution.py:278
  564.8 22.1 %dnormed.2 = (bf16[2,2,1024,512]{3,2,1,0:T(8,128)(2,1)}, bf16[2,2,1024,512]{3,2,1,0:T(8,128)(2,1)}) custom-call(s32[2]{0:T(128)} %pad_add_fusion.1.own_ref, bf16[2048,768]{1,0:T(8,128)(2,1)} %get-tuple-element.114.a_ref.refs_3_, bf16[2048,1024]{1,0:T(8,128)(2,1)} %get-tuple-element.117.b_ref.refs_3_, bf16[4,1024,512]{2,1,0:T(8,128)(2,1)} %heads_own.1.w_ref.wa_ref, ...), custom_call_target="tpu_custom_call" | custom-call | flops 234881024 | bytes 376832 | tf_op jit(solution)/shard_map/dnormed/pallas_call | solution.py:214
  586.9 17.5 %branch.3 = (bf16[2,2,1024,512]{3,2,1,0:T(8,128)(2,1)}, bf16[2,2,1024,512]{3,2,1,0:T(8,128)(2,1)}) custom-call(s32[2]{0:T(128)} %pad_add_fusion.1.own_ref, bf16[2048,256]{1,0:T(8,128)(2,1)} %get-tuple-element.119.a_ref.refs_7_, bf16[2048,1024]{1,0:T(8,128)(2,1)} %get-tuple-element.120.b_ref.refs_3_, bf16[4,1024,512]{2,1,0:T(8,128)(2,1)} %heads_own.1.w_ref.wa_ref, ...), custom_call_target="tpu_custom_call" | custom-call | flops 167772160 | bytes 344064 | tf_op jit(solution)/shard_map/branch/pallas_call | solution.py:214
  629.9 33.0 %collective-permute-done.30 = bf16[2,1024,512]{2,1,0:T(8,128)(2,1)S(1)} collective-permute-done((bf16[2,1024,512]{2,1,0:T(8,128)(2,1)}, bf16[2,1024,512]{2,1,0:T(8,128)(2,1)S(1)}, u32[]{:S(2)}, u32[]{:S(2)}) %collective-permute-start.30) | collective-permute-done | bytes 2097184 | tf_op jit(solution)/shard_map/ppermute | solution.py:910
  685.6 40.1 %collective-permute-done.34 = bf16[2,1,1024,512]{3,2,1,0:T(8,128)(2,1)S(1)} collective-permute-done((bf16[2,1,1024,512]{3,2,1,0:T(8,128)(2,1)S(1)}, bf16[2,1,1024,512]{3,2,1,0:T(8,128)(2,1)S(1)}, u32[]{:S(2)}, u32[]{:S(2)}) %collective-permute-start.34) | collective-permute-done | bytes 2097184 | tf_op jit(solution)/shard_map/ppermute | solution.py:910
  748.6 11.0 %collective-permute-done.39 = bf16[1,1,1024,512]{3,2,1,0:T(8,128)(2,1)} collective-permute-done((bf16[1,1,1024,512]{3,2,1,0:T(8,128)(2,1)S(1)}, bf16[1,1,1024,512]{3,2,1,0:T(8,128)(2,1)}, u32[]{:S(2)}, u32[]{:S(2)}) %collective-permute-start.39) | collective-permute-done | bytes 1048608 | tf_op jit(solution)/shard_map/ppermute | solution.py:910
  767.1 16.1 %collective-permute-done.40 = bf16[2,1024,512]{2,1,0:T(8,128)(2,1)} collective-permute-done((bf16[2,1024,512]{2,1,0:T(8,128)(2,1)}, bf16[2,1024,512]{2,1,0:T(8,128)(2,1)}, u32[]{:S(2)}, u32[]{:S(2)}) %collective-permute-start.40) | collective-permute-done | bytes 2097184 | tf_op jit(solution)/shard_map/ppermute | solution.py:910
  785.1 17.0 %collective-permute-done.42.refs_2_ = bf16[2,1024,512]{2,1,0:T(8,128)(2,1)} collective-permute-done((bf16[2,1024,512]{2,1,0:T(8,128)(2,1)}, bf16[2,1024,512]{2,1,0:T(8,128)(2,1)}, u32[]{:S(2)}, u32[]{:S(2)}) %collective-permute-start.42) | collective-permute-done | bytes 2097184 | tf_op jit(solution)/shard_map/ppermute | solution.py:910
  (343 shorter events, 309.1 us)
Async XLA Ops:
  7.2 130.9 %all-gather.5.cloned.1.call-start = ((), (), s32[]{:S(2)}) async-start(), calls=%async_computation.2 | async-start | bytes 9437184 | tf_op jit(solution)/shard_map/all_gather | solution.py:728
  10.4 153.8 %all-gather.7.cloned.1.call-start = ((), (), s32[]{:S(2)}) async-start(), calls=%async_computation.3 | async-start | bytes 9437184 | tf_op jit(solution)/shard_map/all_gather | solution.py:729
  14.7 245.1 %all-gather.11.cloned.1.call-start = ((), (), s32[]{:S(2)}) async-start(), calls=%async_computation.5 | async-start | bytes 9437184 | tf_op jit(solution)/shard_map/all_gather | solution.py:728
  15.4 261.6 %all-gather.9.cloned.1.call-start = ((), (), s32[]{:S(2)}) async-start(), calls=%async_computation.4 | async-start | bytes 9437184 | tf_op jit(solution)/shard_map/all_gather | solution.py:729
  16.0 747.3 %reduce-scatter.5.cloned.1.call-start = ((), (), s32[]{:S(2)}) async-start(), calls=%async_computation.7 | async-start | bytes 9437184 | tf_op jit(solution)/shard_map/reduce_scatter | solution.py:653
  101.8 90.1 %collective-permute-start.13 = (bf16[1024,512]{1,0:T(8,128)(2,1)}, bf16[1024,512]{1,0:T(8,128)(2,1)S(1)}, u32[]{:S(2)}, u32[]{:S(2)}) collective-permute-start(bf16[1024,512]{1,0:T(8,128)(2,1)} %get-tuple-element.195), channel_id=1, source_target_pairs={{0,2},{2,0},{4,6},{6,4},{1,3},{3,1},{5,7},{7,5},{8,10},{10,8},{12,... | collective-permute-start | bytes 3145736 | tf_op jit(solution)/shard_map/ppermute | solution.py:529
  106.3 49.9 %collective-permute-start.12 = (bf16[512,512]{1,0:T(8,128)(2,1)}, bf16[512,512]{1,0:T(8,128)(2,1)}, u32[]{:S(2)}, u32[]{:S(2)}) collective-permute-start(bf16[512,512]{1,0:T(8,128)(2,1)} %collective-permute-done.11.refs_4_), channel_id=1, source_target_pairs={{0,8},{8,0},{16,24},{24,16},{1,9},{9,1},{17,25},{25,17},{2,10},{10... | collective-permute-start | bytes 1572872 | tf_op jit(solution)/shard_map/ppermute | solution.py:529
  116.5 75.4 %collective-permute-start.15 = (bf16[512,512]{1,0:T(8,128)(2,1)S(1)}, bf16[512,512]{1,0:T(8,128)(2,1)S(1)}, u32[]{:S(2)}, u32[]{:S(2)}) collective-permute-start(bf16[512,512]{1,0:T(8,128)(2,1)S(1)} %collective-permute-done.14.refs_2_), channel_id=1, source_target_pairs={{0,8},{8,0},{16,24},{24,16},{1,9},{9,1},{17,25},{25,17},{2,10},{10... | collective-permute-start | bytes 1572872 | tf_op jit(solution)/shard_map/ppermute | solution.py:529
  135.2 56.6 %collective-permute-start.17 = (bf16[512,512]{1,0:T(8,128)(2,1)S(1)}, bf16[512,512]{1,0:T(8,128)(2,1)S(1)}, u32[]{:S(2)}, u32[]{:S(2)}) collective-permute-start(bf16[512,512]{1,0:T(8,128)(2,1)S(1)} %collective-permute-done.16.refs_4_), channel_id=1, source_target_pairs={{0,8},{8,0},{16,24},{24,16},{1,9},{9,1},{17,25},{25,17},{2,10},{10... | collective-permute-start | bytes 1572872 | tf_op jit(solution)/shard_map/ppermute | solution.py:529
  334.4 55.4 %collective-permute-start.18 = (bf16[2,1024,512]{2,1,0:T(8,128)(2,1)}, bf16[2,1024,512]{2,1,0:T(8,128)(2,1)}, u32[]{:S(2)}, u32[]{:S(2)}) collective-permute-start(bf16[2,1024,512]{2,1,0:T(8,128)(2,1)} %get-tuple-element.132), channel_id=1, source_target_pairs={{0,8},{24,16},{1,9},{25,17},{2,10},{26,18},{3,11},{27,19},{4,12},{... | collective-permute-start | bytes 6291464 | tf_op jit(solution)/shard_map/ppermute | solution.py:910
  389.8 418.5 %reduce-scatter.3.cloned.1.call-start = ((), (), s32[]{:S(2)}) async-start(), calls=%async_computation.6 | async-start | bytes 9437184 | tf_op jit(solution)/shard_map/reduce_scatter | solution.py:653
  395.3 48.4 %collective-permute-start.19 = (bf16[2,1024,512]{2,1,0:T(8,128)(2,1)S(1)}, bf16[2,1024,512]{2,1,0:T(8,128)(2,1)}, u32[]{:S(2)}, u32[]{:S(2)}) collective-permute-start(bf16[2,1024,512]{2,1,0:T(8,128)(2,1)S(1)} %add_convert_fusion.13), channel_id=1, source_target_pairs={{8,16},{16,8},{9,17},{17,9},{10,18},{18,10},{11,19},{19,11},{12,20... | collective-permute-start | bytes 6291464 | tf_op jit(solution)/shard_map/ppermute | solution.py:910
  508.8 48.3 %collective-permute-start.25 = (bf16[2,1024,512]{2,1,0:T(8,128)(2,1)}, bf16[2,1024,512]{2,1,0:T(8,128)(2,1)}, u32[]{:S(2)}, u32[]{:S(2)}) collective-permute-start(bf16[2,1024,512]{2,1,0:T(8,128)(2,1)} %broadcast_select_fusion.6), channel_id=1, source_target_pairs={{0,4},{2,6},{4,0},{6,2},{1,5},{3,7},{5,1},{7,3},{8,12},{10,14},{12... | collective-permute-start | bytes 6291464 | tf_op jit(solution)/shard_map/ppermute | solution.py:910
  612.3 51.2 %collective-permute-start.29 = (bf16[2,2,1024,512]{3,2,1,0:T(8,128)(2,1)}, bf16[2,2,1024,512]{3,2,1,0:T(8,128)(2,1)}, u32[]{:S(2)}, u32[]{:S(2)}) collective-permute-start(bf16[2,2,1024,512]{3,2,1,0:T(8,128)(2,1)} %get-tuple-element.147), channel_id=1, source_target_pairs={{0,2},{2,0},{4,6},{6,4},{1,3},{3,1},{5,7},{7,5},{8,10},{10,8},{12,... | collective-permute-start | bytes 12582920 | tf_op jit(solution)/shard_map/ppermute | solution.py:910
  612.7 53.2 %collective-permute-start.32 = (bf16[2,2,1024,512]{3,2,1,0:T(8,128)(2,1)}, bf16[2,2,1024,512]{3,2,1,0:T(8,128)(2,1)}, u32[]{:S(2)}, u32[]{:S(2)}) collective-permute-start(bf16[2,2,1024,512]{3,2,1,0:T(8,128)(2,1)} %get-tuple-element.151), channel_id=1, source_target_pairs={{0,2},{2,0},{4,6},{6,4},{1,3},{3,1},{5,7},{7,5},{8,10},{10,8},{12,... | collective-permute-start | bytes 12582920 | tf_op jit(solution)/shard_map/ppermute | solution.py:910
  614.7 48.1 %collective-permute-start.30 = (bf16[2,1024,512]{2,1,0:T(8,128)(2,1)}, bf16[2,1024,512]{2,1,0:T(8,128)(2,1)S(1)}, u32[]{:S(2)}, u32[]{:S(2)}) collective-permute-start(bf16[2,1024,512]{2,1,0:T(8,128)(2,1)} %get-tuple-element.148), channel_id=1, source_target_pairs={{0,8},{24,16},{8,0},{16,24},{1,9},{25,17},{9,1},{17,25},{2,10},{26... | collective-permute-start | bytes 6291464 | tf_op jit(solution)/shard_map/ppermute | solution.py:910
  619.6 59.1 %collective-permute-start.33 = (bf16[2,1024,512]{2,1,0:T(8,128)(2,1)}, bf16[2,1024,512]{2,1,0:T(8,128)(2,1)}, u32[]{:S(2)}, u32[]{:S(2)}) collective-permute-start(bf16[2,1024,512]{2,1,0:T(8,128)(2,1)} %broadcast_select_fusion.3), channel_id=1, source_target_pairs={{0,4},{2,6},{4,0},{6,2},{1,5},{3,7},{5,1},{7,3},{8,12},{10,14},{12... | collective-permute-start | bytes 6291464 | tf_op jit(solution)/shard_map/ppermute | solution.py:910
  679.7 49.4 %collective-permute-start.36 = (bf16[1,2,1024,512]{3,2,1,0:T(8,128)(2,1)S(1)}, bf16[1,2,1024,512]{3,2,1,0:T(8,128)(2,1)S(1)}, u32[]{:S(2)}, u32[]{:S(2)}) collective-permute-start(bf16[1,2,1024,512]{3,2,1,0:T(8,128)(2,1)S(1)} %add_convert_fusion.1), channel_id=1, source_target_pairs={{0,1},{1,0},{2,3},{3,2},{4,5},{5,4},{6,7},{7,6},{8,9},{9,8},{10,11... | collective-permute-start | bytes 6291464 | tf_op jit(solution)/shard_map/ppermute | solution.py:910
  680.7 50.8 %collective-permute-start.35 = (bf16[2,1024,512]{2,1,0:T(8,128)(2,1)S(1)}, bf16[2,1024,512]{2,1,0:T(8,128)(2,1)S(1)}, u32[]{:S(2)}, u32[]{:S(2)}) collective-permute-start(bf16[2,1024,512]{2,1,0:T(8,128)(2,1)S(1)} %add_convert_fusion.3), channel_id=1, source_target_pairs={{8,16},{16,8},{9,17},{17,9},{10,18},{18,10},{11,19},{19,11},{12,20... | collective-permute-start | bytes 6291464 | tf_op jit(solution)/shard_map/ppermute | solution.py:910
  684.0 49.4 %collective-permute-start.37 = (bf16[2,1024,512]{2,1,0:T(8,128)(2,1)S(1)}, bf16[2,1024,512]{2,1,0:T(8,128)(2,1)S(1)}, u32[]{:S(2)}, u32[]{:S(2)}) collective-permute-start(bf16[2,1024,512]{2,1,0:T(8,128)(2,1)S(1)} %pad_maximum_fusion.1), channel_id=1, source_target_pairs={{0,2},{2,0},{4,6},{6,4},{1,3},{3,1},{5,7},{7,5},{8,10},{10,8},{12,... | collective-permute-start | bytes 6291464 | tf_op jit(solution)/shard_map/ppermute | solution.py:910
  684.1 52.1 %collective-permute-start.41 = (bf16[2,1024,512]{2,1,0:T(8,128)(2,1)S(1)}, bf16[2,1024,512]{2,1,0:T(8,128)(2,1)S(1)}, u32[]{:S(2)}, u32[]{:S(2)}) collective-permute-start(bf16[2,1024,512]{2,1,0:T(8,128)(2,1)S(1)} %add_convert_fusion.2), channel_id=1, source_target_pairs={{8,0},{16,24},{9,1},{17,25},{10,2},{18,26},{11,3},{19,27},{12,4},{... | collective-permute-start | bytes 6291464 | tf_op jit(solution)/shard_map/ppermute | solution.py:910
  734.8 48.5 %collective-permute-start.40 = (bf16[2,1024,512]{2,1,0:T(8,128)(2,1)}, bf16[2,1024,512]{2,1,0:T(8,128)(2,1)}, u32[]{:S(2)}, u32[]{:S(2)}) collective-permute-start(bf16[2,1024,512]{2,1,0:T(8,128)(2,1)} %add_convert_fusion), channel_id=1, source_target_pairs={{8,0},{16,24},{9,1},{17,25},{10,2},{18,26},{11,3},{19,27},{12,4},{... | collective-permute-start | bytes 6291464 | tf_op jit(solution)/shard_map/ppermute | solution.py:910
  737.7 64.5 %collective-permute-start.42 = (bf16[2,1024,512]{2,1,0:T(8,128)(2,1)}, bf16[2,1024,512]{2,1,0:T(8,128)(2,1)}, u32[]{:S(2)}, u32[]{:S(2)}) collective-permute-start(bf16[2,1024,512]{2,1,0:T(8,128)(2,1)} %broadcast_select_fusion), channel_id=1, source_target_pairs={{0,4},{2,6},{4,0},{6,2},{1,5},{3,7},{5,1},{7,3},{8,12},{10,14},{12... | collective-permute-start | bytes 6291464 | tf_op jit(solution)/shard_map/ppermute | solution.py:910
  740.5 64.6 %collective-permute-start.38 = (bf16[1,1,1024,512]{3,2,1,0:T(8,128)(2,1)}, bf16[1,1,1024,512]{3,2,1,0:T(8,128)(2,1)}, u32[]{:S(2)}, u32[]{:S(2)}) collective-permute-start(bf16[1,1,1024,512]{3,2,1,0:T(8,128)(2,1)} %add_convert_fusion.15), channel_id=1, source_target_pairs={{0,1},{1,0},{2,3},{3,2},{4,5},{5,4},{6,7},{7,6},{8,9},{9,8},{10,11... | collective-permute-start | bytes 3145736 | tf_op jit(solution)/shard_map/ppermute | solution.py:910
  (87 other events, 1551.3 us)
Sparse Core Ops, SparseCore 0:
  10.5 85.9 all-gather.4
  98.4 65.7 all-gather.6
  166.7 54.2 all-gather.10
  222.7 54.2 all-gather.8
  389.9 70.5 reduce-scatter.4
  564.9 82.1 reduce-scatter.2

commit v4 on v3

--- a/solution.py
+++ b/solution.py
@@ -33,6 +33,32 @@
 def cost(flops, *arrays):
     size = sum(a.size * a.dtype.itemsize for a in arrays)
     return pl.CostEstimate(flops=int(flops) // 64, transcendentals=0, bytes_accessed=int(size) // 64)
+
+
+def launch(deps, kernel, grid_spec=None, grid=None, in_specs=None, out_specs=None, **options):
+    prefetch, scratch = 0, ()
+    if grid_spec is not None:
+        prefetch, scratch, grid = grid_spec.num_scalar_prefetch, grid_spec.scratch_shapes, grid_spec.grid
+        in_specs, out_specs = grid_spec.in_specs, grid_spec.out_specs
+    in_specs = list(in_specs)
+    start = prefetch + len(in_specs)
+    end = start + len(deps)
+
+    def body(*refs):
+        kernel(*refs[:start], *refs[end:])
+
+    call = pl.pallas_call(
+        body,
+        grid_spec=pltpu.PrefetchScalarGridSpec(
+            num_scalar_prefetch=prefetch,
+            grid=grid,
+            in_specs=in_specs + [pl.BlockSpec(memory_space=pl.ANY)] * len(deps),
+            out_specs=out_specs,
+            scratch_shapes=scratch,
+        ),
+        **options,
+    )
+    return lambda *args: call(*args, *deps)
 
 
 def sds(shape, dtype):
@@ -57,10 +83,11 @@
         out_ref[0, r] = (hat * gain_ref[r] + bias_ref[r]).astype(bf16)
 
 
-def norm_call(x_all, gain, bias):
+def norm_call(deps, x_all, gain, bias):
     cols, rows, toks, feats = x_all.shape
     tb = min(512, toks)
-    return pl.pallas_call(
+    return launch(
+        deps,
         partial(norm_kernel, width=rows * feats),
         grid=(cols, toks // tb),
         in_specs=[
@@ -92,12 +119,13 @@
     out_ref[...] = acc.astype(out_ref.dtype)
 
 
-def project_call(x_all, weight, width, index, dtype, name):
+def project_call(deps, x_all, weight, width, index, dtype, name):
     cols, rows, toks, feats = x_all.shape
     tb = min(512, toks)
     per = toks // tb
     out = sds((cols * toks, width), dtype)
-    return pl.pallas_call(
+    return launch(
+        deps,
         project_kernel,
         grid=(cols, per),
         in_specs=[
@@ -142,7 +170,7 @@
         sum_ref[:, cut] += jnp.sum(dpre.astype(f32).reshape(tb // 8, 8, chunk), 0)
 
 
-def hidden_call(normed, grad, up, down, bias):
+def hidden_call(deps, normed, grad, up, down, bias):
     cols, rows, toks, feats = normed.shape
     width = up.shape[2]
     tb = min(512, toks)
@@ -150,7 +178,8 @@
     out = sds((cols * toks, width), bf16)
     tok_spec = pl.BlockSpec((1, rows, tb, feats), lambda c, t: (c, 0, t, 0))
     out_spec = pl.BlockSpec((tb, width), lambda c, t: (c * per + t, 0))
-    return pl.pallas_call(
+    return launch(
+        deps,
         partial(hidden_kernel, chunk=min(256, width)),
         grid=(cols, per),
         in_specs=[tok_spec, tok_spec, whole(up.shape), whole(down.shape), whole((1, width))],
@@ -168,7 +197,7 @@
         out_ref[r] = acc.astype(bf16)
 
 
-def combine_all_call(a, b, wa, index, wb, dims_b, cols, feats, name):
+def combine_all_call(deps, a, b, wa, index, wb, dims_b, cols, feats, name):
     toks = a.shape[0] // cols
     rows = wa.shape[0]
     tb = min(512, toks)
@@ -176,7 +205,8 @@
     out = sds((cols * rows, toks, feats), bf16)
     flops = 2 * a.shape[0] * (a.shape[1] + b.shape[1]) * rows * feats
     in_map = lambda c, t: (c * per + t, 0)
-    return pl.pallas_call(
+    return launch(
+        deps,
         partial(combine_all_kernel, dims_b=dims_b),
         grid=(cols, per),
         in_specs=[
@@ -202,7 +232,7 @@
             out_ref[0, j] = acc.astype(bf16)
 
 
-def combine_call(own, a, b, wa, index, wb, dims_b, cols, feats, name):
+def combine_call(deps, own, a, b, wa, index, wb, dims_b, cols, feats, name):
     toks = a.shape[0] // cols
     rows = wa.shape[0]
     tb = min(512, toks)
@@ -211,7 +241,8 @@
     flops = 2 * a.shape[0] * (a.shape[1] + b.shape[1]) * rows * feats
     in_map = lambda c, t, own: (jnp.bitwise_xor(c, own[1]) * per + t, 0)
     out_spec = pl.BlockSpec((1, rows // 2, tb, feats), lambda c, t, own: (c, 0, t, 0))
-    return pl.pallas_call(
+    return launch(
+        deps,
         partial(combine_kernel, dims_b=dims_b),
         grid_spec=pltpu.PrefetchScalarGridSpec(
             num_scalar_prefetch=1,
@@ -262,7 +293,7 @@
                 out_ref[j] = acc_ref[r].astype(bf16)
 
 
-def wgrad_call(own, pairs, chunks, name):
+def wgrad_call(deps, own, pairs, chunks, name):
     cols, rows, toks, feats = pairs[0][0][0].shape
     width = sum(ys[0].shape[1] for _, ys in pairs)
     tb = min(512, toks)
@@ -275,7 +306,8 @@
         specs += [pl.BlockSpec((1, rows, tb, feats), lambda t, own: (t // per, 0, t % per, 0))] * count
         specs += [pl.BlockSpec((tb, ys[0].shape[1]), lambda t, own: (t, 0))] * count
         arrays += xs + ys
-    return pl.pallas_call(
+    return launch(
+        deps,
         partial(wgrad_kernel, terms=len(pairs), count=count),
         grid_spec=pltpu.PrefetchScalarGridSpec(
             num_scalar_prefetch=1,
@@ -312,7 +344,7 @@
             out_ref[0] = far_ref[...]
 
 
-def assemble_call(place, pieces, halves, name):
+def assemble_call(deps, place, pieces, halves, name):
     rows = len(pieces) + len(halves)
     height, width = pieces[0].shape
     half = height // 2
@@ -325,7 +357,8 @@
 
         return at
 
-    return pl.pallas_call(
+    return launch(
+        deps,
         assemble_kernel,
         grid_spec=pltpu.PrefetchScalarGridSpec(
             num_scalar_prefetch=1,
@@ -354,7 +387,7 @@
             out_ref[...] = piece.T if turned else piece
 
 
-def place_call(own, pieces, size, index, turned, name):
+def place_call(deps, own, pieces, size, index, turned, name):
     rows = len(pieces)
     height, width = size, pieces[0][0].shape[2]
     parts = max(1, height // 1024)
@@ -375,7 +408,8 @@
         out = sds((rows * height, width), f32)
         block = (cut, width)
         out_map = lambda i, b, own: (jnp.bitwise_xor(own[0], i) * parts + b, 0)
-    return pl.pallas_call(
+    return launch(
+        deps,
         partial(place_kernel, turned=turned),
         grid_spec=pltpu.PrefetchScalarGridSpec(
             num_scalar_prefetch=1,
@@ -406,7 +440,7 @@
     return tuple(jnp.tile(t, (1, lanes // head_dim)) for t in (keep, from_back, from_front))
 
 
-def attention_call(qkv, bias, datt, lens, tables, heads, head_dim):
+def attention_call(deps, qkv, bias, datt, lens, tables, heads, head_dim):
     lanes = tables[0].shape[1]
     toks = qkv.shape[0]
     slots = toks // SLOT_LEN
@@ -487,7 +521,8 @@
     table_spec = pl.BlockSpec((SLOT_LEN, lanes), lambda s, p, lens: (0, 0), pipeline_mode=pl.Buffered(1))
     slot_lanes = lambda dt: pltpu.VMEM((SLOT_LEN, lanes), dt)
     flops = 6 * 2 * slots * pairs * heads * SLOT_LEN * SLOT_LEN * lanes
-    return pl.pallas_call(
+    return launch(
+        deps,
         kernel,
         grid_spec=pltpu.PrefetchScalarGridSpec(
             num_scalar_prefetch=1,
@@ -550,8 +585,8 @@
         halves.append((near, swap(near, "dp", 1)))
     place = jnp.stack([own, odd]).astype(jnp.int32)
 
-    def assemble(dep):
-        return assemble_call(place, [after(pieces[0], dep)] + pieces[1:], halves, name)
+    def assemble(deps):
+        return assemble_call(deps, place, pieces, halves, name)
 
     return assemble, halves[-1][0]
 
@@ -650,6 +685,10 @@
 
 class WholeSum:
     def __init__(self, blocks):
+        self.blocks, self.value = blocks, None
+
+    def send(self, deps):
+        blocks = after(self.blocks, *deps)
         self.value = lax.psum_scatter(blocks, ("col", "row"), scatter_dimension=0)
 
     def finished(self):
@@ -762,80 +801,69 @@
     line = LineSum()
     flows, grads = {"z": line}, {}
 
-    def norm_m(m, dep):
-        normed, mean, inv = norm_call(after(x_alls[m], dep), norm_full[:, 0], norm_full[:, 1])
+    def norm_m(m, deps):
+        normed, mean, inv = norm_call(deps, x_alls[m], norm_full[:, 0], norm_full[:, 1])
         normeds.append(normed)
         stats.append(
             tuple(lax.dynamic_index_in_dim(v, col_index, 0, False) for v in (mean, inv))
         )
         return inv
 
-    def hidden_m(m, dep):
+    def hidden_m(m, deps):
         if not m:
-            weights["up"], weights["down"] = up_own(dep), down_own(dep)
-        normed = after(normeds[m], dep)
+            weights["up"], weights["down"] = up_own(deps), down_own(deps)
         act, dpre, sum_up = hidden_call(
-            normed, g_alls[m], weights["up"], weights["down"], bias_up
+            deps, normeds[m], g_alls[m], weights["up"], weights["down"], bias_up
         )
         acts.append(act)
         dpres.append(dpre)
         sums_up.append(jnp.sum(sum_up, 0))
         return sum_up
 
-    def qkv_m(m, dep):
+    def qkv_m(m, deps):
         if not m:
-            weights["heads"] = heads_own(dep)
-        normed = after(normeds[m], dep)
-        qkvs[m] = project_call(normed, weights["heads"], qkv_width, 0, f32, "qkv")
-        g_all = after(g_alls[m], qkvs[m])
-        datts[m] = project_call(g_all, weights["heads"], out_width, 3, bf16, "datt")
+            weights["heads"] = heads_own(deps)
+        heads = weights["heads"]
+        qkvs[m] = project_call(deps, normeds[m], heads, qkv_width, 0, f32, "qkv")
+        datts[m] = project_call([qkvs[m]], g_alls[m], heads, out_width, 3, bf16, "datt")
         return datts[m]
 
-    def attention_m(m, dep):
-        datt = after(datts[m], dep)
+    def attention_m(m, deps):
         attns[m], dqkvs[m], sum_qkv = attention_call(
-            qkvs[m], bias_qkv, datt, lengths[m], tables, group, head_dim
+            deps, qkvs[m], bias_qkv, datts[m], lengths[m], tables, group, head_dim
         )
         sums_qkv.append(jnp.sum(sum_qkv, 0))
         return sum_qkv
 
-    def dnormed_m(m, dep):
-        dqkv = after(dqkvs[m], dep)
+    def dnormed_m(m, deps):
+        arrays = (dqkvs[m], dpres[m], weights["heads"], 0, weights["up"], NT, cols, feats)
         if not m:
-            blocks = combine_all_call(
-                dqkv, dpres[m], weights["heads"], 0, weights["up"], NT, cols, feats, "dnormed"
-            )
-            flows["n0"] = WholeSum(blocks)
-            return blocks
-        keep, send = combine_call(
-            own, dqkv, dpres[m], weights["heads"], 0, weights["up"], NT, cols, feats, "dnormed"
-        )
+            flows["n0"] = WholeSum(combine_all_call(deps, *arrays, "dnormed"))
+            return flows["n0"].blocks
+        keep, send = combine_call(deps, own, *arrays, "dnormed")
         flows[f"n{m}"] = ScatterSum(keep, send, False)
         return send
 
-    def branch_m(m, dep):
-        attn = after(attns[m], dep)
+    def branch_m(m, deps):
+        arrays = (attns[m], acts[m], weights["heads"], 3, weights["down"], NN, cols, feats)
         if not m:
-            blocks = combine_all_call(
-                attn, acts[m], weights["heads"], 3, weights["down"], NN, cols, feats, "branch"
-            )
-            flows["b0"] = WholeSum(blocks)
-            return blocks
-        keep, send = combine_call(
-            own, attn, acts[m], weights["heads"], 3, weights["down"], NN, cols, feats, "branch"
-        )
-        flows[f"b{m}"] = ScatterSum(keep, send, True)
+            flows["b0"] = WholeSum(combine_all_call(deps, *arrays, "branch"))
+            return flows["b0"].blocks
+        keep, send = combine_call(deps, own, *arrays, "branch")
+        flows[f"b{m}"] = ScatterSum(keep, send, False)
         return send
 
-    def grad_m(group_name, dep):
+    def grad_m(group_name, deps):
         if group_name == "d":
-            terms = [(g_alls, [after(acts[0], dep)] + acts[1:])]
+            terms = [(g_alls, acts)]
         elif group_name == "u":
-            terms = [(normeds, [after(dpres[0], dep)] + dpres[1:])]
+            terms = [(normeds, dpres)]
         else:
-            dqkv = [after(dqkvs[0], dep)] + [dqkvs[m] for m in range(1, micros)]
-            terms = [(normeds, dqkv), (g_alls, [attns[m] for m in range(micros)])]
-        grads[group_name] = wgrad_call(own, terms, 2, "grad_" + group_name)
+            terms = [
+                (normeds, [dqkvs[m] for m in range(micros)]),
+                (g_alls, [attns[m] for m in range(micros)]),
+            ]
+        grads[group_name] = wgrad_call(deps, own, terms, 2, "grad_" + group_name)
         line.coming += grads[group_name][::-1]
         flows[group_name] = Deliver(line, 2 * len(grads) - 1, 2 * len(grads) - 2)
         return grads[group_name][0]
@@ -848,14 +876,13 @@
 
     def place(name, deps=()):
         parts = flows[name].pieces
-        parts = [(after(parts[0][0], *deps), parts[0][1])] + parts[1:]
         if name == "d":
-            placed["down"] = place_call(own, parts, ff_local, 0, False, "place_down")
+            placed["down"] = place_call(deps, own, parts, ff_local, 0, False, "place_down")
         elif name == "u":
-            placed["up"] = place_call(own, parts, ff_local, 0, True, "place_up")
+            placed["up"] = place_call(deps, own, parts, ff_local, 0, True, "place_up")
         else:
-            placed["qkv"] = place_call(own, parts, qkv_width, 0, False, "place_qkv")
-            placed["out"] = place_call(own, parts, out_width, 3, False, "place_out")
+            placed["qkv"] = place_call(deps, own, parts, qkv_width, 0, False, "place_qkv")
+            placed["out"] = place_call(deps, own, parts, out_width, 3, False, "place_out")
 
     finals = {}
 
@@ -878,13 +905,13 @@
         flows["r"] = SmallSum(jnp.stack(row_parts), ("row",))
         flows["f"] = SmallSum(features, ("col", "dp"))
 
-    def biases_m(which, dep):
+    def biases_m(which, deps):
         flows["s"] = SmallSum(jnp.concatenate([sum(sums_up), sum(sums_qkv)]), ("dp",), True)
-        return dep
-
-    def place_m(name, dep):
-        place(name, [dep])
-        return placed["down" if name == "d" else "up" if name == "u" else "out"]
+        return deps[-1]
+
+    def place_m(name, deps):
+        place(name, deps)
+        return placed["down" if name == "d" else "up" if name == "u" else "qkv"]
 
     kernels.update(biases=biases_m, place=place_m)
 
@@ -892,30 +919,35 @@
         ((), ("norm0", "hidden0", "qkv0", "attention0")),
         ((), ("norm1", "hidden1")),
         ((), ("gradd",)),
-        (("z",), ("gradu", "dnormed0")),
-        (("z",), ("qkv1", "branch0")),
-        (("z",), ("attention1",)),
-        (("z", "d"), ("gradh", "biases0")),
+        (("z",), ("qkv1", "attention1")),
+        (("z",), ("gradh", "dnormed0")),
+        (("z",), ("gradu", "branch0")),
         (("z", "d"), ("dnormed1", "branch1")),
-        (("z", "n1", "b1", "u"), ("placed",)),
-        (("z", "n1", "b1", "u"), ()),
-        (("z", "n1", "b1", "h"), ("placeu",)),
+        (("z", "d", "n1", "b1"), ("biases0",)),
+        (("z", "n1", "h"), ("placed",)),
+        (("z", "n1", "b1", "h"), ()),
+        (("z", "u", "b1", "r", "f"), ("placeh",)),
     ]
     deps = [norm_full]
     for names, work in program:
         moved = []
+        if "r" not in flows and "r" in names and all(flows[f"n{m}"].finished() for m in range(micros)):
+            sums()
+            deps = deps + [flows["r"].value]
         for name in names:
-            if not flows[name].finished():
+            if name in flows and not flows[name].finished():
                 jobs = flows[name].start()
                 moved.append((flows[name], [lax.ppermute(after(v, *deps), *to) for v, *to in jobs]))
         last = deps
         ran = []
         for item in work:
             kind, which = item[:-1], item[-1]
-            dep = last[0] if len(last) == 1 else after(last[0], *last[1:])
-            last = [kernels[kind](int(which) if which.isdigit() else which, dep)]
+            last = [kernels[kind](int(which) if which.isdigit() else which, last)]
             ran = last
         deps = [value for flow, values in moved for value in flow.done(values)] + ran
+        for flow in flows.values():
+            if isinstance(flow, WholeSum) and flow.value is None:
+                flow.send(deps)
     while True:
         if "r" not in flows and all(flows[f"n{m}"].finished() for m in range(micros)):
             sums()

time: 860 us -> 888 us (1.033)
  other arithmetic: 87.6 us -> 101 us
  waiting for transfers between devices: 230 us -> 242 us
    ppermute x36, waiting for transfers between devices: 147 us -> 159 us  [on_device(): lax.ppermute(after(v, *deps), *to)]
    convert_element_type x12, other arithmetic: 28.6 us -> 37.7 us  [add_low(): return sum((v.astype(f32) for v in values)).astype(bf16)]
  transfers between devices with their start and end apart: 60 -> 60, of which waited for: 19 -> 17; matrix products, arithmetic and copies ran while one was open for 14% -> 14% of each run, Pallas kernels for 41% -> 40%
where the time goes in v4:
time: 888 us; the launch traced here: 881 us
  Pallas kernels  409 us (46%)
  waiting for transfers between devices  242 us (27%)
  other arithmetic  101 us (11%)
  starting transfers between devices  65.6 us (7%)
  local copies, waits for them, and re-layouts  47.4 us (5%)
  between operations  15.5 us (2%)
    pallas_call x24, Pallas kernels, launch(): return lambda *args: call(*args, *deps)  409 us
    ppermute x36, waiting for transfers between devices, on_device(): lax.ppermute(after(v, *deps), *to)  159 us
    ppermute x18, waiting for transfers between devices, swap(): lax.ppermute(value, axis, [(i, i ^ mask) for i in range(lax.axis_size(axi...  74.5 us
    ppermute x36, starting transfers between devices, on_device(): lax.ppermute(after(v, *deps), *to)  42.2 us
    convert_element_type x12, other arithmetic, add_low(): return sum((v.astype(f32) for v in values)).astype(bf16)  37.7 us
    ppermute x18, starting transfers between devices, swap(): lax.ppermute(value, axis, [(i, i ^ mask) for i in range(lax.axis_size(axi...  23.2 us
    select_n x4, other arithmetic, start(): moves.append((jnp.where(self.end, enter, leave), 'dp', inward + outward))  19 us
  transfers between devices with their start and end apart: 60, of which 17 were waited for; matrix products, arithmetic and copies ran while one was open for 14% of the time, Pallas kernels for 40%

profile of v4, /device:TPU:0, one launch (start us, length us, event | category | flops | bytes accessed | tf_op | source)
XLA Modules:
  0.0 880.8 jit_solution(13794571979505755779)
XLA Ops:
  28.7 15.4 %collective-permute-done.4.refs_5_ = bf16[256,1024]{1,0:T(8,128)(2,1)} collective-permute-done((bf16[256,1024]{1,0:T(8,128)(2,1)}, bf16[256,1024]{1,0:T(8,128)(2,1)}, u32[]{:S(2)}, u32[]{:S(2)}) %collective-permute-start.4) | collective-permute-done | bytes 524320 | tf_op jit(solution)/shard_map/ppermute | solution.py:564
  63.4 18.4 %collective-permute-done.5.refs_5_ = bf16[512,512]{1,0:T(8,128)(2,1)} collective-permute-done((bf16[512,512]{1,0:T(8,128)(2,1)}, bf16[512,512]{1,0:T(8,128)(2,1)}, u32[]{:S(2)}, u32[]{:S(2)}) %collective-permute-start.5) | collective-permute-done | bytes 524320 | tf_op jit(solution)/shard_map/ppermute | solution.py:564
  90.5 11.3 %collective-permute-done.15.refs_3_ = bf16[512,512]{1,0:T(8,128)(2,1)} collective-permute-done((bf16[512,512]{1,0:T(8,128)(2,1)}, bf16[512,512]{1,0:T(8,128)(2,1)}, u32[]{:S(2)}, u32[]{:S(2)}) %collective-permute-start.15) | collective-permute-done | bytes 524320 | tf_op jit(solution)/shard_map/ppermute | solution.py:564
  119.8 15.6 %collective-permute-done.8.refs_5_ = bf16[512,512]{1,0:T(8,128)(2,1)S(1)} collective-permute-done((bf16[512,512]{1,0:T(8,128)(2,1)}, bf16[512,512]{1,0:T(8,128)(2,1)S(1)}, u32[]{:S(2)}, u32[]{:S(2)}) %collective-permute-start.8) | collective-permute-done | bytes 524320 | tf_op jit(solution)/shard_map/ppermute | solution.py:564
  138.2 10.8 %norm.2 = (bf16[2,4,1024,512]{3,2,1,0:T(8,128)(2,1)}, f32[2,1024,1]{2,1,0:T(8,128)}, f32[2,1024,1]{2,1,0:T(8,128)}) custom-call(bf16[2,4,1024,512]{3,2,1,0:T(8,128)(2,1)} %bitcast.146, f32[4,1,512]{2,1,0:T(1,128)} %get-tuple-element.194.refs_1_, f32[4,1,512]{2,1,0:T(1,128)} %get-tuple-element.193.refs_2_, f32[4,2,512]{2,1,0:T(2,128)} %copy-done.48), custom_call_target="tpu_custom_call" | custom-call | flops 524288 | bytes 262144 | tf_op jit(solution)/shard_map/norm/pallas_call | solution.py:61
  164.2 27.7 %hidden.2 = (bf16[2048,1024]{1,0:T(8,128)(2,1)}, bf16[2048,1024]{1,0:T(8,128)(2,1)}, f32[8,1024]{1,0:T(8,128)}) custom-call(bf16[2,4,1024,512]{3,2,1,0:T(8,128)(2,1)} %get-tuple-element.79.refs_0_.refs_1_, bf16[2,4,1024,512]{3,2,1,0:T(8,128)(2,1)} %bitcast.135, bf16[4,512,1024]{2,1,0:T(8,128)(2,1)} %up_own.1.refs_2_.refs_3_.refs_4_, ...), custom_call_target="tpu_custom_call" | custom-call | flops 268435456 | bytes 524288 | tf_op jit(solution)/shard_map/hidden/pallas_call | solution.py:61
  201.3 11.6 %qkv.2.refs_2_.refs_1_ = f32[2048,768]{1,0:T(8,128)} custom-call(bf16[2,4,1024,512]{3,2,1,0:T(8,128)(2,1)} %get-tuple-element.79.refs_0_.refs_1_, bf16[4,1024,512]{2,1,0:T(8,128)(2,1)} %heads_own.1.refs_1_.refs_2_.refs_3_, f32[8,1024]{1,0:T(8,128)} %get-tuple-element.85.refs_7_.refs_2_), custom_call_target="tpu_custom_call" | custom-call | flops 100663296 | bytes 294912 | tf_op jit(solution)/shard_map/qkv/pallas_call | solution.py:61
  219.7 39.8 %attention.2 = (bf16[2048,256]{1,0:T(8,128)(2,1)}, bf16[2048,768]{1,0:T(8,128)(2,1)}, f32[16,768]{1,0:T(8,128)}) custom-call(s32[2]{0:T(128)} %get-tuple-element.208.refs_0_, f32[2048,768]{1,0:T(8,128)} %qkv.2.refs_2_.refs_1_, f32[1,768]{1,0:T(1,128)} %reshape.480.refs_2_, bf16[2048,256]{1,0:T(8,128)(2,1)} %datt.2.refs_3_.refs_7_, ...), custom_call_target="tpu_custom_call" | custom-call | flops 201326592 | bytes 229376 | tf_op jit(solution)/shard_map/attention/pallas_call | solution.py:61
  277.0 28.1 %hidden.3 = (bf16[2048,1024]{1,0:T(8,128)(2,1)}, bf16[2048,1024]{1,0:T(8,128)(2,1)}, f32[8,1024]{1,0:T(8,128)}) custom-call(bf16[2,4,1024,512]{3,2,1,0:T(8,128)(2,1)} %get-tuple-element.89.refs_0_.refs_2_, bf16[2,4,1024,512]{3,2,1,0:T(8,128)(2,1)} %bitcast.139, bf16[4,512,1024]{2,1,0:T(8,128)(2,1)} %up_own.1.refs_2_.refs_3_.refs_4_, ...), custom_call_target="tpu_custom_call" | custom-call | flops 268435456 | bytes 524288 | tf_op jit(solution)/shard_map/hidden/pallas_call | solution.py:61
  305.1 29.3 %grad_d.1 = (bf16[2,1024,512]{2,1,0:T(8,128)(2,1)}, bf16[2,1024,512]{2,1,0:T(8,128)(2,1)}) custom-call(s32[2]{0:T(128)} %pad_add_fusion.1.refs_0_, bf16[2,4,1024,512]{3,2,1,0:T(8,128)(2,1)} %bitcast.137, bf16[2,4,1024,512]{3,2,1,0:T(8,128)(2,1)} %bitcast.140, bf16[2048,1024]{1,0:T(8,128)(2,1)} %get-tuple-element.87.refs_3_.refs_1_, ...), custom_call_target="tpu_custom_call" | custom-call | flops 268435456 | bytes 458752 | tf_op jit(solution)/shard_map/grad_d/pallas_call | solution.py:61
  337.9 11.7 %qkv.3.refs_2_.refs_1_ = f32[2048,768]{1,0:T(8,128)} custom-call(bf16[2,4,1024,512]{3,2,1,0:T(8,128)(2,1)} %get-tuple-element.89.refs_0_.refs_2_, bf16[4,1024,512]{2,1,0:T(8,128)(2,1)} %heads_own.1.refs_1_.refs_2_.refs_3_, bf16[2,1024,512]{2,1,0:T(8,128)(2,1)} %get-tuple-element.99.refs_2_), custom_call_target="tpu_custom_call" | custom-call | flops 100663296 | bytes 294912 | tf_op jit(solution)/shard_map/qkv/pallas_call | solution.py:61
  356.3 39.8 %attention.3 = (bf16[2048,256]{1,0:T(8,128)(2,1)}, bf16[2048,768]{1,0:T(8,128)(2,1)}, f32[16,768]{1,0:T(8,128)}) custom-call(s32[2]{0:T(128)} %get-tuple-element.209.refs_0_, f32[2048,768]{1,0:T(8,128)} %qkv.3.refs_2_.refs_1_, f32[1,768]{1,0:T(1,128)} %reshape.480.refs_2_, bf16[2048,256]{1,0:T(8,128)(2,1)} %datt.3.refs_3_.refs_7_, ...), custom_call_target="tpu_custom_call" | custom-call | flops 201326592 | bytes 229376 | tf_op jit(solution)/shard_map/attention/pallas_call | solution.py:61
  402.5 33.8 %grad_h.1 = (bf16[2,1024,512]{2,1,0:T(8,128)(2,1)}, bf16[2,1024,512]{2,1,0:T(8,128)(2,1)}) custom-call(s32[2]{0:T(128)} %pad_add_fusion.1.refs_0_, bf16[2,4,1024,512]{3,2,1,0:T(8,128)(2,1)} %get-tuple-element.79.refs_0_.refs_1_, bf16[2,4,1024,512]{3,2,1,0:T(8,128)(2,1)} %get-tuple-element.89.refs_0_.refs_2_, ...), custom_call_target="tpu_custom_call" | custom-call | flops 268435456 | bytes 720896 | tf_op jit(solution)/shard_map/grad_h/pallas_call | solution.py:61
  436.3 21.2 %dnormed.2.refs_7_ = bf16[8,1024,512]{2,1,0:T(8,128)(2,1)} custom-call(bf16[2048,768]{1,0:T(8,128)(2,1)} %get-tuple-element.101.refs_3_.refs_0_, bf16[2048,1024]{1,0:T(8,128)(2,1)} %get-tuple-element.90.refs_1_.refs_3_, bf16[4,1024,512]{2,1,0:T(8,128)(2,1)} %heads_own.1.refs_1_.refs_2_.refs_3_, bf16[4,512,1024]{2,1,0:T(8,128)(2,1)} %up_own.1.refs_2_.refs_3_.refs_4_, ...), custom_call_target="tpu_custom_call" | custom-call | flops 234881024 | bytes 376832 | tf_op jit(solution)/shard_map/dnormed/pallas_call | solution.py:61
  468.7 30.5 %grad_u.1 = (bf16[2,1024,512]{2,1,0:T(8,128)(2,1)}, bf16[2,1024,512]{2,1,0:T(8,128)(2,1)}) custom-call(s32[2]{0:T(128)} %pad_add_fusion.1.refs_0_, bf16[2,4,1024,512]{3,2,1,0:T(8,128)(2,1)} %get-tuple-element.79.refs_0_.refs_1_, bf16[2,4,1024,512]{3,2,1,0:T(8,128)(2,1)} %get-tuple-element.89.refs_0_.refs_2_, ...), custom_call_target="tpu_custom_call" | custom-call | flops 268435456 | bytes 458752 | tf_op jit(solution)/shard_map/grad_u/pallas_call | solution.py:61
  499.2 16.2 %branch.2.refs_7_ = bf16[8,1024,512]{2,1,0:T(8,128)(2,1)} custom-call(bf16[2048,256]{1,0:T(8,128)(2,1)} %get-tuple-element.86.refs_7_.refs_0_, bf16[2048,1024]{1,0:T(8,128)(2,1)} %get-tuple-element.87.refs_3_.refs_1_, bf16[4,1024,512]{2,1,0:T(8,128)(2,1)} %heads_own.1.refs_1_.refs_2_.refs_3_, bf16[4,1024,512]{2,1,0:T(8,128)(2,1)} %down_own.1.refs_3_.refs_4_, ...), custom_call_target="tpu_custom_call" | custom-call | flops 167772160 | bytes 344064 | tf_op jit(solution)/shard_map/branch/pallas_call | solution.py:61
  534.0 22.2 %dnormed.3 = (bf16[2,2,1024,512]{3,2,1,0:T(8,128)(2,1)}, bf16[2,2,1024,512]{3,2,1,0:T(8,128)(2,1)}) custom-call(s32[2]{0:T(128)} %pad_add_fusion.1.refs_0_, bf16[2048,768]{1,0:T(8,128)(2,1)} %get-tuple-element.102.refs_4_.refs_1_, bf16[2048,1024]{1,0:T(8,128)(2,1)} %get-tuple-element.92.refs_4_.refs_2_, ...), custom_call_target="tpu_custom_call" | custom-call | flops 234881024 | bytes 376832 | tf_op jit(solution)/shard_map/dnormed/pallas_call | solution.py:61
  556.2 16.7 %branch.3 = (bf16[2,2,1024,512]{3,2,1,0:T(8,128)(2,1)}, bf16[2,2,1024,512]{3,2,1,0:T(8,128)(2,1)}) custom-call(s32[2]{0:T(128)} %pad_add_fusion.1.refs_0_, bf16[2048,256]{1,0:T(8,128)(2,1)} %get-tuple-element.103.refs_8_.refs_1_, bf16[2048,1024]{1,0:T(8,128)(2,1)} %get-tuple-element.93.refs_4_.refs_2_, ...), custom_call_target="tpu_custom_call" | custom-call | flops 167772160 | bytes 344064 | tf_op jit(solution)/shard_map/branch/pallas_call | solution.py:61
  589.1 41.7 %collective-permute-done.28 = bf16[2,1024,512]{2,1,0:T(8,128)(2,1)S(1)} collective-permute-done((bf16[2,1024,512]{2,1,0:T(8,128)(2,1)}, bf16[2,1024,512]{2,1,0:T(8,128)(2,1)S(1)}, u32[]{:S(2)}, u32[]{:S(2)}) %collective-permute-start.28) | collective-permute-done | bytes 2097184 | tf_op jit(solution)/shard_map/ppermute | solution.py:940
  657.3 41.4 %collective-permute-done.33 = bf16[1,2,1024,512]{3,2,1,0:T(8,128)(2,1)} collective-permute-done((bf16[1,2,1024,512]{3,2,1,0:T(8,128)(2,1)}, bf16[1,2,1024,512]{3,2,1,0:T(8,128)(2,1)}, u32[]{:S(2)}, u32[]{:S(2)}) %collective-permute-start.33) | collective-permute-done | bytes 2097184 | tf_op jit(solution)/shard_map/ppermute | solution.py:940
  723.2 11.0 %collective-permute-done.37.refs_6_ = bf16[1,1,1024,512]{3,2,1,0:T(8,128)(2,1)} collective-permute-done((bf16[1,1,1024,512]{3,2,1,0:T(8,128)(2,1)}, bf16[1,1,1024,512]{3,2,1,0:T(8,128)(2,1)}, u32[]{:S(2)}, u32[]{:S(2)}) %collective-permute-start.37) | collective-permute-done | bytes 1048608 | tf_op jit(solution)/shard_map/ppermute | solution.py:940
  742.3 14.3 %collective-permute-done.35 = bf16[1,2,1024,512]{3,2,1,0:T(8,128)(2,1)} collective-permute-done((bf16[1,2,1024,512]{3,2,1,0:T(8,128)(2,1)}, bf16[1,2,1024,512]{3,2,1,0:T(8,128)(2,1)}, u32[]{:S(2)}, u32[]{:S(2)}) %collective-permute-start.35) | collective-permute-done | bytes 2097184 | tf_op jit(solution)/shard_map/ppermute | solution.py:940
  793.2 20.0 %collective-permute-done.41 = bf16[2,1024,512]{2,1,0:T(8,128)(2,1)} collective-permute-done((bf16[2,1024,512]{2,1,0:T(8,128)(2,1)}, bf16[2,1024,512]{2,1,0:T(8,128)(2,1)}, u32[]{:S(2)}, u32[]{:S(2)}) %collective-permute-start.41) | collective-permute-done | bytes 2097184 | tf_op jit(solution)/shard_map/ppermute | solution.py:940
  815.1 26.3 %collective-permute-done.39 = bf16[1,1,1024,512]{3,2,1,0:T(8,128)(2,1)S(1)} collective-permute-done((bf16[1,1,1024,512]{3,2,1,0:T(8,128)(2,1)S(1)}, bf16[1,1,1024,512]{3,2,1,0:T(8,128)(2,1)S(1)}, u32[]{:S(2)}, u32[]{:S(2)}) %collective-permute-start.39) | collective-permute-done | bytes 1048608 | tf_op jit(solution)/shard_map/ppermute | solution.py:940
  (362 shorter events, 310.7 us)
Async XLA Ops:
  7.2 131.0 %all-gather.5.cloned.1.call-start = ((), (), s32[]{:S(2)}) async-start(), calls=%async_computation.2 | async-start | bytes 9437184 | tf_op jit(solution)/shard_map/all_gather | solution.py:767
  10.4 153.8 %all-gather.7.cloned.1.call-start = ((), (), s32[]{:S(2)}) async-start(), calls=%async_computation.3 | async-start | bytes 9437184 | tf_op jit(solution)/shard_map/all_gather | solution.py:768
  14.8 244.7 %all-gather.9.cloned.1.call-start = ((), (), s32[]{:S(2)}) async-start(), calls=%async_computation.4 | async-start | bytes 9437184 | tf_op jit(solution)/shard_map/all_gather | solution.py:767
  15.5 261.5 %all-gather.11.cloned.1.call-start = ((), (), s32[]{:S(2)}) async-start(), calls=%async_computation.5 | async-start | bytes 9437184 | tf_op jit(solution)/shard_map/all_gather | solution.py:768
  16.1 722.3 %reduce-scatter.5.cloned.1.call-start = ((), (), s32[]{:S(2)}) async-start(), calls=%async_computation.7 | async-start | bytes 9437184 | tf_op jit(solution)/shard_map/reduce_scatter | solution.py:692
  101.8 90.1 %collective-permute-start.3 = (bf16[1024,512]{1,0:T(8,128)(2,1)}, bf16[1024,512]{1,0:T(8,128)(2,1)S(1)}, u32[]{:S(2)}, u32[]{:S(2)}) collective-permute-start(bf16[1024,512]{1,0:T(8,128)(2,1)} %get-tuple-element.177), channel_id=1, source_target_pairs={{0,2},{2,0},{4,6},{6,4},{1,3},{3,1},{5,7},{7,5},{8,10},{10,8},{12,... | collective-permute-start | bytes 3145736 | tf_op jit(solution)/shard_map/ppermute | solution.py:564
  106.4 49.9 %collective-permute-start.17 = (bf16[512,512]{1,0:T(8,128)(2,1)}, bf16[512,512]{1,0:T(8,128)(2,1)}, u32[]{:S(2)}, u32[]{:S(2)}) collective-permute-start(bf16[512,512]{1,0:T(8,128)(2,1)} %collective-permute-done.5.refs_5_), channel_id=1, source_target_pairs={{0,8},{8,0},{16,24},{24,16},{1,9},{9,1},{17,25},{25,17},{2,10},{10... | collective-permute-start | bytes 1572872 | tf_op jit(solution)/shard_map/ppermute | solution.py:564
  116.5 75.4 %collective-permute-start.7 = (bf16[512,512]{1,0:T(8,128)(2,1)S(1)}, bf16[512,512]{1,0:T(8,128)(2,1)S(1)}, u32[]{:S(2)}, u32[]{:S(2)}) collective-permute-start(bf16[512,512]{1,0:T(8,128)(2,1)S(1)} %collective-permute-done.6.refs_3_), channel_id=1, source_target_pairs={{0,8},{8,0},{16,24},{24,16},{1,9},{9,1},{17,25},{25,17},{2,10},{10... | collective-permute-start | bytes 1572872 | tf_op jit(solution)/shard_map/ppermute | solution.py:564
  135.4 56.5 %collective-permute-start.9 = (bf16[512,512]{1,0:T(8,128)(2,1)S(1)}, bf16[512,512]{1,0:T(8,128)(2,1)S(1)}, u32[]{:S(2)}, u32[]{:S(2)}) collective-permute-start(bf16[512,512]{1,0:T(8,128)(2,1)S(1)} %collective-permute-done.8.refs_5_), channel_id=1, source_target_pairs={{0,8},{8,0},{16,24},{24,16},{1,9},{9,1},{17,25},{25,17},{2,10},{10... | collective-permute-start | bytes 1572872 | tf_op jit(solution)/shard_map/ppermute | solution.py:564
  334.4 61.6 %collective-permute-start.18 = (bf16[2,1024,512]{2,1,0:T(8,128)(2,1)}, bf16[2,1024,512]{2,1,0:T(8,128)(2,1)S(1)}, u32[]{:S(2)}, u32[]{:S(2)}) collective-permute-start(bf16[2,1024,512]{2,1,0:T(8,128)(2,1)} %get-tuple-element.97), channel_id=1, source_target_pairs={{0,8},{24,16},{1,9},{25,17},{2,10},{26,18},{3,11},{27,19},{4,12},{... | collective-permute-start | bytes 6291464 | tf_op jit(solution)/shard_map/ppermute | solution.py:940
  398.0 59.5 %collective-permute-start.19 = (bf16[2,1024,512]{2,1,0:T(8,128)(2,1)S(1)}, bf16[2,1024,512]{2,1,0:T(8,128)(2,1)}, u32[]{:S(2)}, u32[]{:S(2)}) collective-permute-start(bf16[2,1024,512]{2,1,0:T(8,128)(2,1)S(1)} %copy-done.25), channel_id=1, source_target_pairs={{0,8},{24,16},{1,9},{25,17},{2,10},{26,18},{3,11},{27,19},{4,12},{... | collective-permute-start | bytes 6291464 | tf_op jit(solution)/shard_map/ppermute | solution.py:940
  400.6 59.9 %collective-permute-start.20 = (bf16[2,1024,512]{2,1,0:T(8,128)(2,1)}, bf16[2,1024,512]{2,1,0:T(8,128)(2,1)}, u32[]{:S(2)}, u32[]{:S(2)}) collective-permute-start(bf16[2,1024,512]{2,1,0:T(8,128)(2,1)} %add_convert_fusion.13.refs_9_), channel_id=1, source_target_pairs={{8,16},{16,8},{9,17},{17,9},{10,18},{18,10},{11,19},{19,11},{12,20... | collective-permute-start | bytes 6291464 | tf_op jit(solution)/shard_map/ppermute | solution.py:940
  466.5 380.1 %reduce-scatter.3.cloned.1.call-start = ((), (), s32[]{:S(2)}) async-start(), calls=%async_computation.6 | async-start | bytes 9437184 | tf_op jit(solution)/shard_map/reduce_scatter | solution.py:692
  466.6 53.1 %collective-permute-start.22 = (bf16[2,1024,512]{2,1,0:T(8,128)(2,1)S(1)}, bf16[2,1024,512]{2,1,0:T(8,128)(2,1)}, u32[]{:S(2)}, u32[]{:S(2)}) collective-permute-start(bf16[2,1024,512]{2,1,0:T(8,128)(2,1)S(1)} %add_convert_fusion.12.refs_5_), channel_id=1, source_target_pairs={{8,16},{16,8},{9,17},{17,9},{10,18},{18,10},{11,19},{19,11},{12,20... | collective-permute-start | bytes 6291464 | tf_op jit(solution)/shard_map/ppermute | solution.py:940
  582.5 52.1 %collective-permute-start.26 = (bf16[2,2,1024,512]{3,2,1,0:T(8,128)(2,1)}, bf16[2,2,1024,512]{3,2,1,0:T(8,128)(2,1)}, u32[]{:S(2)}, u32[]{:S(2)}) collective-permute-start(bf16[2,2,1024,512]{3,2,1,0:T(8,128)(2,1)} %get-tuple-element.116.refs_10_), channel_id=1, source_target_pairs={{0,2},{2,0},{4,6},{6,4},{1,3},{3,1},{5,7},{7,5},{8,10},{10,8},{12,... | collective-permute-start | bytes 12582920 | tf_op jit(solution)/shard_map/ppermute | solution.py:940
  582.5 57.1 %collective-permute-start.30 = (bf16[2,2,1024,512]{3,2,1,0:T(8,128)(2,1)}, bf16[2,2,1024,512]{3,2,1,0:T(8,128)(2,1)}, u32[]{:S(2)}, u32[]{:S(2)}) collective-permute-start(bf16[2,2,1024,512]{3,2,1,0:T(8,128)(2,1)} %get-tuple-element.122.refs_5_), channel_id=1, source_target_pairs={{0,2},{2,0},{4,6},{6,4},{1,3},{3,1},{5,7},{7,5},{8,10},{10,8},{12,... | collective-permute-start | bytes 12582920 | tf_op jit(solution)/shard_map/ppermute | solution.py:940
  589.0 54.7 %collective-permute-start.29 = (bf16[2,1024,512]{2,1,0:T(8,128)(2,1)S(1)}, bf16[2,1024,512]{2,1,0:T(8,128)(2,1)S(1)}, u32[]{:S(2)}, u32[]{:S(2)}) collective-permute-start(bf16[2,1024,512]{2,1,0:T(8,128)(2,1)S(1)} %pad_maximum_fusion), channel_id=1, source_target_pairs={{0,2},{2,0},{4,6},{6,4},{1,3},{3,1},{5,7},{7,5},{8,10},{10,8},{12,... | collective-permute-start | bytes 6291464 | tf_op jit(solution)/shard_map/ppermute | solution.py:940
  643.8 54.9 %collective-permute-start.33 = (bf16[1,2,1024,512]{3,2,1,0:T(8,128)(2,1)}, bf16[1,2,1024,512]{3,2,1,0:T(8,128)(2,1)}, u32[]{:S(2)}, u32[]{:S(2)}) collective-permute-start(bf16[1,2,1024,512]{3,2,1,0:T(8,128)(2,1)} %add_convert_fusion.3.refs_8_), channel_id=1, source_target_pairs={{0,1},{1,0},{2,3},{3,2},{4,5},{5,4},{6,7},{7,6},{8,9},{9,8},{10,11... | collective-permute-start | bytes 6291464 | tf_op jit(solution)/shard_map/ppermute | solution.py:940
  644.2 57.7 %collective-permute-start.31 = (bf16[2,1024,512]{2,1,0:T(8,128)(2,1)}, bf16[2,1024,512]{2,1,0:T(8,128)(2,1)}, u32[]{:S(2)}, u32[]{:S(2)}) collective-permute-start(bf16[2,1024,512]{2,1,0:T(8,128)(2,1)} %get-tuple-element.123), channel_id=1, source_target_pairs={{0,8},{24,16},{8,0},{16,24},{1,9},{25,17},{9,1},{17,25},{2,10},{26... | collective-permute-start | bytes 6291464 | tf_op jit(solution)/shard_map/ppermute | solution.py:940
  647.0 58.5 %collective-permute-start.32 = (bf16[2,1024,512]{2,1,0:T(8,128)(2,1)S(1)}, bf16[2,1024,512]{2,1,0:T(8,128)(2,1)}, u32[]{:S(2)}, u32[]{:S(2)}) collective-permute-start(bf16[2,1024,512]{2,1,0:T(8,128)(2,1)S(1)} %add_convert_fusion.4.refs_5_), channel_id=1, source_target_pairs={{8,16},{16,8},{9,17},{17,9},{10,18},{18,10},{11,19},{19,11},{12,20... | collective-permute-start | bytes 6291464 | tf_op jit(solution)/shard_map/ppermute | solution.py:940
  650.6 58.7 %collective-permute-start.34 = (bf16[2,1024,512]{2,1,0:T(8,128)(2,1)}, bf16[2,1024,512]{2,1,0:T(8,128)(2,1)S(1)}, u32[]{:S(2)}, u32[]{:S(2)}) collective-permute-start(bf16[2,1024,512]{2,1,0:T(8,128)(2,1)} %broadcast_select_fusion.3), channel_id=1, source_target_pairs={{0,4},{2,6},{4,0},{6,2},{1,5},{3,7},{5,1},{7,3},{8,12},{10,14},{12... | collective-permute-start | bytes 6291464 | tf_op jit(solution)/shard_map/ppermute | solution.py:940
  718.0 50.7 %collective-permute-start.42 = (bf16[2,1024,512]{2,1,0:T(8,128)(2,1)}, bf16[2,1024,512]{2,1,0:T(8,128)(2,1)}, u32[]{:S(2)}, u32[]{:S(2)}) collective-permute-start(bf16[2,1024,512]{2,1,0:T(8,128)(2,1)} %add_convert_fusion.1), channel_id=1, source_target_pairs={{8,0},{16,24},{9,1},{17,25},{10,2},{18,26},{11,3},{19,27},{12,4},{... | collective-permute-start | bytes 6291464 | tf_op jit(solution)/shard_map/ppermute | solution.py:940
  772.0 69.5 %collective-permute-start.43 = (bf16[2,1024,512]{2,1,0:T(8,128)(2,1)}, bf16[2,1024,512]{2,1,0:T(8,128)(2,1)}, u32[]{:S(2)}, u32[]{:S(2)}) collective-permute-start(bf16[2,1024,512]{2,1,0:T(8,128)(2,1)} %broadcast_select_fusion), channel_id=1, source_target_pairs={{0,4},{2,6},{4,0},{6,2},{1,5},{3,7},{5,1},{7,3},{8,12},{10,14},{12... | collective-permute-start | bytes 6291464 | tf_op jit(solution)/shard_map/ppermute | solution.py:940
  773.3 68.1 %collective-permute-start.39 = (bf16[1,1,1024,512]{3,2,1,0:T(8,128)(2,1)S(1)}, bf16[1,1,1024,512]{3,2,1,0:T(8,128)(2,1)S(1)}, u32[]{:S(2)}, u32[]{:S(2)}) collective-permute-start(bf16[1,1,1024,512]{3,2,1,0:T(8,128)(2,1)S(1)} %copy-done.23), channel_id=1, source_target_pairs={{0,4},{2,6},{4,0},{6,2},{1,5},{3,7},{5,1},{7,3},{8,12},{10,14},{12... | collective-permute-start | bytes 3145736 | tf_op jit(solution)/shard_map/ppermute | solution.py:940
  (97 other events, 1706.6 us)
Sparse Core Ops, SparseCore 0:
  10.5 85.9 all-gather.4
  98.4 65.7 all-gather.6
  166.7 54.2 all-gather.8
  222.7 54.2 all-gather.10
  466.6 71.3 reduce-scatter.4
  583.1 79.8 reduce-scatter.2

commit v5 on v4

--- a/solution.py
+++ b/solution.py
@@ -850,7 +850,7 @@
             flows["b0"] = WholeSum(combine_all_call(deps, *arrays, "branch"))
             return flows["b0"].blocks
         keep, send = combine_call(deps, own, *arrays, "branch")
-        flows[f"b{m}"] = ScatterSum(keep, send, False)
+        flows[f"b{m}"] = ScatterSum(keep, send, True)
         return send
 
     def grad_m(group_name, deps):
@@ -919,14 +919,14 @@
         ((), ("norm0", "hidden0", "qkv0", "attention0")),
         ((), ("norm1", "hidden1")),
         ((), ("gradd",)),
-        (("z",), ("qkv1", "attention1")),
-        (("z",), ("gradh", "dnormed0")),
         (("z",), ("gradu", "branch0")),
+        (("z",), ("qkv1", "dnormed0")),
+        (("z",), ("attention1",)),
+        (("z", "d"), ("gradh", "biases0")),
         (("z", "d"), ("dnormed1", "branch1")),
-        (("z", "d", "n1", "b1"), ("biases0",)),
-        (("z", "n1", "h"), ("placed",)),
-        (("z", "n1", "b1", "h"), ()),
-        (("z", "u", "b1", "r", "f"), ("placeh",)),
+        (("z", "n1", "b1", "u"), ("placed",)),
+        (("z", "n1", "b1", "u"), ()),
+        (("z", "h", "n1", "b1"), ("placeu",)),
     ]
     deps = [norm_full]
     for names, work in program:

time: 888 us -> 865 us (0.974)
  waiting for transfers between devices: 242 us -> 223 us
    ppermute x36, waiting for transfers between devices: 159 us -> 140 us  [on_device(): lax.ppermute(after(v, *deps), *to)]
  transfers between devices with their start and end apart: 60 -> 60, of which waited for: 17 -> 21; matrix products, arithmetic and copies ran while one was open for 14% -> 14% of each run, Pallas kernels for 40% -> 41%
where the time goes in v5:
time: 865 us; the launch traced here: 858 us
  Pallas kernels  409 us (47%)
  waiting for transfers between devices  223 us (26%)
  other arithmetic  98 us (11%)
  starting transfers between devices  70.4 us (8%)
  local copies, waits for them, and re-layouts  41.7 us (5%)
  between operations  15.5 us (2%)
    pallas_call x24, Pallas kernels, launch(): return lambda *args: call(*args, *deps)  409 us
    ppermute x36, waiting for transfers between devices, on_device(): lax.ppermute(after(v, *deps), *to)  140 us
    ppermute x18, waiting for transfers between devices, swap(): lax.ppermute(value, axis, [(i, i ^ mask) for i in range(lax.axis_size(axi...  74.5 us
    ppermute x36, starting transfers between devices, on_device(): lax.ppermute(after(v, *deps), *to)  47 us
    convert_element_type x12, other arithmetic, add_low(): return sum((v.astype(f32) for v in values)).astype(bf16)  34.5 us
    ppermute x18, starting transfers between devices, swap(): lax.ppermute(value, axis, [(i, i ^ mask) for i in range(lax.axis_size(axi...  23.2 us
    select_n x4, other arithmetic, start(): moves.append((jnp.where(self.end, enter, leave), 'dp', inward + outward))  20.1 us
  transfers between devices with their start and end apart: 60, of which 21 were waited for; matrix products, arithmetic and copies ran while one was open for 14% of the time, Pallas kernels for 41%

profile of v5, /device:TPU:0, one launch (start us, length us, event | category | flops | bytes accessed | tf_op | source)
XLA Modules:
  0.0 858.0 jit_solution(3226303611351000914)
XLA Ops:
  28.7 15.5 %collective-permute-done.4.refs_5_ = bf16[256,1024]{1,0:T(8,128)(2,1)} collective-permute-done((bf16[256,1024]{1,0:T(8,128)(2,1)}, bf16[256,1024]{1,0:T(8,128)(2,1)}, u32[]{:S(2)}, u32[]{:S(2)}) %collective-permute-start.4) | collective-permute-done | bytes 524320 | tf_op jit(solution)/shard_map/ppermute | solution.py:564
  63.3 18.4 %collective-permute-done.5.refs_5_ = bf16[512,512]{1,0:T(8,128)(2,1)} collective-permute-done((bf16[512,512]{1,0:T(8,128)(2,1)}, bf16[512,512]{1,0:T(8,128)(2,1)}, u32[]{:S(2)}, u32[]{:S(2)}) %collective-permute-start.5) | collective-permute-done | bytes 524320 | tf_op jit(solution)/shard_map/ppermute | solution.py:564
  90.4 11.3 %collective-permute-done.15.refs_3_ = bf16[512,512]{1,0:T(8,128)(2,1)} collective-permute-done((bf16[512,512]{1,0:T(8,128)(2,1)}, bf16[512,512]{1,0:T(8,128)(2,1)}, u32[]{:S(2)}, u32[]{:S(2)}) %collective-permute-start.15) | collective-permute-done | bytes 524320 | tf_op jit(solution)/shard_map/ppermute | solution.py:564
  119.6 15.6 %collective-permute-done.8.refs_5_ = bf16[512,512]{1,0:T(8,128)(2,1)S(1)} collective-permute-done((bf16[512,512]{1,0:T(8,128)(2,1)}, bf16[512,512]{1,0:T(8,128)(2,1)S(1)}, u32[]{:S(2)}, u32[]{:S(2)}) %collective-permute-start.8) | collective-permute-done | bytes 524320 | tf_op jit(solution)/shard_map/ppermute | solution.py:564
  138.2 10.9 %norm.2 = (bf16[2,4,1024,512]{3,2,1,0:T(8,128)(2,1)}, f32[2,1024,1]{2,1,0:T(8,128)}, f32[2,1024,1]{2,1,0:T(8,128)}) custom-call(bf16[2,4,1024,512]{3,2,1,0:T(8,128)(2,1)} %bitcast.146, f32[4,1,512]{2,1,0:T(1,128)} %get-tuple-element.194.refs_1_, f32[4,1,512]{2,1,0:T(1,128)} %get-tuple-element.193.refs_2_, f32[4,2,512]{2,1,0:T(2,128)} %copy-done.48), custom_call_target="tpu_custom_call" | custom-call | flops 524288 | bytes 262144 | tf_op jit(solution)/shard_map/norm/pallas_call | solution.py:61
  164.2 27.6 %hidden.2 = (bf16[2048,1024]{1,0:T(8,128)(2,1)}, bf16[2048,1024]{1,0:T(8,128)(2,1)}, f32[8,1024]{1,0:T(8,128)}) custom-call(bf16[2,4,1024,512]{3,2,1,0:T(8,128)(2,1)} %get-tuple-element.79.refs_0_.refs_1_, bf16[2,4,1024,512]{3,2,1,0:T(8,128)(2,1)} %bitcast.135, bf16[4,512,1024]{2,1,0:T(8,128)(2,1)} %up_own.1.refs_2_.refs_3_.refs_4_, ...), custom_call_target="tpu_custom_call" | custom-call | flops 268435456 | bytes 524288 | tf_op jit(solution)/shard_map/hidden/pallas_call | solution.py:61
  201.3 11.6 %qkv.2.refs_2_.refs_1_ = f32[2048,768]{1,0:T(8,128)} custom-call(bf16[2,4,1024,512]{3,2,1,0:T(8,128)(2,1)} %get-tuple-element.79.refs_0_.refs_1_, bf16[4,1024,512]{2,1,0:T(8,128)(2,1)} %heads_own.1.refs_1_.refs_2_.refs_3_, f32[8,1024]{1,0:T(8,128)} %get-tuple-element.85.refs_7_.refs_2_), custom_call_target="tpu_custom_call" | custom-call | flops 100663296 | bytes 294912 | tf_op jit(solution)/shard_map/qkv/pallas_call | solution.py:61
  219.7 39.9 %attention.2 = (bf16[2048,256]{1,0:T(8,128)(2,1)}, bf16[2048,768]{1,0:T(8,128)(2,1)}, f32[16,768]{1,0:T(8,128)}) custom-call(s32[2]{0:T(128)} %get-tuple-element.208.refs_0_, f32[2048,768]{1,0:T(8,128)} %qkv.2.refs_2_.refs_1_, f32[1,768]{1,0:T(1,128)} %reshape.481.refs_2_, bf16[2048,256]{1,0:T(8,128)(2,1)} %datt.2.refs_3_.refs_7_, ...), custom_call_target="tpu_custom_call" | custom-call | flops 201326592 | bytes 229376 | tf_op jit(solution)/shard_map/attention/pallas_call | solution.py:61
  259.6 10.7 %norm.3 = (bf16[2,4,1024,512]{3,2,1,0:T(8,128)(2,1)}, f32[2,1024,1]{2,1,0:T(8,128)}, f32[2,1024,1]{2,1,0:T(8,128)}) custom-call(bf16[2,4,1024,512]{3,2,1,0:T(8,128)(2,1)} %bitcast.147, f32[4,1,512]{2,1,0:T(1,128)} %get-tuple-element.194.refs_1_, f32[4,1,512]{2,1,0:T(1,128)} %get-tuple-element.193.refs_2_, f32[16,768]{1,0:T(8,128)} %get-tuple-element.88.refs_3_), custom_call_target="tpu_custom_call" | custom-call | flops 524288 | bytes 262144 | tf_op jit(solution)/shard_map/norm/pallas_call | solution.py:61
  277.0 27.9 %hidden.3 = (bf16[2048,1024]{1,0:T(8,128)(2,1)}, bf16[2048,1024]{1,0:T(8,128)(2,1)}, f32[8,1024]{1,0:T(8,128)}) custom-call(bf16[2,4,1024,512]{3,2,1,0:T(8,128)(2,1)} %get-tuple-element.89.refs_0_.refs_2_, bf16[2,4,1024,512]{3,2,1,0:T(8,128)(2,1)} %bitcast.139, bf16[4,512,1024]{2,1,0:T(8,128)(2,1)} %up_own.1.refs_2_.refs_3_.refs_4_, ...), custom_call_target="tpu_custom_call" | custom-call | flops 268435456 | bytes 524288 | tf_op jit(solution)/shard_map/hidden/pallas_call | solution.py:61
  304.9 29.3 %grad_d.1 = (bf16[2,1024,512]{2,1,0:T(8,128)(2,1)}, bf16[2,1024,512]{2,1,0:T(8,128)(2,1)}) custom-call(s32[2]{0:T(128)} %pad_add_fusion.1.refs_0_, bf16[2,4,1024,512]{3,2,1,0:T(8,128)(2,1)} %bitcast.137, bf16[2,4,1024,512]{3,2,1,0:T(8,128)(2,1)} %bitcast.140, bf16[2048,1024]{1,0:T(8,128)(2,1)} %get-tuple-element.87.refs_3_.refs_1_, ...), custom_call_target="tpu_custom_call" | custom-call | flops 268435456 | bytes 458752 | tf_op jit(solution)/shard_map/grad_d/pallas_call | solution.py:61
  338.9 29.9 %grad_u.1 = (bf16[2,1024,512]{2,1,0:T(8,128)(2,1)}, bf16[2,1024,512]{2,1,0:T(8,128)(2,1)}) custom-call(s32[2]{0:T(128)} %pad_add_fusion.1.refs_0_, bf16[2,4,1024,512]{3,2,1,0:T(8,128)(2,1)} %get-tuple-element.79.refs_0_.refs_1_, bf16[2,4,1024,512]{3,2,1,0:T(8,128)(2,1)} %get-tuple-element.89.refs_0_.refs_2_, ...), custom_call_target="tpu_custom_call" | custom-call | flops 268435456 | bytes 458752 | tf_op jit(solution)/shard_map/grad_u/pallas_call | solution.py:61
  368.8 15.9 %branch.2.refs_3_ = bf16[8,1024,512]{2,1,0:T(8,128)(2,1)} custom-call(bf16[2048,256]{1,0:T(8,128)(2,1)} %get-tuple-element.86.refs_0_.refs_7_, bf16[2048,1024]{1,0:T(8,128)(2,1)} %get-tuple-element.87.refs_3_.refs_1_, bf16[4,1024,512]{2,1,0:T(8,128)(2,1)} %heads_own.1.refs_1_.refs_2_.refs_3_, bf16[4,1024,512]{2,1,0:T(8,128)(2,1)} %down_own.1.refs_3_.refs_4_, ...), custom_call_target="tpu_custom_call" | custom-call | flops 167772160 | bytes 344064 | tf_op jit(solution)/shard_map/branch/pallas_call | solution.py:61
  393.8 11.6 %qkv.3.refs_2_.refs_1_ = f32[2048,768]{1,0:T(8,128)} custom-call(bf16[2,4,1024,512]{3,2,1,0:T(8,128)(2,1)} %get-tuple-element.89.refs_0_.refs_2_, bf16[4,1024,512]{2,1,0:T(8,128)(2,1)} %heads_own.1.refs_1_.refs_2_.refs_3_, bf16[2,1024,512]{2,1,0:T(8,128)(2,1)} %copy-done.4, bf16[8,1024,512]{2,1,0:T(8,128)(2,1)} %branch.2.refs_3_), custom_call_target="tpu_custom_call" | custom-call | flops 100663296 | bytes 294912 | tf_op jit(solution)/shard_map/qkv/pallas_call | solution.py:61
  412.1 21.2 %dnormed.2.refs_9_ = bf16[8,1024,512]{2,1,0:T(8,128)(2,1)} custom-call(bf16[2048,768]{1,0:T(8,128)(2,1)} %get-tuple-element.102.refs_0_.refs_3_, bf16[2048,1024]{1,0:T(8,128)(2,1)} %get-tuple-element.90.refs_3_.refs_1_, bf16[4,1024,512]{2,1,0:T(8,128)(2,1)} %heads_own.1.refs_1_.refs_2_.refs_3_, bf16[4,512,1024]{2,1,0:T(8,128)(2,1)} %up_own.1.refs_2_.refs_3_.refs_4_, ...), custom_call_target="tpu_custom_call" | custom-call | flops 234881024 | bytes 376832 | tf_op jit(solution)/shard_map/dnormed/pallas_call | solution.py:61
  448.6 39.9 %attention.3 = (bf16[2048,256]{1,0:T(8,128)(2,1)}, bf16[2048,768]{1,0:T(8,128)(2,1)}, f32[16,768]{1,0:T(8,128)}) custom-call(s32[2]{0:T(128)} %get-tuple-element.209.refs_0_, f32[2048,768]{1,0:T(8,128)} %qkv.3.refs_2_.refs_1_, f32[1,768]{1,0:T(1,128)} %reshape.481.refs_2_, bf16[2048,256]{1,0:T(8,128)(2,1)} %datt.3.refs_4_.refs_3_, ...), custom_call_target="tpu_custom_call" | custom-call | flops 201326592 | bytes 229376 | tf_op jit(solution)/shard_map/attention/pallas_call | solution.py:61
  508.1 34.1 %grad_h.1 = (bf16[2,1024,512]{2,1,0:T(8,128)(2,1)}, bf16[2,1024,512]{2,1,0:T(8,128)(2,1)}) custom-call(s32[2]{0:T(128)} %pad_add_fusion.1.refs_0_, bf16[2,4,1024,512]{3,2,1,0:T(8,128)(2,1)} %get-tuple-element.79.refs_0_.refs_1_, bf16[2,4,1024,512]{3,2,1,0:T(8,128)(2,1)} %get-tuple-element.89.refs_0_.refs_2_, ...), custom_call_target="tpu_custom_call" | custom-call | flops 268435456 | bytes 720896 | tf_op jit(solution)/shard_map/grad_h/pallas_call | solution.py:61
  567.2 22.1 %dnormed.3 = (bf16[2,2,1024,512]{3,2,1,0:T(8,128)(2,1)}, bf16[2,2,1024,512]{3,2,1,0:T(8,128)(2,1)}) custom-call(s32[2]{0:T(128)} %pad_add_fusion.1.refs_0_, bf16[2048,768]{1,0:T(8,128)(2,1)} %get-tuple-element.104.refs_4_.refs_1_, bf16[2048,1024]{1,0:T(8,128)(2,1)} %get-tuple-element.92.refs_4_.refs_2_, ...), custom_call_target="tpu_custom_call" | custom-call | flops 234881024 | bytes 376832 | tf_op jit(solution)/shard_map/dnormed/pallas_call | solution.py:61
  589.3 17.5 %branch.3 = (bf16[2,2,1024,512]{3,2,1,0:T(8,128)(2,1)}, bf16[2,2,1024,512]{3,2,1,0:T(8,128)(2,1)}) custom-call(s32[2]{0:T(128)} %pad_add_fusion.1.refs_0_, bf16[2048,256]{1,0:T(8,128)(2,1)} %get-tuple-element.103.refs_8_.refs_1_, bf16[2048,1024]{1,0:T(8,128)(2,1)} %get-tuple-element.93.refs_4_.refs_2_, ...), custom_call_target="tpu_custom_call" | custom-call | flops 167772160 | bytes 344064 | tf_op jit(solution)/shard_map/branch/pallas_call | solution.py:61
  633.6 33.3 %collective-permute-done.30 = bf16[2,1024,512]{2,1,0:T(8,128)(2,1)} collective-permute-done((bf16[2,1024,512]{2,1,0:T(8,128)(2,1)}, bf16[2,1024,512]{2,1,0:T(8,128)(2,1)}, u32[]{:S(2)}, u32[]{:S(2)}) %collective-permute-start.30) | collective-permute-done | bytes 2097184 | tf_op jit(solution)/shard_map/ppermute | solution.py:940
  690.2 38.5 %collective-permute-done.34 = bf16[2,1,1024,512]{3,2,1,0:T(8,128)(2,1)S(1)} collective-permute-done((bf16[2,1,1024,512]{3,2,1,0:T(8,128)(2,1)S(1)}, bf16[2,1,1024,512]{3,2,1,0:T(8,128)(2,1)S(1)}, u32[]{:S(2)}, u32[]{:S(2)}) %collective-permute-start.34) | collective-permute-done | bytes 2097184 | tf_op jit(solution)/shard_map/ppermute | solution.py:940
  753.0 9.8 %collective-permute-done.39 = bf16[1,1,1024,512]{3,2,1,0:T(8,128)(2,1)} collective-permute-done((bf16[1,1,1024,512]{3,2,1,0:T(8,128)(2,1)S(1)}, bf16[1,1,1024,512]{3,2,1,0:T(8,128)(2,1)}, u32[]{:S(2)}, u32[]{:S(2)}) %collective-permute-start.39) | collective-permute-done | bytes 1048608 | tf_op jit(solution)/shard_map/ppermute | solution.py:940
  770.2 15.2 %collective-permute-done.40 = bf16[2,1024,512]{2,1,0:T(8,128)(2,1)} collective-permute-done((bf16[2,1024,512]{2,1,0:T(8,128)(2,1)}, bf16[2,1024,512]{2,1,0:T(8,128)(2,1)}, u32[]{:S(2)}, u32[]{:S(2)}) %collective-permute-start.40) | collective-permute-done | bytes 2097184 | tf_op jit(solution)/shard_map/ppermute | solution.py:940
  787.4 18.2 %collective-permute-done.42.refs_3_ = bf16[2,1024,512]{2,1,0:T(8,128)(2,1)} collective-permute-done((bf16[2,1024,512]{2,1,0:T(8,128)(2,1)}, bf16[2,1024,512]{2,1,0:T(8,128)(2,1)}, u32[]{:S(2)}, u32[]{:S(2)}) %collective-permute-start.42) | collective-permute-done | bytes 2097184 | tf_op jit(solution)/shard_map/ppermute | solution.py:940
  (359 shorter events, 316.5 us)
Async XLA Ops:
  7.2 131.0 %all-gather.5.cloned.1.call-start = ((), (), s32[]{:S(2)}) async-start(), calls=%async_computation.2 | async-start | bytes 9437184 | tf_op jit(solution)/shard_map/all_gather | solution.py:767
  10.4 153.8 %all-gather.7.cloned.1.call-start = ((), (), s32[]{:S(2)}) async-start(), calls=%async_computation.3 | async-start | bytes 9437184 | tf_op jit(solution)/shard_map/all_gather | solution.py:768
  14.7 244.8 %all-gather.9.cloned.1.call-start = ((), (), s32[]{:S(2)}) async-start(), calls=%async_computation.4 | async-start | bytes 9437184 | tf_op jit(solution)/shard_map/all_gather | solution.py:767
  15.5 261.5 %all-gather.11.cloned.1.call-start = ((), (), s32[]{:S(2)}) async-start(), calls=%async_computation.5 | async-start | bytes 9437184 | tf_op jit(solution)/shard_map/all_gather | solution.py:768
  16.0 750.5 %reduce-scatter.5.cloned.1.call-start = ((), (), s32[]{:S(2)}) async-start(), calls=%async_computation.7 | async-start | bytes 9437184 | tf_op jit(solution)/shard_map/reduce_scatter | solution.py:692
  101.8 90.1 %collective-permute-start.3 = (bf16[1024,512]{1,0:T(8,128)(2,1)}, bf16[1024,512]{1,0:T(8,128)(2,1)S(1)}, u32[]{:S(2)}, u32[]{:S(2)}) collective-permute-start(bf16[1024,512]{1,0:T(8,128)(2,1)} %get-tuple-element.177), channel_id=1, source_target_pairs={{0,2},{2,0},{4,6},{6,4},{1,3},{3,1},{5,7},{7,5},{8,10},{10,8},{12,... | collective-permute-start | bytes 3145736 | tf_op jit(solution)/shard_map/ppermute | solution.py:564
  106.4 49.8 %collective-permute-start.17 = (bf16[512,512]{1,0:T(8,128)(2,1)}, bf16[512,512]{1,0:T(8,128)(2,1)}, u32[]{:S(2)}, u32[]{:S(2)}) collective-permute-start(bf16[512,512]{1,0:T(8,128)(2,1)} %collective-permute-done.5.refs_5_), channel_id=1, source_target_pairs={{0,8},{8,0},{16,24},{24,16},{1,9},{9,1},{17,25},{25,17},{2,10},{10... | collective-permute-start | bytes 1572872 | tf_op jit(solution)/shard_map/ppermute | solution.py:564
  116.5 75.4 %collective-permute-start.7 = (bf16[512,512]{1,0:T(8,128)(2,1)S(1)}, bf16[512,512]{1,0:T(8,128)(2,1)S(1)}, u32[]{:S(2)}, u32[]{:S(2)}) collective-permute-start(bf16[512,512]{1,0:T(8,128)(2,1)S(1)} %collective-permute-done.6.refs_3_), channel_id=1, source_target_pairs={{0,8},{8,0},{16,24},{24,16},{1,9},{9,1},{17,25},{25,17},{2,10},{10... | collective-permute-start | bytes 1572872 | tf_op jit(solution)/shard_map/ppermute | solution.py:564
  135.3 56.6 %collective-permute-start.9 = (bf16[512,512]{1,0:T(8,128)(2,1)S(1)}, bf16[512,512]{1,0:T(8,128)(2,1)S(1)}, u32[]{:S(2)}, u32[]{:S(2)}) collective-permute-start(bf16[512,512]{1,0:T(8,128)(2,1)S(1)} %collective-permute-done.8.refs_5_), channel_id=1, source_target_pairs={{0,8},{8,0},{16,24},{24,16},{1,9},{9,1},{17,25},{25,17},{2,10},{10... | collective-permute-start | bytes 1572872 | tf_op jit(solution)/shard_map/ppermute | solution.py:564
  334.2 50.5 %collective-permute-start.18 = (bf16[2,1024,512]{2,1,0:T(8,128)(2,1)}, bf16[2,1024,512]{2,1,0:T(8,128)(2,1)}, u32[]{:S(2)}, u32[]{:S(2)}) collective-permute-start(bf16[2,1024,512]{2,1,0:T(8,128)(2,1)} %get-tuple-element.98), channel_id=1, source_target_pairs={{0,8},{24,16},{1,9},{25,17},{2,10},{26,18},{3,11},{27,19},{4,12},{... | collective-permute-start | bytes 6291464 | tf_op jit(solution)/shard_map/ppermute | solution.py:940
  443.9 368.0 %reduce-scatter.3.cloned.1.call-start = ((), (), s32[]{:S(2)}) async-start(), calls=%async_computation.6 | async-start | bytes 9437184 | tf_op jit(solution)/shard_map/reduce_scatter | solution.py:692
  506.7 52.4 %collective-permute-start.25 = (bf16[2,1024,512]{2,1,0:T(8,128)(2,1)}, bf16[2,1024,512]{2,1,0:T(8,128)(2,1)S(1)}, u32[]{:S(2)}, u32[]{:S(2)}) collective-permute-start(bf16[2,1024,512]{2,1,0:T(8,128)(2,1)} %broadcast_select_fusion.7), channel_id=1, source_target_pairs={{0,4},{2,6},{4,0},{6,2},{1,5},{3,7},{5,1},{7,3},{8,12},{10,14},{12... | collective-permute-start | bytes 6291464 | tf_op jit(solution)/shard_map/ppermute | solution.py:940
  560.6 50.1 %collective-permute-start.27 = (bf16[2,1024,512]{2,1,0:T(8,128)(2,1)}, bf16[2,1024,512]{2,1,0:T(8,128)(2,1)}, u32[]{:S(2)}, u32[]{:S(2)}) collective-permute-start(bf16[2,1024,512]{2,1,0:T(8,128)(2,1)} %add_convert_fusion.8.refs_5_), channel_id=1, source_target_pairs={{8,16},{16,8},{9,17},{17,9},{10,18},{18,10},{11,19},{19,11},{12,20... | collective-permute-start | bytes 6291464 | tf_op jit(solution)/shard_map/ppermute | solution.py:940
  567.2 48.8 %collective-permute-start.28 = (bf16[2,1024,512]{2,1,0:T(8,128)(2,1)}, bf16[2,1024,512]{2,1,0:T(8,128)(2,1)S(1)}, u32[]{:S(2)}, u32[]{:S(2)}) collective-permute-start(bf16[2,1024,512]{2,1,0:T(8,128)(2,1)} %pad_maximum_fusion), channel_id=1, source_target_pairs={{0,2},{2,0},{4,6},{6,4},{1,3},{3,1},{5,7},{7,5},{8,10},{10,8},{12,... | collective-permute-start | bytes 6291464 | tf_op jit(solution)/shard_map/ppermute | solution.py:940
  616.0 53.0 %collective-permute-start.29 = (bf16[2,2,1024,512]{3,2,1,0:T(8,128)(2,1)}, bf16[2,2,1024,512]{3,2,1,0:T(8,128)(2,1)}, u32[]{:S(2)}, u32[]{:S(2)}) collective-permute-start(bf16[2,2,1024,512]{3,2,1,0:T(8,128)(2,1)} %get-tuple-element.120.refs_8_), channel_id=1, source_target_pairs={{0,2},{2,0},{4,6},{6,4},{1,3},{3,1},{5,7},{7,5},{8,10},{10,8},{12,... | collective-permute-start | bytes 12582920 | tf_op jit(solution)/shard_map/ppermute | solution.py:940
  616.6 54.9 %collective-permute-start.32 = (bf16[2,2,1024,512]{3,2,1,0:T(8,128)(2,1)}, bf16[2,2,1024,512]{3,2,1,0:T(8,128)(2,1)}, u32[]{:S(2)}, u32[]{:S(2)}) collective-permute-start(bf16[2,2,1024,512]{3,2,1,0:T(8,128)(2,1)} %get-tuple-element.124.refs_5_), channel_id=1, source_target_pairs={{0,2},{2,0},{4,6},{6,4},{1,3},{3,1},{5,7},{7,5},{8,10},{10,8},{12,... | collective-permute-start | bytes 12582920 | tf_op jit(solution)/shard_map/ppermute | solution.py:940
  618.6 48.3 %collective-permute-start.30 = (bf16[2,1024,512]{2,1,0:T(8,128)(2,1)}, bf16[2,1024,512]{2,1,0:T(8,128)(2,1)}, u32[]{:S(2)}, u32[]{:S(2)}) collective-permute-start(bf16[2,1024,512]{2,1,0:T(8,128)(2,1)} %get-tuple-element.121), channel_id=1, source_target_pairs={{0,8},{24,16},{8,0},{16,24},{1,9},{25,17},{9,1},{17,25},{2,10},{26... | collective-permute-start | bytes 6291464 | tf_op jit(solution)/shard_map/ppermute | solution.py:940
  623.6 58.0 %collective-permute-start.33 = (bf16[2,1024,512]{2,1,0:T(8,128)(2,1)}, bf16[2,1024,512]{2,1,0:T(8,128)(2,1)}, u32[]{:S(2)}, u32[]{:S(2)}) collective-permute-start(bf16[2,1024,512]{2,1,0:T(8,128)(2,1)} %broadcast_select_fusion.3), channel_id=1, source_target_pairs={{0,4},{2,6},{4,0},{6,2},{1,5},{3,7},{5,1},{7,3},{8,12},{10,14},{12... | collective-permute-start | bytes 6291464 | tf_op jit(solution)/shard_map/ppermute | solution.py:940
  681.9 50.2 %collective-permute-start.36 = (bf16[1,2,1024,512]{3,2,1,0:T(8,128)(2,1)S(1)}, bf16[1,2,1024,512]{3,2,1,0:T(8,128)(2,1)S(1)}, u32[]{:S(2)}, u32[]{:S(2)}) collective-permute-start(bf16[1,2,1024,512]{3,2,1,0:T(8,128)(2,1)S(1)} %add_convert_fusion.1), channel_id=1, source_target_pairs={{0,1},{1,0},{2,3},{3,2},{4,5},{5,4},{6,7},{7,6},{8,9},{9,8},{10,11... | collective-permute-start | bytes 6291464 | tf_op jit(solution)/shard_map/ppermute | solution.py:940
  683.6 51.0 %collective-permute-start.35 = (bf16[2,1024,512]{2,1,0:T(8,128)(2,1)S(1)}, bf16[2,1024,512]{2,1,0:T(8,128)(2,1)S(1)}, u32[]{:S(2)}, u32[]{:S(2)}) collective-permute-start(bf16[2,1024,512]{2,1,0:T(8,128)(2,1)S(1)} %add_convert_fusion.3), channel_id=1, source_target_pairs={{8,16},{16,8},{9,17},{17,9},{10,18},{18,10},{11,19},{19,11},{12,20... | collective-permute-start | bytes 6291464 | tf_op jit(solution)/shard_map/ppermute | solution.py:940
  688.7 49.9 %collective-permute-start.41 = (bf16[2,1024,512]{2,1,0:T(8,128)(2,1)S(1)}, bf16[2,1024,512]{2,1,0:T(8,128)(2,1)S(1)}, u32[]{:S(2)}, u32[]{:S(2)}) collective-permute-start(bf16[2,1024,512]{2,1,0:T(8,128)(2,1)S(1)} %add_convert_fusion.2), channel_id=1, source_target_pairs={{8,0},{16,24},{9,1},{17,25},{10,2},{18,26},{11,3},{19,27},{12,4},{... | collective-permute-start | bytes 6291464 | tf_op jit(solution)/shard_map/ppermute | solution.py:940
  736.9 48.5 %collective-permute-start.40 = (bf16[2,1024,512]{2,1,0:T(8,128)(2,1)}, bf16[2,1024,512]{2,1,0:T(8,128)(2,1)}, u32[]{:S(2)}, u32[]{:S(2)}) collective-permute-start(bf16[2,1024,512]{2,1,0:T(8,128)(2,1)} %add_convert_fusion.refs_5_), channel_id=1, source_target_pairs={{8,0},{16,24},{9,1},{17,25},{10,2},{18,26},{11,3},{19,27},{12,4},{... | collective-permute-start | bytes 6291464 | tf_op jit(solution)/shard_map/ppermute | solution.py:940
  740.2 65.3 %collective-permute-start.42 = (bf16[2,1024,512]{2,1,0:T(8,128)(2,1)}, bf16[2,1024,512]{2,1,0:T(8,128)(2,1)}, u32[]{:S(2)}, u32[]{:S(2)}) collective-permute-start(bf16[2,1024,512]{2,1,0:T(8,128)(2,1)} %broadcast_select_fusion), channel_id=1, source_target_pairs={{0,4},{2,6},{4,0},{6,2},{1,5},{3,7},{5,1},{7,3},{8,12},{10,14},{12... | collective-permute-start | bytes 6291464 | tf_op jit(solution)/shard_map/ppermute | solution.py:940
  744.6 63.8 %collective-permute-start.38 = (bf16[1,1,1024,512]{3,2,1,0:T(8,128)(2,1)}, bf16[1,1,1024,512]{3,2,1,0:T(8,128)(2,1)}, u32[]{:S(2)}, u32[]{:S(2)}) collective-permute-start(bf16[1,1,1024,512]{3,2,1,0:T(8,128)(2,1)} %add_convert_fusion.15.refs_7_), channel_id=1, source_target_pairs={{0,1},{1,0},{2,3},{3,2},{4,5},{5,4},{6,7},{7,6},{8,9},{9,8},{10,11... | collective-permute-start | bytes 3145736 | tf_op jit(solution)/shard_map/ppermute | solution.py:940
  (95 other events, 1559.9 us)
Sparse Core Ops, SparseCore 0:
  10.5 85.9 all-gather.4
  98.4 65.7 all-gather.6
  166.7 54.2 all-gather.8
  222.7 54.2 all-gather.10
  444.1 77.6 reduce-scatter.4
  567.3 81.1 reduce-scatter.2
